TPU v7x, 128 devices: a whole 4x4x4 slice. The times are simulated.
128 devices in a mesh: mx: 16 (over y, x), my: 8 (over z, core).
Axes of the slice: x: 4, y: 4, z: 4, core: 2. Of those that a mesh axis runs over, the one named last changes fastest.
Arguments:
- density: float32 [256, 128, 128], P('mx', 'my'), may hold values from 0.5 to 2
- momentum: float32 [3, 256, 128, 128], P(None, 'mx', 'my'), may hold values from -1.8 to 1.8
- energy: float32 [256, 128, 128], P('mx', 'my'), may hold values from -6 to 6
- entropy: float32 [256, 128, 128], P('mx', 'my'), may hold values from 0.5 to 16, as said below
- tracers: float32 [9, 256, 128, 128], P(None, 'mx', 'my'), may hold values from -6 to 6
- leaf_flags: int32 [32, 16, 16], P('mx', 'my'), may hold values 0 or 1
Outputs:
- section: float32 [15, 256, 128, 128], P(None, 'mx', 'my')
- gravity_accel: float32 [3, 256, 128, 128], P(None, 'mx', 'my')
Inputs may be any that keep to these rules, and one draw needn't show every extreme that they name: `entropy`: positive.
All inputs are finite; a program needn't handle non-finite values. No bound on the sum of `leaf_flags` on one device may be relied on, other than what follows from the above.
Results may differ from a plain program's by a relative error of at most 0.0003.
Values sent between devices are 32-bit elements; how exact they have to be, the bound alone decides.
No kernel may reach another device: no remote copies, remote signals or barrier semaphores. Data moves between devices by JAX's collectives and lax.ppermute only.
A program may use at most 128 MiB of HBM per device.

v0:
```python
import functools
import math

import jax
import jax.numpy as jnp
import ml_dtypes
import numpy as np
from jax import lax
from jax.experimental import pallas as pl
from jax.experimental.pallas import tpu as pltpu
from jax.sharding import PartitionSpec as P

F32 = jnp.float32
BF16 = jnp.bfloat16
HIGHEST = lax.Precision.HIGHEST
GRAVITY = 0.02
GAMMA = 5.0 / 3.0
COURANT = 0.3
SUB = 8
NF = 15
GX, GY = 16, 8
ROWS = 256

ALPHA = [
    (px, py, d - px - py)
    for d in range(4)
    for px in range(d, -1, -1)
    for py in range(d - px, -1, -1)
]
NA = len(ALPHA)
NG = 24
WIN = 40
PAIRS = [(px, py) for px in range(4) for py in range(4 - px)]


def factorial_of(e):
    return math.factorial(e[0]) * math.factorial(e[1]) * math.factorial(e[2])


def inverse_derivative(exponent, r):
    axes = [0] * exponent[0] + [1] * exponent[1] + [2] * exponent[2]
    norm = math.sqrt(r[0] ** 2 + r[1] ** 2 + r[2] ** 2)
    if norm == 0.0:
        return 0.0
    if not axes:
        return 1.0 / norm
    if len(axes) == 1:
        return -r[axes[0]] / norm**3
    if len(axes) == 2:
        a, b = axes
        return 3.0 * r[a] * r[b] / norm**5 - float(a == b) / norm**3
    a, b, c = axes
    crossed = float(a == b) * r[c] + float(a == c) * r[b] + float(b == c) * r[a]
    return -15.0 * r[a] * r[b] * r[c] / norm**7 + 3.0 * crossed / norm**5


def split_np(x):
    high = x.astype(np.float32).astype(ml_dtypes.bfloat16)
    low = (x - high.astype(np.float64)).astype(ml_dtypes.bfloat16)
    return high, low


@functools.cache
def constants():
    out = {}
    w = np.zeros((7, NG, NA, WIN))
    for z in range(7):
        for i in range(6):
            for j in range(6):
                r = (-(i - 2.0), -(j - 2.0), -(z - 3.0))
                for g, eg in enumerate(ALPHA):
                    for a, ea in enumerate(ALPHA):
                        if sum(eg) + sum(ea) <= 3:
                            e = tuple(eg[k] + ea[k] for k in range(3))
                            w[z, g, a, i * 6 + j] = (
                                -GRAVITY * (-1.0) ** sum(ea) / factorial_of(ea) * inverse_derivative(e, r)
                            )
    out["w_high"], out["w_low"] = split_np(w.reshape(7 * NG, NA * WIN))
    sel = np.zeros((4, WIN, 72))
    sign = np.zeros((4, 384))
    for c in range(4):
        cx, cy = c >> 1, c & 1
        for i in range(6):
            for j in range(6):
                si, sj = (5 - i if cx else i), (5 - j if cy else j)
                sel[c, i * 6 + j, ((si // 2) * 3 + sj // 2) * 8 + (si % 2) * 2 + sj % 2] = 1.0
        for a, e in enumerate(ALPHA):
            sign[c, a * 16 : a * 16 + 16] = (-1.0) ** (cx * e[0] + cy * e[1])
    out["sel_zero"] = sel.reshape(4 * WIN, 72).astype(ml_dtypes.bfloat16)
    lanes = np.zeros((16, 384), np.float32)
    lanes[0:4] = sign
    for a, e in enumerate(ALPHA):
        for r in range(16):
            lane = a * 16 + r
            level = 1 if r < 8 else 2 if r < 12 else 3
            lanes[4 + level, lane] = e[0] % 2
            lanes[8 + level, lane] = e[1] % 2
    out["lane_odd"] = lanes
    up = np.zeros((384, 384))
    for t, et in enumerate(ALPHA):
        for s, es in enumerate(ALPHA):
            if all(es[k] <= et[k] for k in range(3)):
                for base, to, count in ((0, 8, 8), (8, 12, 4)):
                    for z in range(count):
                        v = 2.0 ** -sum(et)
                        for k in range(3):
                            d = -0.5 if k < 2 or z % 2 == 0 else 0.5
                            v *= math.comb(et[k], es[k]) * d ** (et[k] - es[k])
                        up[s * 16 + base + z, t * 16 + to + z // 2] = v
    assert np.array_equal(up, up.astype(ml_dtypes.bfloat16).astype(np.float64))
    out["up"] = up.astype(ml_dtypes.bfloat16)
    odd = np.zeros((16, 384), np.float32)
    for a, e in enumerate(ALPHA):
        odd[0, a * 16 : a * 16 + 16] = e[0] % 2
        odd[1, a * 16 : a * 16 + 16] = e[1] % 2
    out["alpha_odd"] = odd
    agg = np.zeros((32, 128))
    for x in range(GX):
        for y in range(GY):
            agg[(x // 2) * 4 + y // 2, x * 8 + y] = 1.0
    out["agg"] = agg.astype(ml_dtypes.bfloat16)
    mask = np.zeros((8, 128), np.float32)
    info = np.zeros((16, 128), np.float32)
    expand = np.zeros((128, 128), np.float32)
    for lane in range(96):
        g, r = lane // 16, lane % 16
        if g < 4:
            n, z, level = 16, r, 0
        elif r < 8:
            n, z, level = 8, r, 1
        elif r < 12:
            n, z, level = 4, r - 8, 2
        elif r < 14:
            n, z, level = 2, r - 12, 3
        else:
            continue
        for k in range(7):
            o = k - 3
            ok = 0 <= z + o < n and abs((z + o) // 2 - z // 2) <= 1
            if g == 4:
                ok = ok and abs(o) > 1
            if g == 5:
                ok = ok and abs(o) <= 1
            mask[k, lane] = float(ok)
        if g < 5:
            info[0, lane] = 2.0**-level
            info[1, lane] = float(g >> 1) if level == 0 else 0.0
            info[2, lane] = float(g & 1) if level == 0 else 0.0
            info[2 + 2 * level, lane] = 1.0 if level else info[2, lane]
            info[9, lane] = float(z % 2)
            if level == 0:
                expand[64 + z // 2, lane] = 1.0
            elif level == 1:
                expand[64 + 8 + z // 2, lane] = 1.0
            elif level == 2:
                expand[64 + 12 + z // 2, lane] = 1.0
    out["mask"] = mask
    out["info"] = info
    out["expand"] = expand
    gamma_odd = np.zeros((3 * NG, 128), np.float32)
    down = np.zeros((NG, NG), np.float32)
    for g, eg in enumerate(ALPHA):
        for k in range(3):
            gamma_odd[k * NG + g] = eg[k] % 2
        for b, eb in enumerate(ALPHA):
            if all(eb[k] >= eg[k] for k in range(3)):
                v = 2.0 ** -sum(eg)
                for k in range(3):
                    n = eb[k] - eg[k]
                    v *= (-0.25) ** n / math.factorial(n)
                down[g, b] = v
    out["gamma_odd"] = gamma_odd
    out["down"] = down
    h = (np.arange(SUB) + 0.5) / SUB - 0.5
    spread = np.zeros((16, 384))
    for k in range(3):
        for z in range(128):
            spread[z // 8, k * 128 + z] = h[z % 8] ** k
    out["spread"] = spread.astype(np.float32)
    poly = np.zeros((3, 8, 8, 3, NG))
    for i in range(3):
        for g, e in enumerate(ALPHA):
            if e[i] > 0:
                low = list(e)
                low[i] -= 1
                poly[i, :, :, low[2], g] = (
                    -e[i] / factorial_of(e) * h[:, None] ** low[0] * h[None, :] ** low[1]
                )
    out["poly"] = poly.reshape(192, 72).astype(np.float32)
    cells = np.arange(16)
    near = h[cells % 8]
    far = ((cells + 0.5) / 8 - 1.0) / 2
    left = np.zeros((2, len(PAIRS), 8, 16, 16))
    for q, (px, py) in enumerate(PAIRS):
        for c in range(4):
            block = ((cells // 8 == c >> 1)[:, None] & (cells // 8 == (c & 1))[None, :]).astype(float)
            left[0, q, c] = block * near[:, None] ** px * near[None, :] ** py
            left[1, q, c] = block * far[:, None] ** px * far[None, :] ** py
    out["left"] = left.reshape(160, 256).astype(np.float32)
    right = np.zeros((128, 128))
    flag = np.zeros((128, 128))
    for z in range(128):
        s = z // 8
        f = ((z % 16 + 0.5) / 8 - 1.0) / 2
        for pz in range(4):
            right[z, pz * 16 + s] = h[z % 8] ** pz / SUB**3
            right[z, 64 + (s % 2) * 32 + pz * 8 + s // 2] = f**pz / SUB**3
    for s in range(16):
        for pz in range(4):
            flag[s, pz * 16 + s] = 1.0
            flag[s, 64 + (s % 2) * 32 + pz * 8 + s // 2] = 1.0
    out["right"] = right.astype(np.float32)
    out["flag"] = flag.astype(ml_dtypes.bfloat16)
    return out


def split(x):
    high = x.astype(BF16)
    return high, (x - high.astype(F32)).astype(BF16)


def mxu(a, b):
    return jnp.dot(a, b, preferred_element_type=F32)


def exact(a, b):
    return jnp.dot(a, b, precision=HIGHEST, preferred_element_type=F32)


def lane_ids(shape):
    return lax.broadcasted_iota(jnp.int32, shape, len(shape) - 1)


def row_ids(shape):
    return lax.broadcasted_iota(jnp.int32, shape, len(shape) - 2)


def power(s):
    return jnp.exp(GAMMA * jnp.log(s))


def field_ref(refs, f):
    den, mom, ene, ent, tra = refs
    if f == 0:
        return den, 0
    if f < 4:
        return mom, (f - 1) * ROWS
    if f == 4:
        return ene, 0
    if f == 5:
        return ent, 0
    return tra, (f - 6) * ROWS


def prepare_kernel(den, mom, ene, ent, tra, flags, left, right, flag, pay, xlo, xhi, ylo, yhi, fl):
    refs = (den, mom, ene, ent, tra)
    for f in range(NF):
        ref, base = field_ref(refs, f)
        for k in range(3):
            xlo[f * 3 + k] = ref[base + k * 16 : base + k * 16 + 16]
            xhi[f * 3 + k] = ref[base + (13 + k) * 16 : base + (13 + k) * 16 + 16]
            for s in range(2):
                ylo[f * 3 + k, s * 8 : s * 8 + 8] = ref[pl.ds(base + s * 128 + k, 8, stride=16)]
                yhi[f * 3 + k, s * 8 : s * 8 + 8] = ref[pl.ds(base + s * 128 + 13 + k, 8, stride=16)]
    rho = den[...]
    inverse = 1.0 / rho
    fast = jnp.maximum(jnp.maximum(jnp.abs(mom[0:ROWS]), jnp.abs(mom[ROWS : 2 * ROWS])), jnp.abs(mom[2 * ROWS :]))
    sound = jnp.sqrt(GAMMA * (GAMMA - 1.0) * power(ent[...]) * inverse)
    fastest = jnp.max(fast * inverse + sound)
    fl[...] = jnp.zeros((8, 128), F32)
    fl[0:2, 0:16] = flags[0].astype(F32)
    fl[2:4, 0:16] = flags[1].astype(F32)
    tile = mxu(fl[...].astype(BF16), flag[...])
    sums = exact(left[...], exact(rho, right[...]))
    lane = lane_ids((8, 128))
    row = row_ids((8, 128))
    tiles = [jnp.zeros((8, 128), F32) for _ in range(3)]
    zero, one = {}, {}
    for q, pair in enumerate(PAIRS):
        zero[pair] = sums[q * 8 : q * 8 + 8] * tile
        v = jnp.sum(sums[80 + q * 8 : 88 + q * 8] * tile, axis=0, keepdims=True)
        v = jnp.broadcast_to(v, (8, 128))
        one[pair] = v + pltpu.roll(v, 96, 1)
    for a, e in enumerate(ALPHA):
        c, to = a // 8, (a % 8) * 16
        low = pltpu.roll(zero[e[0], e[1]], (to - e[2] * 16) % 128, 1)
        top = pltpu.roll(one[e[0], e[1]], (to - 64 - e[2] * 8) % 128, 1)
        here = (lane >= to) & (lane < to + 16)
        tiles[c] = jnp.where(here & (row < 4), low, tiles[c])
        tiles[c] = jnp.where(here & (row == 4) & (lane < to + 8), top, tiles[c])
    tiles[2] = jnp.where((row == 4) & (lane >= 64), fastest, tiles[2])
    for c in range(3):
        pay[c * 8 : c * 8 + 8] = tiles[c]


def states(ol, il, l, r, ir, orr):
    face = (37.0 / 60.0) * (l + r) - (8.0 / 60.0) * (il + ir) + (1.0 / 60.0) * (ol + orr)
    low, high = jnp.minimum(l, r), jnp.maximum(l, r)
    left = jnp.minimum(jnp.maximum(face, jnp.minimum(il, low)), jnp.maximum(il, high))
    right = jnp.minimum(jnp.maximum(face, jnp.minimum(low, ir)), jnp.maximum(high, ir))
    return left, right


def fluxes(load, d):
    rl, rr = load(0)
    ml, mr = load(1 + d)
    sl, sr = load(5)
    il, ir = 1.0 / rl, 1.0 / rr
    vl, vr = ml * il, mr * ir
    pl_, pr = (GAMMA - 1.0) * power(sl), (GAMMA - 1.0) * power(sr)
    cl, cr = jnp.sqrt(GAMMA * pl_ * il), jnp.sqrt(GAMMA * pr * ir)
    a = 4.0 * jnp.maximum(jnp.abs(vl) + cl, jnp.abs(vr) + cr)
    wl, wr = 4.0 * vl, 4.0 * vr
    kl, kr = wl + a, wr - a
    got = {0: (rl, rr), 1 + d: (ml, mr), 5: (sl, sr)}
    out = []
    for f in range(NF):
        left, right = got[f] if f in got else load(f)
        flux = left * kl + right * kr
        if f == 1 + d:
            flux = flux + 4.0 * (pl_ + pr)
        if f == 4:
            flux = flux + (pl_ * wl + pr * wr)
        out.append(flux)
    return out


def flux_kernel(pos, den, mom, ene, ent, tra, xl, xr, yl, yr, out, ux, uy, edge):
    refs = (den, mom, ene, ent, tra)
    first_x, last_x = pos[0] == 0, pos[0] == GX - 1
    first_y, last_y = pos[1] == 0, pos[1] == GY - 1
    for f in range(NF):
        ref, base = field_ref(refs, f)
        ux[f, 48 : 48 + ROWS] = ref[base : base + ROWS]
        for s in range(2):
            rows = slice(s * 8, s * 8 + 8)
            for y in range(16):
                uy[f, (3 + y) * 16 + s * 8 : (3 + y) * 16 + s * 8 + 8] = ref[pl.ds(base + s * 128 + y, 8, stride=16)]
            lo, hi = ref[base + s * 8 : base + s * 8 + 8], ref[base + 240 + s * 8 : base + 248 + s * 8]
            ylo, yhi = ref[pl.ds(base + s * 128, 8, stride=16)], ref[pl.ds(base + s * 128 + 15, 8, stride=16)]
            for k in range(3):
                ux[f, k * 16 + s * 8 : k * 16 + s * 8 + 8] = jnp.where(first_x, lo, xl[f * 3 + k, rows])
                ux[f, (19 + k) * 16 + s * 8 : (19 + k) * 16 + s * 8 + 8] = jnp.where(last_x, hi, xr[f * 3 + k, rows])
                uy[f, k * 16 + s * 8 : k * 16 + s * 8 + 8] = jnp.where(first_y, ylo, yl[f * 3 + k, rows])
                uy[f, (19 + k) * 16 + s * 8 : (19 + k) * 16 + s * 8 + 8] = jnp.where(last_y, yhi, yr[f * 3 + k, rows])

    def sweep(buf, d, s, emit):
        def faces(i):
            def load(f):
                cells = [buf[f, pl.ds(pl.multiple_of((i + k) * 16 + s * 8, 8), 8)] for k in range(6)]
                return states(*cells)

            return fluxes(load, d)

        def step(i, before):
            now = faces(i)
            for f in range(NF):
                emit(f, i - 1, before[f] - now[f])
            return tuple(now)

        lax.fori_loop(1, 17, step, tuple(faces(0)))

    for s in range(2):

        def emit_y(f, y, value, s=s):
            out[pl.ds(f * ROWS + s * 128 + y, 8, stride=16)] = value

        sweep(uy, 1, s, emit_y)
    for s in range(2):

        def emit_x(f, x, value, s=s):
            at = pl.ds(pl.multiple_of(f * ROWS + x * 16 + s * 8, 8), 8)
            out[at] = out[at] + value

        sweep(ux, 0, s, emit_x)

    lane = lane_ids((8, 128))
    group = lane // 8
    for s in range(2):

        def load_edge(f, s=s):
            packed = jnp.zeros((8, 128), F32)
            for x in range(16):
                u = ux[f, (3 + x) * 16 + s * 8 : (3 + x) * 16 + s * 8 + 8]
                packed = jnp.where(group == x, pltpu.roll(u, x * 8, 1), packed)
            one, two = pltpu.roll(packed, 127, 1), pltpu.roll(packed, 126, 1)
            return states(packed, packed, packed, packed, one, two)

        for f, value in enumerate(fluxes(load_edge, 2)):
            edge[f, s * 8 : s * 8 + 8] = value
    low_end, high_end = lane == 0, lane == 127

    def along_z(i, carry):
        x, s = i // 2, i % 2
        at = pl.multiple_of(i * 8, 8)

        def load(f):
            u = ux[f, pl.ds(48 + at, 8)]
            m1 = jnp.where(low_end, u, pltpu.roll(u, 1, 1))
            m2 = jnp.where(low_end, u, pltpu.roll(m1, 1, 1))
            p1 = jnp.where(high_end, u, pltpu.roll(u, 127, 1))
            p2 = jnp.where(high_end, u, pltpu.roll(p1, 127, 1))
            p3 = jnp.where(high_end, u, pltpu.roll(p2, 127, 1))
            return states(m2, m1, u, p1, p2, p3)

        for f, value in enumerate(fluxes(load, 2)):
            lower = pltpu.roll(edge[f, pl.ds(pl.multiple_of(s * 8, 8), 8)], lax.rem(128 - x * 8, 128), 1)
            below = jnp.where(low_end, lower, pltpu.roll(value, 1, 1))
            rows = pl.ds(pl.multiple_of(f * ROWS + i * 8, 8), 8)
            out[rows] = out[rows] + (below - value)
        return carry

    lax.fori_loop(0, 32, along_z, 0)


def tree_kernel(
    pos, far, mid, xl, xr, den, mom, ene, ent, tra, tend,
    w_high, w_low, sel_zero, lane_odd, up, alpha_odd, agg, mask, info, expand, gamma_odd, down, spread, poly,
    section, accel, rhs, field,
):
    px, py = pos[0], pos[1]
    around = jnp.concatenate(
        [
            jnp.concatenate([ref[(dy * 3 + c) * 8 : (dy * 3 + c) * 8 + 8] for ref in (xl, mid, xr) for dy in range(3)], 0)
            for c in range(3)
        ],
        1,
    )
    zero = mxu(sel_zero[...], jnp.concatenate(split(around), 1))
    zero = zero[:, :384] + zero[:, 384:]
    arrays = [zero[c * WIN : c * WIN + WIN] * lane_odd[c : c + 1] for c in range(4)]
    gathered = jnp.concatenate([far[:, c].reshape(128, 128) for c in range(3)], 1)
    speeds = far[:, 2].reshape(128, 128)
    fastest = jnp.max(jnp.where(lane_ids((128, 128)) >= 64, speeds, 0.0))

    def lifted(x, x_odd, y_odd):
        sign = (1.0 - 2.0 * x_odd * alpha_odd[0:1]) * (1.0 - 2.0 * y_odd * alpha_odd[1:2])
        n = x.shape[0]
        z = mxu(jnp.concatenate(split(x * sign), 0), up[...])
        return (z[:n] + z[n:]) * sign

    def picked(matrix, x):
        y = mxu(matrix, jnp.concatenate(split(x), 1))
        return y[:, :384] + y[:, 384:]

    dev = lax.broadcasted_iota(jnp.int32, (128, 1), 0)
    raised = lifted(gathered, ((dev // 8) % 2).astype(F32), (dev % 2).astype(F32))
    two = picked(agg[...], raised)
    cell = lax.broadcasted_iota(jnp.int32, (32, 1), 0)
    raised_two = lifted(two, ((cell // 4) % 2).astype(F32), (cell % 2).astype(F32))

    def window(level, columns, count_y, shift):
        tx, ty = px >> (level - 1), py >> (level - 1)
        row = lax.broadcasted_iota(jnp.int32, (WIN, columns), 0)
        col = lax.broadcasted_iota(jnp.int32, (WIN, columns), 1)
        i, j = row // 6, row % 6
        i = jnp.where((tx & 1) == 1, 5 - i, i) + 2 * ((tx >> 1) - 1)
        j = jnp.where((ty & 1) == 1, 5 - j, j) + 2 * ((ty >> 1) - 1)
        sx, sy = (col // count_y) >> shift, (col % count_y) >> shift
        return ((row < 36) & (sx == i) & (sy == j)).astype(F32).astype(BF16)

    levels = (
        picked(window(1, 128, 8, 0), gathered)
        + picked(window(2, 128, 8, 1), raised)
        + picked(window(3, 32, 4, 1), raised_two)
    )
    sign = jnp.ones((1, 384), F32)
    for level in (1, 2, 3):
        bx = ((px >> (level - 1)) & 1).astype(F32)
        by = ((py >> (level - 1)) & 1).astype(F32)
        sign = sign * (1.0 - 2.0 * bx * lane_odd[4 + level : 5 + level])
        sign = sign * (1.0 - 2.0 * by * lane_odd[8 + level : 9 + level])
    levels = levels * sign
    wrow = lax.broadcasted_iota(jnp.int32, (WIN, 384), 0)
    wi, wj = wrow // 6, wrow % 6
    touching = (wi >= 1) & (wi <= 3) & (wj >= 1) & (wj <= 3)
    arrays += [levels, jnp.where(touching, 0.0, levels)]
    lane = lane_ids((WIN, 128)) // 16
    for a in range(NA):
        c, off = a // 8, (a % 8) * 16
        block = jnp.zeros((WIN, 128), F32)
        for g, array in enumerate(arrays):
            block = jnp.where(lane == g, pltpu.roll(array[:, c * 128 : c * 128 + 128], (16 * g - off) % 128, 1), block)
        rhs[a * WIN : a * WIN + WIN] = block
    high, low = split(rhs[...])
    y = mxu(w_high[...], jnp.concatenate([high, low], 1))
    y = y[:, :128] + y[:, 128:] + mxu(w_low[...], high)
    base = jnp.zeros((NG, 128), F32)
    for k in range(7):
        base = base + mask[k : k + 1] * pltpu.roll(y[k * NG : k * NG + NG], (3 - k) % 128, 1)
    lanes = lane_ids((NG, 128)) // 16
    base = base + jnp.where(lanes == 4, pltpu.roll(base, 112, 1), 0.0)
    bx, by = info[1:2], info[2:3]
    for level in (1, 2, 3):
        bx = bx + info[2 + 2 * level : 3 + 2 * level] * ((px >> (level - 1)) & 1).astype(F32)
        by = by + info[2 + 2 * level : 3 + 2 * level] * ((py >> (level - 1)) & 1).astype(F32)
    flip = (1.0 - 2.0 * bx * gamma_odd[0:NG]) * (1.0 - 2.0 * by * gamma_odd[NG : 2 * NG])
    base = base * info[0:1] * flip
    flip = flip * (1.0 - 2.0 * info[9:10] * gamma_odd[2 * NG :])
    total = base
    for _ in range(3):
        total = base + flip * exact(down[...], flip * exact(total, expand[...]))
    rows = jnp.concatenate([pltpu.roll(total, (128 - 16 * c) % 128, 1) for c in range(4)], 0)[:, :16]
    spreads = exact(rows, spread[...])
    terms = jnp.concatenate(
        [
            jnp.concatenate([spreads[c * NG : c * NG + NG, k * 128 : k * 128 + 128] for k in range(3)], 0)
            for c in range(4)
        ],
        1,
    )
    field[...] = exact(poly[...], terms)
    step = jnp.full((8, 128), COURANT / SUB, F32) / fastest
    refs = (den, mom, ene, ent, tra)

    def finish(x, carry):
        for c in range(4):
            at = pl.multiple_of(((c >> 1) * 8 + x) * 16 + (c & 1) * 8, 8)
            acc = [field[pl.ds(pl.multiple_of(i * 64 + x * 8, 8), 8), c * 128 : c * 128 + 128] for i in range(3)]
            rho = den[pl.ds(at, 8)]
            moms = [mom[pl.ds(i * ROWS + at, 8)] for i in range(3)]
            for i in range(3):
                accel[pl.ds(i * ROWS + at, 8)] = acc[i]
            for f in range(NF):
                ref, start = field_ref(refs, f)
                change = tend[pl.ds(f * ROWS + at, 8)]
                if 1 <= f <= 3:
                    change = change + rho * acc[f - 1]
                if f == 4:
                    change = change + moms[0] * acc[0] + moms[1] * acc[1] + moms[2] * acc[2]
                section[pl.ds(f * ROWS + at, 8)] = ref[pl.ds(start + at, 8)] + step * change
        return carry

    lax.fori_loop(0, 8, finish, 0)


VMEM = pl.BlockSpec(memory_space=pltpu.VMEM)
SMEM = pl.BlockSpec(memory_space=pltpu.SMEM)


def call(kernel, ins, shapes, scratch, cost, name, smem=0):
    return pl.pallas_call(
        kernel,
        out_shape=[jax.ShapeDtypeStruct(s, F32) for s in shapes],
        in_specs=[SMEM] * smem + [VMEM] * (len(ins) - smem),
        out_specs=[VMEM] * len(shapes),
        scratch_shapes=scratch,
        cost_estimate=cost,
        name=name,
        compiler_params=pltpu.CompilerParams(vmem_limit_bytes=48 << 20),
    )(*ins)


def shards(density, momentum, energy, entropy, tracers, leaf_flags):
    con = {k: jnp.asarray(v) for k, v in constants().items()}
    fields = [
        density.reshape(ROWS, 128),
        momentum.reshape(3 * ROWS, 128),
        energy.reshape(ROWS, 128),
        entropy.reshape(ROWS, 128),
        tracers.reshape(9 * ROWS, 128),
    ]
    ix, iy = lax.axis_index("mx"), lax.axis_index("my")
    pos = jnp.stack([ix, iy]).astype(jnp.int32)
    pay, xlo, xhi, ylo, yhi = call(
        prepare_kernel,
        fields + [leaf_flags, con["left"], con["right"], con["flag"]],
        [(24, 128), (50, 16, 128), (50, 16, 128), (45, 16, 128), (45, 16, 128)],
        [pltpu.VMEM((8, 128), F32)],
        pl.CostEstimate(flops=10**7, bytes_accessed=3 * 10**6, transcendentals=10**5),
        "prepare",
    )
    up_x, down_x = [(i, i + 1) for i in range(GX - 1)], [(i + 1, i) for i in range(GX - 1)]
    up_y, down_y = [(i, i + 1) for i in range(GY - 1)], [(i + 1, i) for i in range(GY - 1)]
    yl = lax.ppermute(yhi, "my", up_y)
    yr = lax.ppermute(ylo, "my", down_y)
    column = lax.all_to_all(jnp.broadcast_to(pay[None], (GY, 24, 128)), "my", 0, 0)
    ones = jnp.transpose(column.reshape(GY, 3, 8, 128)[:, :, 4], (1, 0, 2))
    far = lax.all_to_all(jnp.broadcast_to(ones[None], (GX, 3, GY, 128)), "mx", 0, 0)
    padded = jnp.pad(column, ((1, 1), (0, 0), (0, 0)))
    mid = lax.dynamic_slice_in_dim(padded, iy, 3, 0).reshape(72, 128)
    extra = jnp.pad(mid, ((0, 8), (0, 0))).reshape(5, 16, 128)
    xl = lax.ppermute(lax.dynamic_update_slice_in_dim(xhi, extra, 45, 0), "mx", up_x)
    xr = lax.ppermute(lax.dynamic_update_slice_in_dim(xlo, extra, 45, 0), "mx", down_x)
    (tend,) = call(
        flux_kernel,
        [pos] + fields + [xl, xr, yl, yr],
        [(NF * ROWS, 128)],
        [pltpu.VMEM((NF, 22 * 16, 128), F32), pltpu.VMEM((NF, 22 * 16, 128), F32), pltpu.VMEM((NF, 16, 128), F32)],
        pl.CostEstimate(flops=5 * 10**7, bytes_accessed=6 * 10**6, transcendentals=10**6),
        "flux",
        smem=1,
    )
    names = (
        "w_high", "w_low", "sel_zero", "lane_odd", "up", "alpha_odd", "agg", "mask", "info", "expand", "gamma_odd",
        "down", "spread", "poly",
    )
    section, accel = call(
        tree_kernel,
        [pos, far, mid, xl[45:].reshape(80, 128), xr[45:].reshape(80, 128)] + fields + [tend] + [con[n] for n in names],
        [(NF * ROWS, 128), (3 * ROWS, 128)],
        [pltpu.VMEM((NA * WIN, 128), F32), pltpu.VMEM((192, 512), F32)],
        pl.CostEstimate(flops=10**8, bytes_accessed=8 * 10**6, transcendentals=0),
        "tree",
        smem=1,
    )
    return section.reshape(NF, 16, 16, 128), accel.reshape(3, 16, 16, 128)


def solution(mesh):
    placed = (
        P("mx", "my", None),
        P(None, "mx", "my", None),
        P("mx", "my", None),
        P("mx", "my", None),
        P(None, "mx", "my", None),
        P("mx", "my", None),
    )
    return jax.shard_map(
        shards,
        mesh=mesh,
        in_specs=placed,
        out_specs=(P(None, "mx", "my", None), P(None, "mx", "my", None)),
        check_vma=False,
    )
```

profile of v0, /device:TPU:1, one launch (start us, length us, event | category | flops | bytes accessed | tf_op | source)
XLA Modules:
  0.0 97.3 jit_solution(2481449848636361820)
XLA Ops:
  0.6 1.3 %copy-done = f32[9,16,16,128]{3,2,1,0:T(8,128)S(1)} copy-done((f32[9,16,16,128]{3,2,1,0:T(8,128)S(1)}, f32[9,16,16,128]{3,2,1,0:T(8,128)}, u32[]{:S(2)}) %copy-start) | copy-done | bytes 1179672
  1.9 1.0 %copy-done.2 = f32[3,16,16,128]{3,2,1,0:T(8,128)S(1)} copy-done((f32[3,16,16,128]{3,2,1,0:T(8,128)S(1)}, f32[3,16,16,128]{3,2,1,0:T(8,128)}, u32[]{:S(2)}) %copy-start.2) | copy-done | bytes 393240
  5.6 0.9 copy-done.28
  8.8 1.8 %prepare.1 = (f32[24,128]{1,0:T(8,128)S(1)}, f32[50,16,128]{2,1,0:T(8,128)S(1)}, f32[50,16,128]{2,1,0:T(8,128)}, f32[45,16,128]{2,1,0:T(8,128)S(1)}, f32[45,16,128]{2,1,0:T(8,128)}) custom-call(f32[256,128]{1,0:T(8,128)S(1)} %bitcast.25, f32[768,128]{1,0:T(8,128)S(1)} %bitcast.22, f32[256,128]{1,0:T(8,128)S(1)} %bitcast.28, f32[256,128]{1,0:T(8,128)S(1)} %bitcast.31, ...), custom_call_target="tpu_custom_call" | custom-call | flops 10000000 | bytes 3000000 | tf_op jit(solution)/shard_map/prepare/pallas_call | solution.py:542
  12.0 6.8 %all-to-all-start = ((f32[8,24,128]{2,1,0:T(8,128)}), f32[8,24,128]{2,1,0:T(8,128)S(1)}, u32[]{:S(2)}, u32[]{:S(2)}) async-start(f32[8,24,128]{2,1,0:T(8,128)} %broadcast_in_dim.4), calls=%async_computation | async-start | bytes 196608 | tf_op jit(solution)/shard_map/all_to_all | solution.py:577
  18.8 5.0 %all-to-all-done = f32[8,24,128]{2,1,0:T(8,128)S(1)} async-done(((f32[8,24,128]{2,1,0:T(8,128)}), f32[8,24,128]{2,1,0:T(8,128)S(1)}, u32[]{:S(2)}, u32[]{:S(2)}) %all-to-all-start) | async-done | bytes 98336 | tf_op jit(solution)/shard_map/all_to_all | solution.py:577
  24.5 1.3 %collective-permute-start.1 = (f32[50,16,128]{2,1,0:T(8,128)S(1)}, f32[50,16,128]{2,1,0:T(8,128)S(1)}, u32[]{:S(2)}, u32[]{:S(2)}) collective-permute-start(f32[50,16,128]{2,1,0:T(8,128)S(1)} %get-tuple-element.16), channel_id=1, source_target_pairs={{8,0},{16,8},{24,16},{32,24},{40,32},{48,40},{56,48},{64,56},{72,6... | collective-permute-start | bytes 1228808 | tf_op jit(solution)/shard_map/ppermute | solution.py:584
  25.8 4.0 %collective-permute-start = (f32[50,16,128]{2,1,0:T(8,128)}, f32[50,16,128]{2,1,0:T(8,128)S(1)}, u32[]{:S(2)}, u32[]{:S(2)}) collective-permute-start(f32[50,16,128]{2,1,0:T(8,128)} %get-tuple-element.17), channel_id=1, source_target_pairs={{0,8},{8,16},{16,24},{24,32},{32,40},{40,48},{48,56},{56,64},{64,7... | collective-permute-start | bytes 1228808 | tf_op jit(solution)/shard_map/ppermute | solution.py:583
  29.8 3.5 %collective-permute-start.2 = (f32[45,16,128]{2,1,0:T(8,128)}, f32[45,16,128]{2,1,0:T(8,128)S(1)}, u32[]{:S(2)}, u32[]{:S(2)}) collective-permute-start(f32[45,16,128]{2,1,0:T(8,128)} %get-tuple-element.12), channel_id=1, source_target_pairs={{0,1},{1,2},{2,3},{3,4},{4,5},{5,6},{6,7},{8,9},{9,10},{10,11},{11... | collective-permute-start | bytes 1105928 | tf_op jit(solution)/shard_map/ppermute | solution.py:575
  33.2 1.9 %collective-permute-start.3 = (f32[45,16,128]{2,1,0:T(8,128)}, f32[45,16,128]{2,1,0:T(8,128)S(1)}, u32[]{:S(2)}, u32[]{:S(2)}) collective-permute-start(f32[45,16,128]{2,1,0:T(8,128)} %copy-done.45), channel_id=1, source_target_pairs={{1,0},{2,1},{3,2},{4,3},{5,4},{6,5},{7,6},{9,8},{10,9},{11,10},{12... | collective-permute-start | bytes 1105928 | tf_op jit(solution)/shard_map/ppermute | solution.py:576
  35.2 0.9 slice.12
  36.8 8.6 %all-to-all-start.1 = ((f32[16,3,8,128]{3,2,1,0:T(8,128)}), f32[16,3,8,128]{3,2,1,0:T(8,128)}, u32[]{:S(2)}, u32[]{:S(2)}) async-start(f32[16,3,8,128]{3,2,1,0:T(8,128)} %broadcast_in_dim.5), calls=%async_computation.1 | async-start | bytes 393216 | tf_op jit(solution)/shard_map/all_to_all | solution.py:579
  49.8 0.9 copy-done.5
  50.7 0.9 copy-done.8
  51.6 0.9 copy-done.11
  52.5 1.0 %copy-done.14 = f32[50,16,128]{2,1,0:T(8,128)S(1)} copy-done((f32[50,16,128]{2,1,0:T(8,128)S(1)}, f32[50,16,128]{2,1,0:T(8,128)}, u32[]{:S(2)}) %copy-start.14) | copy-done | bytes 409624
  53.5 1.0 %copy-done.16 = f32[50,16,128]{2,1,0:T(8,128)S(1)} copy-done((f32[50,16,128]{2,1,0:T(8,128)S(1)}, f32[50,16,128]{2,1,0:T(8,128)}, u32[]{:S(2)}) %copy-start.16) | copy-done | bytes 409624
  54.5 1.0 %copy-done.18 = f32[45,16,128]{2,1,0:T(8,128)S(1)} copy-done((f32[45,16,128]{2,1,0:T(8,128)S(1)}, f32[45,16,128]{2,1,0:T(8,128)}, u32[]{:S(2)}) %copy-start.18) | copy-done | bytes 368664
  55.5 1.0 %copy-done.20 = f32[45,16,128]{2,1,0:T(8,128)S(1)} copy-done((f32[45,16,128]{2,1,0:T(8,128)S(1)}, f32[45,16,128]{2,1,0:T(8,128)}, u32[]{:S(2)}) %copy-start.20) | copy-done | bytes 368664
  56.5 19.3 %flux.1.tend = f32[3840,128]{1,0:T(8,128)S(1)} custom-call(s32[2]{0:T(128)S(1)} %pad_add_fusion.pos, f32[256,128]{1,0:T(8,128)S(1)} %bitcast.26, f32[768,128]{1,0:T(8,128)S(1)} %bitcast.23, f32[256,128]{1,0:T(8,128)S(1)} %bitcast.29, f32[256,128]{1,0:T(8,128)S(1)} %bitcast.32, f32[2304,128]{1,0:T(8,128)S(1)} %bitcast.20, f32[50,16,128]{2,1,0:T(8,128)S(1)} %copy-done.16, ...), custom_call_target="tpu_custom_call" | custom-call | flops 50000000 | bytes 6000000 | tf_op jit(solution)/shard_map/flux/pallas_call | solution.py:542
  79.2 1.0 copy-done.23
  80.2 1.0 copy-done.24
  81.2 1.0 copy-done.25
  91.2 6.0 %tree.1 = (f32[3840,128]{1,0:T(8,128)}, f32[768,128]{1,0:T(8,128)}) custom-call(s32[2]{0:T(128)S(1)} %copy-done.44, f32[16,3,8,128]{3,2,1,0:T(8,128)} %all-to-all-done.1.far, f32[72,128]{1,0:T(8,128)S(1)} %bitcast.35, f32[80,128]{1,0:T(8,128)S(1)} %bitcast.37, f32[80,128]{1,0:T(8,128)S(1)} %bitcast.36, f32[256,128]{1,0:T(8,128)S(1)} %bitcast.27, ...), custom_call_target="tpu_custom_call" | custom-call | flops 100000000 | bytes 8000000 | tf_op jit(solution)/shard_map/tree/pallas_call | solution.py:542
  (95 shorter events, 24.7 us)
Async XLA Ops:
  0.6 1.3 %copy-start = (f32[9,16,16,128]{3,2,1,0:T(8,128)S(1)}, f32[9,16,16,128]{3,2,1,0:T(8,128)}, u32[]{:S(2)}) copy-start(f32[9,16,16,128]{3,2,1,0:T(8,128)} %param.27) | copy-start | bytes 3538948
  1.9 1.0 %copy-start.2 = (f32[3,16,16,128]{3,2,1,0:T(8,128)S(1)}, f32[3,16,16,128]{3,2,1,0:T(8,128)}, u32[]{:S(2)}) copy-start(f32[3,16,16,128]{3,2,1,0:T(8,128)} %param.24) | copy-start | bytes 1179652
  3.8 0.9 copy-start.7
  5.6 0.9 copy-start.28
  8.8 40.9 %copy-start.1 = (f32[9,16,16,128]{3,2,1,0:T(8,128)S(1)}, f32[9,16,16,128]{3,2,1,0:T(8,128)}, u32[]{:S(2)}) copy-start(f32[9,16,16,128]{3,2,1,0:T(8,128)} %param.27) | copy-start | bytes 3538948
  8.8 40.9 %copy-start.3 = (f32[3,16,16,128]{3,2,1,0:T(8,128)S(1)}, f32[3,16,16,128]{3,2,1,0:T(8,128)}, u32[]{:S(2)}) copy-start(f32[3,16,16,128]{3,2,1,0:T(8,128)} %param.24) | copy-start | bytes 1179652
  12.0 11.8 %all-to-all-start = ((f32[8,24,128]{2,1,0:T(8,128)}), f32[8,24,128]{2,1,0:T(8,128)S(1)}, u32[]{:S(2)}, u32[]{:S(2)}) async-start(f32[8,24,128]{2,1,0:T(8,128)} %broadcast_in_dim.4), calls=%async_computation | async-start | bytes 196608 | tf_op jit(solution)/shard_map/all_to_all | solution.py:577
  24.5 21.0 %collective-permute-start.1 = (f32[50,16,128]{2,1,0:T(8,128)S(1)}, f32[50,16,128]{2,1,0:T(8,128)S(1)}, u32[]{:S(2)}, u32[]{:S(2)}) collective-permute-start(f32[50,16,128]{2,1,0:T(8,128)S(1)} %get-tuple-element.16), channel_id=1, source_target_pairs={{8,0},{16,8},{24,16},{32,24},{40,32},{48,40},{56,48},{64,56},{72,6... | collective-permute-start | bytes 1228808 | tf_op jit(solution)/shard_map/ppermute | solution.py:584
  25.8 21.1 %collective-permute-start = (f32[50,16,128]{2,1,0:T(8,128)}, f32[50,16,128]{2,1,0:T(8,128)S(1)}, u32[]{:S(2)}, u32[]{:S(2)}) collective-permute-start(f32[50,16,128]{2,1,0:T(8,128)} %get-tuple-element.17), channel_id=1, source_target_pairs={{0,8},{8,16},{16,24},{24,32},{32,40},{40,48},{48,56},{56,64},{64,7... | collective-permute-start | bytes 1228808 | tf_op jit(solution)/shard_map/ppermute | solution.py:583
  29.8 18.5 %collective-permute-start.2 = (f32[45,16,128]{2,1,0:T(8,128)}, f32[45,16,128]{2,1,0:T(8,128)S(1)}, u32[]{:S(2)}, u32[]{:S(2)}) collective-permute-start(f32[45,16,128]{2,1,0:T(8,128)} %get-tuple-element.12), channel_id=1, source_target_pairs={{0,1},{1,2},{2,3},{3,4},{4,5},{5,6},{6,7},{8,9},{9,10},{10,11},{11... | collective-permute-start | bytes 1105928 | tf_op jit(solution)/shard_map/ppermute | solution.py:575
  33.2 15.8 %collective-permute-start.3 = (f32[45,16,128]{2,1,0:T(8,128)}, f32[45,16,128]{2,1,0:T(8,128)S(1)}, u32[]{:S(2)}, u32[]{:S(2)}) collective-permute-start(f32[45,16,128]{2,1,0:T(8,128)} %copy-done.45), channel_id=1, source_target_pairs={{1,0},{2,1},{3,2},{4,3},{5,4},{6,5},{7,6},{9,8},{10,9},{11,10},{12... | collective-permute-start | bytes 1105928 | tf_op jit(solution)/shard_map/ppermute | solution.py:576
  36.8 39.0 %all-to-all-start.1 = ((f32[16,3,8,128]{3,2,1,0:T(8,128)}), f32[16,3,8,128]{3,2,1,0:T(8,128)}, u32[]{:S(2)}, u32[]{:S(2)}) async-start(f32[16,3,8,128]{3,2,1,0:T(8,128)} %broadcast_in_dim.5), calls=%async_computation.1 | async-start | bytes 393216 | tf_op jit(solution)/shard_map/all_to_all | solution.py:579
  45.5 3.5 %copy-start.43 = (s32[2]{0:T(128)}, s32[2]{0:T(128)S(1)}, u32[]{:S(2)}) copy-start(s32[2]{0:T(128)S(1)} %pad_add_fusion.pos) | copy-start | bytes 28
  46.9 28.8 %copy-start.38 = (f32[24,24]{1,0:T(8,128)S(1)}, f32[24,24]{1,0:T(8,128)}, u32[]{:S(2)}) copy-start(f32[24,24]{1,0:T(8,128)} %constant.62.clone.down) | copy-start | bytes 6916
  46.9 28.9 %copy-start.41 = (f32[8,128]{1,0:T(8,128)S(1)}, f32[8,128]{1,0:T(8,128)}, u32[]{:S(2)}) copy-start(f32[8,128]{1,0:T(8,128)} %constant.58.clone.mask) | copy-start | bytes 12292
  49.8 0.9 copy-start.5
  52.5 1.0 %copy-start.14 = (f32[50,16,128]{2,1,0:T(8,128)S(1)}, f32[50,16,128]{2,1,0:T(8,128)}, u32[]{:S(2)}) copy-start(f32[50,16,128]{2,1,0:T(8,128)} %copy-done.13) | copy-start | bytes 1228804
  53.5 1.0 %copy-start.16 = (f32[50,16,128]{2,1,0:T(8,128)S(1)}, f32[50,16,128]{2,1,0:T(8,128)}, u32[]{:S(2)}) copy-start(f32[50,16,128]{2,1,0:T(8,128)} %copy-done.15) | copy-start | bytes 1228804
  54.5 1.0 %copy-start.18 = (f32[45,16,128]{2,1,0:T(8,128)S(1)}, f32[45,16,128]{2,1,0:T(8,128)}, u32[]{:S(2)}) copy-start(f32[45,16,128]{2,1,0:T(8,128)} %copy-done.17) | copy-start | bytes 1105924
  55.5 1.0 %copy-start.20 = (f32[45,16,128]{2,1,0:T(8,128)S(1)}, f32[45,16,128]{2,1,0:T(8,128)}, u32[]{:S(2)}) copy-start(f32[45,16,128]{2,1,0:T(8,128)} %copy-done.19) | copy-start | bytes 1105924
  75.8 0.9 copy-start.6
  79.2 1.0 copy-start.23
  80.2 1.0 copy-start.24
  81.2 1.0 copy-start.25
  (29 other events, 22.7 us)
where the time goes:
time: 99 us; the launch traced here: 97.3 us
  local copies, waits for them, and re-layouts  38.2 us (39%)
  Pallas kernels  27 us (27%)
  starting transfers between devices  26.1 us (26%)
  waiting for transfers between devices  5 us (5%)
    unnamed x95, local copies, waits for them, and re-layouts  34.1 us
    pallas_call x3, Pallas kernels, call(): pl.pallas_call(kernel, out_shape=[jax.ShapeDtypeStruct(s, F32) for s in s...  27 us
    all_to_all x1, starting transfers between devices, shards(): lax.all_to_all(jnp.broadcast_to(ones[None], (GX, 3, GY, 128)), 'mx', 0, 0)  8.62 us
    all_to_all x1, starting transfers between devices, shards(): lax.all_to_all(jnp.broadcast_to(pay[None], (GY, 24, 128)), 'my', 0, 0)  6.81 us
    all_to_all x1, waiting for transfers between devices, shards(): lax.all_to_all(jnp.broadcast_to(pay[None], (GY, 24, 128)), 'my', 0, 0)  4.98 us
    ppermute x1, starting transfers between devices, shards(): lax.ppermute(lax.dynamic_update_slice_in_dim(xhi, extra, 45, 0), 'mx', up_x)  4.01 us
    ppermute x1, starting transfers between devices, shards(): yl = lax.ppermute(yhi, 'my', up_y)  3.46 us
  transfers between devices with their start and end apart: 6, of which 1 were waited for; matrix products, arithmetic and copies ran while one was open for 3% of the time, Pallas kernels for 20%

commit v1 on v0

--- a/solution.py
+++ b/solution.py
@@ -76,17 +76,17 @@
                                 -GRAVITY * (-1.0) ** sum(ea) / factorial_of(ea) * inverse_derivative(e, r)
                             )
     out["w_high"], out["w_low"] = split_np(w.reshape(7 * NG, NA * WIN))
-    sel = np.zeros((4, WIN, 72))
+    sel = np.zeros((4, WIN, 40))
     sign = np.zeros((4, 384))
     for c in range(4):
         cx, cy = c >> 1, c & 1
         for i in range(6):
             for j in range(6):
                 si, sj = (5 - i if cx else i), (5 - j if cy else j)
-                sel[c, i * 6 + j, ((si // 2) * 3 + sj // 2) * 8 + (si % 2) * 2 + sj % 2] = 1.0
+                sel[c, i * 6 + j, ((si // 2) * 3 + sj // 2) * 4 + (si % 2) * 2 + sj % 2] = 1.0
         for a, e in enumerate(ALPHA):
             sign[c, a * 16 : a * 16 + 16] = (-1.0) ** (cx * e[0] + cy * e[1])
-    out["sel_zero"] = sel.reshape(4 * WIN, 72).astype(ml_dtypes.bfloat16)
+    out["sel_zero"] = sel.reshape(4 * WIN, 40).astype(ml_dtypes.bfloat16)
     lanes = np.zeros((16, 384), np.float32)
     lanes[0:4] = sign
     for a, e in enumerate(ALPHA):
@@ -236,42 +236,47 @@
 
 
 def power(s):
-    return jnp.exp(GAMMA * jnp.log(s))
-
-
-def field_ref(refs, f):
-    den, mom, ene, ent, tra = refs
-    if f == 0:
-        return den, 0
-    if f < 4:
-        return mom, (f - 1) * ROWS
-    if f == 4:
-        return ene, 0
-    if f == 5:
-        return ent, 0
-    return tra, (f - 6) * ROWS
-
-
-def prepare_kernel(den, mom, ene, ent, tra, flags, left, right, flag, pay, xlo, xhi, ylo, yhi, fl):
-    refs = (den, mom, ene, ent, tra)
-    for f in range(NF):
-        ref, base = field_ref(refs, f)
-        for k in range(3):
-            xlo[f * 3 + k] = ref[base + k * 16 : base + k * 16 + 16]
-            xhi[f * 3 + k] = ref[base + (13 + k) * 16 : base + (13 + k) * 16 + 16]
-            for s in range(2):
-                ylo[f * 3 + k, s * 8 : s * 8 + 8] = ref[pl.ds(base + s * 128 + k, 8, stride=16)]
-                yhi[f * 3 + k, s * 8 : s * 8 + 8] = ref[pl.ds(base + s * 128 + 13 + k, 8, stride=16)]
-    rho = den[...]
+    return jnp.exp2(GAMMA * jnp.log2(s))
+
+
+def root(x):
+    return x * lax.rsqrt(x)
+
+
+PLACES = ((0, 1), (1, 3), (4, 1), (5, 1), (6, 9))
+
+
+def load_all(pairs, sems):
+    copies = [pltpu.make_async_copy(source, target, sems.at[k]) for k, (source, target) in enumerate(pairs)]
+    for copy in copies:
+        copy.start()
+    return copies
+
+
+def fields_into(refs, target, source=slice(0, ROWS), rows=None):
+    place = slice(0, source.stop - source.start) if rows is None else rows
+    return [
+        (ref.at[:, source], target.at[start : start + count, place]) for ref, (start, count) in zip(refs, PLACES)
+    ]
+
+
+def prepare_kernel(den, mom, ene, ent, tra, flags, left, right, flag, pay, xlo, xhi, ylo, yhi, u, fl, flv, leftv, rightv, flagv, sems):
+    small = load_all(zip((flags, left, right, flag), (flv, leftv, rightv, flagv)), sems.at[7:11])
+    loads = load_all(fields_into((den, mom, ene, ent, tra), u), sems.at[0:5])
+    for copy in small:
+        copy.wait()
+    fl[...] = jnp.zeros((8, 128), F32)
+    fl[0:2, 0:16] = flv[0].astype(F32)
+    fl[2:4, 0:16] = flv[1].astype(F32)
+    tile = mxu(fl[...].astype(BF16), flagv[...])
+    for k in (0, 1, 3):
+        loads[k].wait()
+    rho = u[0]
+    sums = exact(leftv[...], exact(rho, rightv[...]))
     inverse = 1.0 / rho
-    fast = jnp.maximum(jnp.maximum(jnp.abs(mom[0:ROWS]), jnp.abs(mom[ROWS : 2 * ROWS])), jnp.abs(mom[2 * ROWS :]))
-    sound = jnp.sqrt(GAMMA * (GAMMA - 1.0) * power(ent[...]) * inverse)
+    fast = jnp.maximum(jnp.maximum(jnp.abs(u[1]), jnp.abs(u[2])), jnp.abs(u[3]))
+    sound = root(GAMMA * (GAMMA - 1.0) * power(u[5]) * inverse)
     fastest = jnp.max(fast * inverse + sound)
-    fl[...] = jnp.zeros((8, 128), F32)
-    fl[0:2, 0:16] = flags[0].astype(F32)
-    fl[2:4, 0:16] = flags[1].astype(F32)
-    tile = mxu(fl[...].astype(BF16), flag[...])
-    sums = exact(left[...], exact(rho, right[...]))
     lane = lane_ids((8, 128))
     row = row_ids((8, 128))
     tiles = [jnp.zeros((8, 128), F32) for _ in range(3)]
@@ -289,8 +294,38 @@
         tiles[c] = jnp.where(here & (row < 4), low, tiles[c])
         tiles[c] = jnp.where(here & (row == 4) & (lane < to + 8), top, tiles[c])
     tiles[2] = jnp.where((row == 4) & (lane >= 64), fastest, tiles[2])
-    for c in range(3):
-        pay[c * 8 : c * 8 + 8] = tiles[c]
+    for y in range(GY):
+        for c in range(3):
+            pay[y, c * 8 : c * 8 + 8] = tiles[c]
+    for k in (2, 4):
+        loads[k].wait()
+    slabs = load_all([(u.at[:, 0:48], xlo), (u.at[:, 208:256], xhi)], sems.at[5:7])
+    for f in range(NF):
+        for k in range(3):
+            for s in range(2):
+                ylo[f, k * 16 + s * 8 : k * 16 + s * 8 + 8] = u[f, pl.ds(s * 128 + k, 8, stride=16)]
+                yhi[f, k * 16 + s * 8 : k * 16 + s * 8 + 8] = u[f, pl.ds(s * 128 + 13 + k, 8, stride=16)]
+    for copy in slabs:
+        copy.wait()
+
+
+def relay_kernel(pos, column, *rest):
+    out = rest[-1]
+    y = pos[1]
+    tiles = [column[pl.ds(c * 8 + 4, 8, stride=24)] for c in range(3)]
+    near = []
+    for dy in range(3):
+        here = jnp.clip(y + dy - 1, 0, GY - 1)
+        inside = here == y + dy - 1
+        for c in range(3):
+            tile = column[pl.ds(pl.multiple_of(here * 24 + c * 8, 8), 8)]
+            near.append(jnp.where(inside, tile, 0.0))
+    for x in range(GX):
+        for c in range(3):
+            out[x, c * 8 : c * 8 + 8] = tiles[c]
+        for n, tile in enumerate(near):
+            out[x, 24 + n * 4 : 28 + n * 4] = tile[0:4]
+        out[x, 60:64] = jnp.zeros((4, 128), F32)
 
 
 def states(ol, il, l, r, ir, orr):
@@ -301,136 +336,172 @@
     return left, right
 
 
-def fluxes(load, d):
+def fluxes(load, d, store):
     rl, rr = load(0)
     ml, mr = load(1 + d)
     sl, sr = load(5)
     il, ir = 1.0 / rl, 1.0 / rr
     vl, vr = ml * il, mr * ir
-    pl_, pr = (GAMMA - 1.0) * power(sl), (GAMMA - 1.0) * power(sr)
-    cl, cr = jnp.sqrt(GAMMA * pl_ * il), jnp.sqrt(GAMMA * pr * ir)
+    gl, gr = power(sl), power(sr)
+    cl, cr = root(GAMMA * (GAMMA - 1.0) * gl * il), root(GAMMA * (GAMMA - 1.0) * gr * ir)
     a = 4.0 * jnp.maximum(jnp.abs(vl) + cl, jnp.abs(vr) + cr)
     wl, wr = 4.0 * vl, 4.0 * vr
     kl, kr = wl + a, wr - a
     got = {0: (rl, rr), 1 + d: (ml, mr), 5: (sl, sr)}
-    out = []
     for f in range(NF):
         left, right = got[f] if f in got else load(f)
         flux = left * kl + right * kr
         if f == 1 + d:
-            flux = flux + 4.0 * (pl_ + pr)
+            flux = flux + (4.0 * (GAMMA - 1.0)) * (gl + gr)
         if f == 4:
-            flux = flux + (pl_ * wl + pr * wr)
-        out.append(flux)
-    return out
-
-
-def flux_kernel(pos, den, mom, ene, ent, tra, xl, xr, yl, yr, out, ux, uy, edge):
-    refs = (den, mom, ene, ent, tra)
-    first_x, last_x = pos[0] == 0, pos[0] == GX - 1
-    first_y, last_y = pos[1] == 0, pos[1] == GY - 1
-    for f in range(NF):
-        ref, base = field_ref(refs, f)
-        ux[f, 48 : 48 + ROWS] = ref[base : base + ROWS]
+            flux = flux + (GAMMA - 1.0) * (gl * wl + gr * wr)
+        store(f, flux)
+
+
+def sweep(buf, target, d):
+    def step(i, carry):
         for s in range(2):
-            rows = slice(s * 8, s * 8 + 8)
+
+            def load(f):
+                return states(*[buf[f, pl.ds(pl.multiple_of((i + k) * 16 + s * 8, 8), 8)] for k in range(6)])
+
+            def store(f, flux):
+                target[f, pl.ds(pl.multiple_of(i * 16 + s * 8, 8), 8)] = flux
+
+            fluxes(load, d, store)
+        return carry
+
+    lax.fori_loop(0, 17, step, 0)
+
+
+def flux_z_kernel(den, mom, ene, ent, tra, out_h, u, uz, fz, turn, out, sems):
+    row = row_ids((8, 128))
+    loads = load_all(fields_into((den, mom, ene, ent, tra), u), sems.at[0:5])
+
+    def into(f, carry):
+        for half in range(2):
+            turn[half] = u[f, half * 128 : half * 128 + 128].T
+            cells = [turn[half, pl.ds(m, 8, stride=16)] for m in range(16)]
+            first = jnp.broadcast_to(cells[0][0:1], (8, 128))
+            last = jnp.broadcast_to(cells[15][7:8], (8, 128))
+            below = [jnp.where(row == 0, first, pltpu.roll(cells[m], 1, 0)) for m in (13, 14, 15)]
+            above = [jnp.where(row == 7, last, pltpu.roll(cells[m], 7, 0)) for m in (0, 1, 2)]
+            for m, value in enumerate(below + cells + above):
+                uz[f, m * 16 + half * 8 : m * 16 + half * 8 + 8] = value
+        return carry
+
+    for copy, (start, n) in zip(loads, PLACES):
+        copy.wait()
+        lax.fori_loop(start, start + n, into, 0)
+    sweep(uz, fz, 2)
+
+    def back(f, carry):
+        for half in range(2):
+            at = half * 8
+            for m in range(16):
+                low = fz[f, m * 16 + at : m * 16 + at + 8]
+                high = fz[f, m * 16 + 16 + at : m * 16 + 24 + at]
+                turn[half, pl.ds(m, 8, stride=16)] = low - high
+            out[f, half * 128 : half * 128 + 128] = turn[half].T
+        return carry
+
+    stores = []
+    for part in range(3):
+        lax.fori_loop(part * 5, part * 5 + 5, back, 0)
+        some = slice(part * 5, part * 5 + 5)
+        stores.append(pltpu.make_async_copy(out.at[some], out_h.at[some], sems.at[5 + part]))
+        stores[-1].start()
+    for copy in stores:
+        copy.wait()
+
+
+def flux_xy_kernel(pos, den, mom, ene, ent, tra, along_z_h, xl, xr, yl, yr, out_h, ux, uy, fx, fy, along_z, out, sems):
+    interior = load_all(fields_into((den, mom, ene, ent, tra), ux, rows=slice(48, 304)), sems.at[0:5])
+    loads = load_all(
+        [
+            (yl, uy.at[:, 0:48]),
+            (yr, uy.at[:, 304:352]),
+            (xl, ux.at[:, 0:48]),
+            (xr, ux.at[:, 304:352]),
+            (along_z_h, along_z),
+        ],
+        sems.at[5:10],
+    )
+    for copy, (start, n) in zip(interior, PLACES):
+        copy.wait()
+        for f in range(start, start + n):
             for y in range(16):
-                uy[f, (3 + y) * 16 + s * 8 : (3 + y) * 16 + s * 8 + 8] = ref[pl.ds(base + s * 128 + y, 8, stride=16)]
-            lo, hi = ref[base + s * 8 : base + s * 8 + 8], ref[base + 240 + s * 8 : base + 248 + s * 8]
-            ylo, yhi = ref[pl.ds(base + s * 128, 8, stride=16)], ref[pl.ds(base + s * 128 + 15, 8, stride=16)]
+                for s in range(2):
+                    at = (3 + y) * 16 + s * 8
+                    uy[f, at : at + 8] = ux[f, pl.ds(48 + s * 128 + y, 8, stride=16)]
+    for copy in loads[:-1]:
+        copy.wait()
+
+    def repeat(buf, source, target):
+        for f in range(NF):
+            cells = buf[f, source : source + 16]
             for k in range(3):
-                ux[f, k * 16 + s * 8 : k * 16 + s * 8 + 8] = jnp.where(first_x, lo, xl[f * 3 + k, rows])
-                ux[f, (19 + k) * 16 + s * 8 : (19 + k) * 16 + s * 8 + 8] = jnp.where(last_x, hi, xr[f * 3 + k, rows])
-                uy[f, k * 16 + s * 8 : k * 16 + s * 8 + 8] = jnp.where(first_y, ylo, yl[f * 3 + k, rows])
-                uy[f, (19 + k) * 16 + s * 8 : (19 + k) * 16 + s * 8 + 8] = jnp.where(last_y, yhi, yr[f * 3 + k, rows])
-
-    def sweep(buf, d, s, emit):
-        def faces(i):
-            def load(f):
-                cells = [buf[f, pl.ds(pl.multiple_of((i + k) * 16 + s * 8, 8), 8)] for k in range(6)]
-                return states(*cells)
-
-            return fluxes(load, d)
-
-        def step(i, before):
-            now = faces(i)
-            for f in range(NF):
-                emit(f, i - 1, before[f] - now[f])
-            return tuple(now)
-
-        lax.fori_loop(1, 17, step, tuple(faces(0)))
-
-    for s in range(2):
-
-        def emit_y(f, y, value, s=s):
-            out[pl.ds(f * ROWS + s * 128 + y, 8, stride=16)] = value
-
-        sweep(uy, 1, s, emit_y)
-    for s in range(2):
-
-        def emit_x(f, x, value, s=s):
-            at = pl.ds(pl.multiple_of(f * ROWS + x * 16 + s * 8, 8), 8)
-            out[at] = out[at] + value
-
-        sweep(ux, 0, s, emit_x)
-
-    lane = lane_ids((8, 128))
-    group = lane // 8
-    for s in range(2):
-
-        def load_edge(f, s=s):
-            packed = jnp.zeros((8, 128), F32)
-            for x in range(16):
-                u = ux[f, (3 + x) * 16 + s * 8 : (3 + x) * 16 + s * 8 + 8]
-                packed = jnp.where(group == x, pltpu.roll(u, x * 8, 1), packed)
-            one, two = pltpu.roll(packed, 127, 1), pltpu.roll(packed, 126, 1)
-            return states(packed, packed, packed, packed, one, two)
-
-        for f, value in enumerate(fluxes(load_edge, 2)):
-            edge[f, s * 8 : s * 8 + 8] = value
-    low_end, high_end = lane == 0, lane == 127
-
-    def along_z(i, carry):
-        x, s = i // 2, i % 2
-        at = pl.multiple_of(i * 8, 8)
-
-        def load(f):
-            u = ux[f, pl.ds(48 + at, 8)]
-            m1 = jnp.where(low_end, u, pltpu.roll(u, 1, 1))
-            m2 = jnp.where(low_end, u, pltpu.roll(m1, 1, 1))
-            p1 = jnp.where(high_end, u, pltpu.roll(u, 127, 1))
-            p2 = jnp.where(high_end, u, pltpu.roll(p1, 127, 1))
-            p3 = jnp.where(high_end, u, pltpu.roll(p2, 127, 1))
-            return states(m2, m1, u, p1, p2, p3)
-
-        for f, value in enumerate(fluxes(load, 2)):
-            lower = pltpu.roll(edge[f, pl.ds(pl.multiple_of(s * 8, 8), 8)], lax.rem(128 - x * 8, 128), 1)
-            below = jnp.where(low_end, lower, pltpu.roll(value, 1, 1))
-            rows = pl.ds(pl.multiple_of(f * ROWS + i * 8, 8), 8)
-            out[rows] = out[rows] + (below - value)
+                buf[f, target + k * 16 : target + k * 16 + 16] = cells
+
+    pl.when(pos[0] == 0)(lambda: repeat(ux, 48, 0))
+    pl.when(pos[0] == GX - 1)(lambda: repeat(ux, 288, 304))
+    pl.when(pos[1] == 0)(lambda: repeat(uy, 48, 0))
+    pl.when(pos[1] == GY - 1)(lambda: repeat(uy, 288, 304))
+    sweep(uy, fy, 1)
+    sweep(ux, fx, 0)
+    loads[-1].wait()
+
+    def gather(x, carry):
+        for f in range(NF):
+            for s in range(2):
+                at = pl.multiple_of(x * 16 + s * 8, 8)
+                change = along_z[f, pl.ds(at, 8)] + (fx[f, pl.ds(at, 8)] - fx[f, pl.ds(at + 16, 8)])
+                low, high = fy[f, pl.ds(s * 128 + x, 8, stride=16)], fy[f, pl.ds(s * 128 + 16 + x, 8, stride=16)]
+                out[f, pl.ds(at, 8)] = change + (low - high)
         return carry
 
-    lax.fori_loop(0, 32, along_z, 0)
+    stores = []
+    for part in range(4):
+        lax.fori_loop(part * 4, part * 4 + 4, gather, 0)
+        rows = slice(part * 64, part * 64 + 64)
+        stores.append(pltpu.make_async_copy(out.at[:, rows], out_h.at[:, rows], sems.at[10 + part]))
+        stores[-1].start()
+    for copy in stores:
+        copy.wait()
+
+
+TREE_CONSTANTS = (
+    "w_high", "w_low", "sel_zero", "lane_odd", "up", "alpha_odd", "agg", "mask", "info", "expand", "gamma_odd", "down",
+    "spread", "poly",
+)
 
 
 def tree_kernel(
-    pos, far, mid, xl, xr, den, mom, ene, ent, tra, tend,
-    w_high, w_low, sel_zero, lane_odd, up, alpha_odd, agg, mask, info, expand, gamma_odd, down, spread, poly,
-    section, accel, rhs, field,
+    pos, far_h, den, mom, ene, ent, tra, change_h, *args,
 ):
+    count = len(TREE_CONSTANTS)
+    section, accel, rhs, field, result, force, far, change, u, sems = args[count : count + 10]
+    loaded = args[count + 10 :]
+    late = fields_into((den, mom, ene, ent, tra), u) + [(change_h, change)]
+    loads = load_all([(far_h, far)] + list(zip(args[:count], loaded)) + late, sems)
+    for copy in loads[: 1 + count]:
+        copy.wait()
+    (w_high, w_low, sel_zero, lane_odd, up, alpha_odd, agg, mask, info, expand, gamma_odd, down, spread, poly) = loaded
     px, py = pos[0], pos[1]
+    blocks = []
+    for dx in range(3):
+        here = jnp.clip(px + dx - 1, 0, GX - 1)
+        inside = here == px + dx - 1
+        blocks.append([jnp.where(inside, far[here, 24 + n * 4 : 28 + n * 4], 0.0) for n in range(9)])
+    gap = jnp.zeros((4, 128), F32)
     around = jnp.concatenate(
-        [
-            jnp.concatenate([ref[(dy * 3 + c) * 8 : (dy * 3 + c) * 8 + 8] for ref in (xl, mid, xr) for dy in range(3)], 0)
-            for c in range(3)
-        ],
-        1,
+        [jnp.concatenate([blocks[dx][dy * 3 + c] for dx in range(3) for dy in range(3)] + [gap], 0) for c in range(3)], 1
     )
     zero = mxu(sel_zero[...], jnp.concatenate(split(around), 1))
     zero = zero[:, :384] + zero[:, 384:]
     arrays = [zero[c * WIN : c * WIN + WIN] * lane_odd[c : c + 1] for c in range(4)]
-    gathered = jnp.concatenate([far[:, c].reshape(128, 128) for c in range(3)], 1)
-    speeds = far[:, 2].reshape(128, 128)
+    gathered = jnp.concatenate([far[:, c * 8 : c * 8 + 8].reshape(128, 128) for c in range(3)], 1)
+    speeds = gathered[:, 256:]
     fastest = jnp.max(jnp.where(lane_ids((128, 128)) >= 64, speeds, 0.0))
 
     def lifted(x, x_odd, y_odd):
@@ -511,98 +582,128 @@
     )
     field[...] = exact(poly[...], terms)
     step = jnp.full((8, 128), COURANT / SUB, F32) / fastest
-    refs = (den, mom, ene, ent, tra)
-
-    def finish(x, carry):
-        for c in range(4):
-            at = pl.multiple_of(((c >> 1) * 8 + x) * 16 + (c & 1) * 8, 8)
-            acc = [field[pl.ds(pl.multiple_of(i * 64 + x * 8, 8), 8), c * 128 : c * 128 + 128] for i in range(3)]
-            rho = den[pl.ds(at, 8)]
-            moms = [mom[pl.ds(i * ROWS + at, 8)] for i in range(3)]
-            for i in range(3):
-                accel[pl.ds(i * ROWS + at, 8)] = acc[i]
-            for f in range(NF):
-                ref, start = field_ref(refs, f)
-                change = tend[pl.ds(f * ROWS + at, 8)]
-                if 1 <= f <= 3:
-                    change = change + rho * acc[f - 1]
-                if f == 4:
-                    change = change + moms[0] * acc[0] + moms[1] * acc[1] + moms[2] * acc[2]
-                section[pl.ds(f * ROWS + at, 8)] = ref[pl.ds(start + at, 8)] + step * change
-        return carry
-
-    lax.fori_loop(0, 8, finish, 0)
-
-
+    for copy in loads[1 + count :]:
+        copy.wait()
+    stores = []
+    for half in range(2):
+
+        def finish(x, carry, half=half):
+            for s in range(2):
+                c = half * 2 + s
+                at = pl.multiple_of(half * 128 + x * 16 + s * 8, 8)
+                rows = pl.ds(at, 8)
+                acc = [field[pl.ds(pl.multiple_of(i * 64 + x * 8, 8), 8), c * 128 : c * 128 + 128] for i in range(3)]
+                old = [u[f, rows] for f in range(NF)]
+                for i in range(3):
+                    force[i, rows] = acc[i]
+                for f in range(NF):
+                    slope = change[f, rows]
+                    if 1 <= f <= 3:
+                        slope = slope + old[0] * acc[f - 1]
+                    if f == 4:
+                        slope = slope + (old[1] * acc[0] + old[2] * acc[1] + old[3] * acc[2])
+                    result[f, rows] = old[f] + step * slope
+            return carry
+
+        lax.fori_loop(0, 8, finish, 0)
+        rows = slice(half * 128, half * 128 + 128)
+        for k, (source, target) in enumerate(((result, section), (force, accel))):
+            stores.append(pltpu.make_async_copy(source.at[:, rows], target.at[:, rows], sems.at[2 * half + k]))
+            stores[-1].start()
+    for copy in stores:
+        copy.wait()
+
+
+ANY = pl.BlockSpec(memory_space=pl.ANY)
+HBM = pl.BlockSpec(memory_space=pltpu.HBM)
 VMEM = pl.BlockSpec(memory_space=pltpu.VMEM)
 SMEM = pl.BlockSpec(memory_space=pltpu.SMEM)
 
 
-def call(kernel, ins, shapes, scratch, cost, name, smem=0):
+def call(kernel, name, ins, outs, scratch, cost):
     return pl.pallas_call(
         kernel,
-        out_shape=[jax.ShapeDtypeStruct(s, F32) for s in shapes],
-        in_specs=[SMEM] * smem + [VMEM] * (len(ins) - smem),
-        out_specs=[VMEM] * len(shapes),
+        out_shape=[pltpu.HBM(s, F32) if spec is HBM else jax.ShapeDtypeStruct(s, F32) for s, spec in outs],
+        in_specs=[spec for _, spec in ins],
+        out_specs=[spec for _, spec in outs],
         scratch_shapes=scratch,
-        cost_estimate=cost,
+        cost_estimate=pl.CostEstimate(flops=cost[0], bytes_accessed=cost[1], transcendentals=cost[2]),
         name=name,
-        compiler_params=pltpu.CompilerParams(vmem_limit_bytes=48 << 20),
-    )(*ins)
+        compiler_params=pltpu.CompilerParams(vmem_limit_bytes=32 << 20),
+    )(*[in_hbm(x) if spec is HBM else x for x, spec in ins])
+
+
+def in_hbm(x):
+    return pltpu.with_memory_space_constraint(x, pltpu.HBM)
+
+
+def scratch_like(x):
+    return pltpu.VMEM(x.shape, x.dtype)
 
 
 def shards(density, momentum, energy, entropy, tracers, leaf_flags):
     con = {k: jnp.asarray(v) for k, v in constants().items()}
-    fields = [
-        density.reshape(ROWS, 128),
-        momentum.reshape(3 * ROWS, 128),
-        energy.reshape(ROWS, 128),
-        entropy.reshape(ROWS, 128),
-        tracers.reshape(9 * ROWS, 128),
-    ]
+    fields = [(x.reshape(-1, ROWS, 128), HBM) for x in (density, momentum, energy, entropy, tracers)]
     ix, iy = lax.axis_index("mx"), lax.axis_index("my")
-    pos = jnp.stack([ix, iy]).astype(jnp.int32)
+    pos = (jnp.stack([ix, iy]).astype(jnp.int32), SMEM)
+    first = [con[n] for n in ("left", "right", "flag")]
+    whole = (NF, ROWS, 128)
+    slab = ((NF, 48, 128), HBM)
     pay, xlo, xhi, ylo, yhi = call(
         prepare_kernel,
-        fields + [leaf_flags, con["left"], con["right"], con["flag"]],
-        [(24, 128), (50, 16, 128), (50, 16, 128), (45, 16, 128), (45, 16, 128)],
-        [pltpu.VMEM((8, 128), F32)],
-        pl.CostEstimate(flops=10**7, bytes_accessed=3 * 10**6, transcendentals=10**5),
         "prepare",
+        fields + [(leaf_flags, HBM)] + [(x, HBM) for x in first],
+        [((GY, 24, 128), VMEM), slab, slab, ((NF, 48, 128), VMEM), ((NF, 48, 128), VMEM)],
+        [pltpu.VMEM(whole, F32), pltpu.VMEM((8, 128), F32), scratch_like(leaf_flags)] + [scratch_like(x) for x in first] + [pltpu.SemaphoreType.DMA((11,))],
+        (10**7, 4 * 10**6, 10**5),
     )
     up_x, down_x = [(i, i + 1) for i in range(GX - 1)], [(i + 1, i) for i in range(GX - 1)]
     up_y, down_y = [(i, i + 1) for i in range(GY - 1)], [(i + 1, i) for i in range(GY - 1)]
+    column = lax.all_to_all(pay, "my", 0, 0)
     yl = lax.ppermute(yhi, "my", up_y)
     yr = lax.ppermute(ylo, "my", down_y)
-    column = lax.all_to_all(jnp.broadcast_to(pay[None], (GY, 24, 128)), "my", 0, 0)
-    ones = jnp.transpose(column.reshape(GY, 3, 8, 128)[:, :, 4], (1, 0, 2))
-    far = lax.all_to_all(jnp.broadcast_to(ones[None], (GX, 3, GY, 128)), "mx", 0, 0)
-    padded = jnp.pad(column, ((1, 1), (0, 0), (0, 0)))
-    mid = lax.dynamic_slice_in_dim(padded, iy, 3, 0).reshape(72, 128)
-    extra = jnp.pad(mid, ((0, 8), (0, 0))).reshape(5, 16, 128)
-    xl = lax.ppermute(lax.dynamic_update_slice_in_dim(xhi, extra, 45, 0), "mx", up_x)
-    xr = lax.ppermute(lax.dynamic_update_slice_in_dim(xlo, extra, 45, 0), "mx", down_x)
+    xl = lax.ppermute(xhi, "mx", up_x)
+    xr = lax.ppermute(xlo, "mx", down_x)
+    block = pltpu.VMEM(whole, F32)
+    extended, faces = pltpu.VMEM((NF, 352, 128), F32), pltpu.VMEM((NF, 272, 128), F32)
+    (along_z,) = call(
+        flux_z_kernel,
+        "flux_z",
+        fields,
+        [(whole, HBM)],
+        [block, extended, faces, pltpu.VMEM((2, 128, 128), F32), block, pltpu.SemaphoreType.DMA((8,))],
+        (2 * 10**7, 4 * 10**6, 3 * 10**5),
+    )
+    (chunks,) = call(
+        relay_kernel, "relay", [pos, (column.reshape(GY * 24, 128), VMEM), (along_z, HBM)] + [(x, ANY) for x in (xl, xr, yl, yr)], [((GX, 64, 128), VMEM)], [], (10**4, 10**6, 0)
+    )
+    far = lax.all_to_all(chunks, "mx", 0, 0)
     (tend,) = call(
-        flux_kernel,
-        [pos] + fields + [xl, xr, yl, yr],
-        [(NF * ROWS, 128)],
-        [pltpu.VMEM((NF, 22 * 16, 128), F32), pltpu.VMEM((NF, 22 * 16, 128), F32), pltpu.VMEM((NF, 16, 128), F32)],
-        pl.CostEstimate(flops=5 * 10**7, bytes_accessed=6 * 10**6, transcendentals=10**6),
-        "flux",
-        smem=1,
-    )
-    names = (
-        "w_high", "w_low", "sel_zero", "lane_odd", "up", "alpha_odd", "agg", "mask", "info", "expand", "gamma_odd",
-        "down", "spread", "poly",
-    )
+        flux_xy_kernel,
+        "flux_xy",
+        [pos] + fields + [(along_z, HBM)] + [(x, ANY) for x in (xl, xr, yl, yr)],
+        [(whole, HBM)],
+        [extended, extended, faces, faces, block, block, pltpu.SemaphoreType.DMA((14,))],
+        (4 * 10**7, 6 * 10**6, 6 * 10**5),
+    )
+    second = [con[n] for n in TREE_CONSTANTS]
     section, accel = call(
         tree_kernel,
-        [pos, far, mid, xl[45:].reshape(80, 128), xr[45:].reshape(80, 128)] + fields + [tend] + [con[n] for n in names],
-        [(NF * ROWS, 128), (3 * ROWS, 128)],
-        [pltpu.VMEM((NA * WIN, 128), F32), pltpu.VMEM((192, 512), F32)],
-        pl.CostEstimate(flops=10**8, bytes_accessed=8 * 10**6, transcendentals=0),
         "tree",
-        smem=1,
+        [pos, (far, ANY)] + fields + [(tend, HBM)] + [(x, HBM) for x in second],
+        [(whole, ANY), ((3, ROWS, 128), ANY)],
+        [
+            pltpu.VMEM((NA * WIN, 128), F32),
+            pltpu.VMEM((192, 512), F32),
+            pltpu.VMEM(whole, F32),
+            pltpu.VMEM((3, ROWS, 128), F32),
+            pltpu.VMEM((GX, 64, 128), F32),
+            block,
+            block,
+            pltpu.SemaphoreType.DMA((7 + len(second),)),
+        ]
+        + [scratch_like(x) for x in second],
+        (10**8, 8 * 10**6, 0),
     )
     return section.reshape(NF, 16, 16, 128), accel.reshape(3, 16, 16, 128)
 

time: 99 us -> 57 us (0.58)
  the two profiles are of different devices: /device:TPU:1 before, /device:TPU:0 now
where the time goes in v1:
time: 57 us; the launch traced here: 56.6 us
  Pallas kernels  29.1 us (51%)
  starting transfers between devices  23.8 us (42%)
  waiting for transfers between devices  2.84 us (5%)
  between operations  0.72 us (1%)
    pallas_call x5, Pallas kernels, call(): pl.pallas_call(kernel, out_shape=[pltpu.HBM(s, F32) if spec is HBM else j...  29.1 us
    all_to_all x1, starting transfers between devices, shards(): far = lax.all_to_all(chunks, 'mx', 0, 0)  8.17 us
    all_to_all x1, starting transfers between devices, shards(): column = lax.all_to_all(pay, 'my', 0, 0)  8.11 us
    ppermute x1, starting transfers between devices, shards(): xl = lax.ppermute(xhi, 'mx', up_x)  3.5 us
    all_to_all x1, waiting for transfers between devices, shards(): far = lax.all_to_all(chunks, 'mx', 0, 0)  2.83 us
    ppermute x1, starting transfers between devices, shards(): yl = lax.ppermute(yhi, 'my', up_y)  1.48 us
    ppermute x1, starting transfers between devices, shards(): xr = lax.ppermute(xlo, 'mx', down_x)  1.29 us
    ppermute x1, starting transfers between devices, shards(): yr = lax.ppermute(ylo, 'my', down_y)  1.29 us
  transfers between devices with their start and end apart: 6, of which 1 were waited for; matrix products, arithmetic and copies ran while one was open for 0% of the time, Pallas kernels for 30%

profile of v1, /device:TPU:0, one launch (start us, length us, event | category | flops | bytes accessed | tf_op | source)
XLA Modules:
  0.0 56.6 jit_solution(8379963351374139250)
XLA Ops:
  0.6 3.7 %prepare.1 = (f32[8,24,128]{2,1,0:T(8,128)}, f32[15,48,128]{2,1,0:T(8,128)}, f32[15,48,128]{2,1,0:T(8,128)}, f32[15,48,128]{2,1,0:T(8,128)S(1)}, f32[15,48,128]{2,1,0:T(8,128)S(1)}) custom-call(f32[1,256,128]{2,1,0:T(8,128)} %bitcast.19, f32[3,256,128]{2,1,0:T(8,128)} %bitcast.15, f32[1,256,128]{2,1,0:T(8,128)} %bitcast.23, f32[1,256,128]{2,1,0:T(8,128)} %bitcast.27, ...), custom_call_target="tpu_custom_call" | custom-call | flops 10000000 | bytes 4000000 | tf_op jit(solution)/shard_map/prepare/pallas_call | solution.py:624
  4.3 3.5 %collective-permute-start = (f32[15,48,128]{2,1,0:T(8,128)}, f32[15,48,128]{2,1,0:T(8,128)S(1)}, u32[]{:S(2)}, u32[]{:S(2)}) collective-permute-start(f32[15,48,128]{2,1,0:T(8,128)} %get-tuple-element.10), channel_id=1, source_target_pairs={{0,8},{8,16},{16,24},{24,32},{32,40},{40,48},{48,56},{56,64},{64,7... | collective-permute-start | bytes 1105928 | tf_op jit(solution)/shard_map/ppermute | solution.py:665
  7.8 1.3 %collective-permute-start.1 = (f32[15,48,128]{2,1,0:T(8,128)}, f32[15,48,128]{2,1,0:T(8,128)S(1)}, u32[]{:S(2)}, u32[]{:S(2)}) collective-permute-start(f32[15,48,128]{2,1,0:T(8,128)} %get-tuple-element.11), channel_id=1, source_target_pairs={{8,0},{16,8},{24,16},{32,24},{40,32},{48,40},{56,48},{64,56},{72,6... | collective-permute-start | bytes 1105928 | tf_op jit(solution)/shard_map/ppermute | solution.py:666
  9.1 1.5 %collective-permute-start.2 = (f32[15,48,128]{2,1,0:T(8,128)S(1)}, f32[15,48,128]{2,1,0:T(8,128)S(1)}, u32[]{:S(2)}, u32[]{:S(2)}) collective-permute-start(f32[15,48,128]{2,1,0:T(8,128)S(1)} %get-tuple-element.12), channel_id=1, source_target_pairs={{0,1},{1,2},{2,3},{3,4},{4,5},{5,6},{6,7},{8,9},{9,10},{10,11},{11... | collective-permute-start | bytes 1105928 | tf_op jit(solution)/shard_map/ppermute | solution.py:663
  10.6 1.3 %collective-permute-start.3 = (f32[15,48,128]{2,1,0:T(8,128)S(1)}, f32[15,48,128]{2,1,0:T(8,128)S(1)}, u32[]{:S(2)}, u32[]{:S(2)}) collective-permute-start(f32[15,48,128]{2,1,0:T(8,128)S(1)} %get-tuple-element.13), channel_id=1, source_target_pairs={{1,0},{2,1},{3,2},{4,3},{5,4},{6,5},{7,6},{9,8},{10,9},{11,10},{12... | collective-permute-start | bytes 1105928 | tf_op jit(solution)/shard_map/ppermute | solution.py:664
  11.9 8.1 %all-to-all-start = ((f32[8,24,128]{2,1,0:T(8,128)}), f32[8,24,128]{2,1,0:T(8,128)S(1)}, u32[]{:S(2)}, u32[]{:S(2)}) async-start(f32[8,24,128]{2,1,0:T(8,128)} %get-tuple-element.9), calls=%async_computation | async-start | bytes 196608 | tf_op jit(solution)/shard_map/all_to_all | solution.py:662
  20.0 7.6 %flux_z.1.rest_0_.along_z_h = f32[15,256,128]{2,1,0:T(8,128)} custom-call(f32[1,256,128]{2,1,0:T(8,128)} %bitcast.20, f32[3,256,128]{2,1,0:T(8,128)} %bitcast.16, f32[1,256,128]{2,1,0:T(8,128)} %bitcast.24, f32[1,256,128]{2,1,0:T(8,128)} %bitcast.28, f32[9,256,128]{2,1,0:T(8,128)} %bitcast.12), custom_call_target="tpu_custom_call" | custom-call | flops 20000000 | bytes 4000000 | tf_op jit(solution)/shard_map/flux_z/pallas_call | solution.py:624
  27.7 0.1 pad_add_fusion.pos
  27.8 0.0 all-to-all-done
  27.8 0.0 collective-permute-done.rest_1_.xl
  27.8 0.0 collective-permute-done.1.rest_2_.xr
  27.8 0.0 collective-permute-done.2.rest_3_.yl
  27.8 0.0 collective-permute-done.3.rest_4_.yr
  27.8 1.4 %relay.1 = f32[16,64,128]{2,1,0:T(8,128)} custom-call(s32[2]{0:T(128)S(1)} %pad_add_fusion.pos, f32[192,128]{1,0:T(8,128)S(1)} %bitcast.10, f32[15,256,128]{2,1,0:T(8,128)} %flux_z.1.rest_0_.along_z_h, f32[15,48,128]{2,1,0:T(8,128)S(1)} %collective-permute-done.rest_1_.xl, f32[15,48,128]{2,1,0:T(8,128)S(1)} %collective-permute-done.1.rest_2_.xr, ...), custom_call_target="tpu_custom_call" | custom-call | flops 10000 | bytes 1000000 | tf_op jit(solution)/shard_map/relay/pallas_call | solution.py:624
  29.2 8.2 %all-to-all-start.1 = ((f32[16,64,128]{2,1,0:T(8,128)}), f32[16,64,128]{2,1,0:T(8,128)S(1)}, u32[]{:S(2)}, u32[]{:S(2)}) async-start(f32[16,64,128]{2,1,0:T(8,128)} %relay.1), calls=%async_computation.1 | async-start | bytes 1048576 | tf_op jit(solution)/shard_map/all_to_all | solution.py:680
  37.4 9.4 %flux_xy.1.change_h = f32[15,256,128]{2,1,0:T(8,128)} custom-call(s32[2]{0:T(128)S(1)} %pad_add_fusion.pos, f32[1,256,128]{2,1,0:T(8,128)} %bitcast.21, f32[3,256,128]{2,1,0:T(8,128)} %bitcast.17, f32[1,256,128]{2,1,0:T(8,128)} %bitcast.25, f32[1,256,128]{2,1,0:T(8,128)} %bitcast.29, f32[9,256,128]{2,1,0:T(8,128)} %bitcast.13, ...), custom_call_target="tpu_custom_call" | custom-call | flops 40000000 | bytes 6000000 | tf_op jit(solution)/shard_map/flux_xy/pallas_call | solution.py:624
  46.8 2.8 %all-to-all-done.1.far_h = f32[16,64,128]{2,1,0:T(8,128)S(1)} async-done(((f32[16,64,128]{2,1,0:T(8,128)}), f32[16,64,128]{2,1,0:T(8,128)S(1)}, u32[]{:S(2)}, u32[]{:S(2)}) %all-to-all-start.1) | async-done | bytes 524320 | tf_op jit(solution)/shard_map/all_to_all | solution.py:680
  49.6 7.0 %tree.1 = (f32[15,256,128]{2,1,0:T(8,128)}, f32[3,256,128]{2,1,0:T(8,128)}) custom-call(s32[2]{0:T(128)S(1)} %pad_add_fusion.pos, f32[16,64,128]{2,1,0:T(8,128)S(1)} %all-to-all-done.1.far_h, f32[1,256,128]{2,1,0:T(8,128)} %bitcast.22, f32[3,256,128]{2,1,0:T(8,128)} %bitcast.18, f32[1,256,128]{2,1,0:T(8,128)} %bitcast.26, f32[1,256,128]{2,1,0:T(8,128)} %bitcast.30, ...), custom_call_target="tpu_custom_call" | custom-call | flops 100000000 | bytes 8000000 | tf_op jit(solution)/shard_map/tree/pallas_call | solution.py:624
Async XLA Ops:
  4.3 23.4 %collective-permute-start = (f32[15,48,128]{2,1,0:T(8,128)}, f32[15,48,128]{2,1,0:T(8,128)S(1)}, u32[]{:S(2)}, u32[]{:S(2)}) collective-permute-start(f32[15,48,128]{2,1,0:T(8,128)} %get-tuple-element.10), channel_id=1, source_target_pairs={{0,8},{8,16},{16,24},{24,32},{32,40},{40,48},{48,56},{56,64},{64,7... | collective-permute-start | bytes 1105928 | tf_op jit(solution)/shard_map/ppermute | solution.py:665
  7.8 19.9 %collective-permute-start.1 = (f32[15,48,128]{2,1,0:T(8,128)}, f32[15,48,128]{2,1,0:T(8,128)S(1)}, u32[]{:S(2)}, u32[]{:S(2)}) collective-permute-start(f32[15,48,128]{2,1,0:T(8,128)} %get-tuple-element.11), channel_id=1, source_target_pairs={{8,0},{16,8},{24,16},{32,24},{40,32},{48,40},{56,48},{64,56},{72,6... | collective-permute-start | bytes 1105928 | tf_op jit(solution)/shard_map/ppermute | solution.py:666
  9.1 18.6 %collective-permute-start.2 = (f32[15,48,128]{2,1,0:T(8,128)S(1)}, f32[15,48,128]{2,1,0:T(8,128)S(1)}, u32[]{:S(2)}, u32[]{:S(2)}) collective-permute-start(f32[15,48,128]{2,1,0:T(8,128)S(1)} %get-tuple-element.12), channel_id=1, source_target_pairs={{0,1},{1,2},{2,3},{3,4},{4,5},{5,6},{6,7},{8,9},{9,10},{10,11},{11... | collective-permute-start | bytes 1105928 | tf_op jit(solution)/shard_map/ppermute | solution.py:663
  10.6 17.2 %collective-permute-start.3 = (f32[15,48,128]{2,1,0:T(8,128)S(1)}, f32[15,48,128]{2,1,0:T(8,128)S(1)}, u32[]{:S(2)}, u32[]{:S(2)}) collective-permute-start(f32[15,48,128]{2,1,0:T(8,128)S(1)} %get-tuple-element.13), channel_id=1, source_target_pairs={{1,0},{2,1},{3,2},{4,3},{5,4},{6,5},{7,6},{9,8},{10,9},{11,10},{12... | collective-permute-start | bytes 1105928 | tf_op jit(solution)/shard_map/ppermute | solution.py:664
  11.9 15.8 %all-to-all-start = ((f32[8,24,128]{2,1,0:T(8,128)}), f32[8,24,128]{2,1,0:T(8,128)S(1)}, u32[]{:S(2)}, u32[]{:S(2)}) async-start(f32[8,24,128]{2,1,0:T(8,128)} %get-tuple-element.9), calls=%async_computation | async-start | bytes 196608 | tf_op jit(solution)/shard_map/all_to_all | solution.py:662
  29.2 20.4 %all-to-all-start.1 = ((f32[16,64,128]{2,1,0:T(8,128)}), f32[16,64,128]{2,1,0:T(8,128)S(1)}, u32[]{:S(2)}, u32[]{:S(2)}) async-start(f32[16,64,128]{2,1,0:T(8,128)} %relay.1), calls=%async_computation.1 | async-start | bytes 1048576 | tf_op jit(solution)/shard_map/all_to_all | solution.py:680

commit v2 on v1

--- a/solution.py
+++ b/solution.py
@@ -260,17 +260,24 @@
     ]
 
 
-def prepare_kernel(den, mom, ene, ent, tra, flags, left, right, flag, pay, xlo, xhi, ylo, yhi, u, fl, flv, leftv, rightv, flagv, sems):
+def prepare_kernel(den, mom, ene, ent, tra, flags, left, right, flag, pay_h, u, xlo, xhi, ylo_h, yhi_h, pay, ylo, yhi, fl, flv, leftv, rightv, flagv, sems):
     small = load_all(zip((flags, left, right, flag), (flv, leftv, rightv, flagv)), sems.at[7:11])
     loads = load_all(fields_into((den, mom, ene, ent, tra), u), sems.at[0:5])
+    for copy in loads:
+        copy.wait()
+    slabs = load_all([(u.at[:, 0:48], xlo), (u.at[:, 208:256], xhi)], sems.at[5:7])
+    for f in range(NF):
+        for k in range(3):
+            for s in range(2):
+                ylo[f, k * 16 + s * 8 : k * 16 + s * 8 + 8] = u[f, pl.ds(s * 128 + k, 8, stride=16)]
+                yhi[f, k * 16 + s * 8 : k * 16 + s * 8 + 8] = u[f, pl.ds(s * 128 + 13 + k, 8, stride=16)]
+    slabs += load_all([(ylo, ylo_h), (yhi, yhi_h)], sems.at[11:13])
     for copy in small:
         copy.wait()
     fl[...] = jnp.zeros((8, 128), F32)
     fl[0:2, 0:16] = flv[0].astype(F32)
     fl[2:4, 0:16] = flv[1].astype(F32)
     tile = mxu(fl[...].astype(BF16), flagv[...])
-    for k in (0, 1, 3):
-        loads[k].wait()
     rho = u[0]
     sums = exact(leftv[...], exact(rho, rightv[...]))
     inverse = 1.0 / rho
@@ -294,23 +301,15 @@
         tiles[c] = jnp.where(here & (row < 4), low, tiles[c])
         tiles[c] = jnp.where(here & (row == 4) & (lane < to + 8), top, tiles[c])
     tiles[2] = jnp.where((row == 4) & (lane >= 64), fastest, tiles[2])
-    for y in range(GY):
-        for c in range(3):
-            pay[y, c * 8 : c * 8 + 8] = tiles[c]
-    for k in (2, 4):
-        loads[k].wait()
-    slabs = load_all([(u.at[:, 0:48], xlo), (u.at[:, 208:256], xhi)], sems.at[5:7])
-    for f in range(NF):
-        for k in range(3):
-            for s in range(2):
-                ylo[f, k * 16 + s * 8 : k * 16 + s * 8 + 8] = u[f, pl.ds(s * 128 + k, 8, stride=16)]
-                yhi[f, k * 16 + s * 8 : k * 16 + s * 8 + 8] = u[f, pl.ds(s * 128 + 13 + k, 8, stride=16)]
+    for c in range(3):
+        pay[c * 8 : c * 8 + 8] = tiles[c]
+    slabs += load_all([(pay, pay_h.at[y]) for y in range(GY)], sems.at[13 : 13 + GY])
     for copy in slabs:
         copy.wait()
 
 
 def relay_kernel(pos, column, *rest):
-    out = rest[-1]
+    out_h, out, sems = rest[-3:]
     y = pos[1]
     tiles = [column[pl.ds(c * 8 + 4, 8, stride=24)] for c in range(3)]
     near = []
@@ -320,12 +319,13 @@
         for c in range(3):
             tile = column[pl.ds(pl.multiple_of(here * 24 + c * 8, 8), 8)]
             near.append(jnp.where(inside, tile, 0.0))
-    for x in range(GX):
-        for c in range(3):
-            out[x, c * 8 : c * 8 + 8] = tiles[c]
-        for n, tile in enumerate(near):
-            out[x, 24 + n * 4 : 28 + n * 4] = tile[0:4]
-        out[x, 60:64] = jnp.zeros((4, 128), F32)
+    for c in range(3):
+        out[c * 8 : c * 8 + 8] = tiles[c]
+    for n, tile in enumerate(near):
+        out[24 + n * 4 : 28 + n * 4] = tile[0:4]
+    out[60:64] = jnp.zeros((4, 128), F32)
+    for copy in load_all([(out, out_h.at[x]) for x in range(GX)], sems):
+        copy.wait()
 
 
 def states(ol, il, l, r, ir, orr):
@@ -358,115 +358,142 @@
         store(f, flux)
 
 
-def sweep(buf, target, d):
-    def step(i, carry):
+def flux_z_kernel(u, out_h, uz, fz, out, sems):
+    for f in range(NF):
+        for half in range(2):
+            cells = u[f, half * 128 : half * 128 + 128].T
+            uz[2 * f + half, 8:136] = cells
+            uz[2 * f + half, 0:8] = jnp.broadcast_to(cells[0:1], (8, 128))
+            uz[2 * f + half, 136:144] = jnp.broadcast_to(cells[127:128], (8, 128))
+
+    def faces_z(i, carry):
+        for half in range(2):
+
+            def load(f):
+                return states(*[uz[2 * f + half, pl.ds(i * 8 + 5 + k, 8)] for k in range(6)])
+
+            def store(f, flux):
+                fz[2 * f + half, pl.ds(pl.multiple_of(i * 8, 8), 8)] = flux
+
+            fluxes(load, 2, store)
+        return carry
+
+    lax.fori_loop(0, 16, faces_z, 0)
+    for half in range(2):
+
+        def load_top(f, half=half):
+            rows = [uz[2 * f + half, 133 + k : 141 + k] for k in range(4)]
+            return states(*rows, rows[3], rows[3])
+
+        def store_top(f, flux, half=half):
+            fz[2 * f + half, 128:136] = flux
+
+        fluxes(load_top, 2, store_top)
+
+    stores = []
+    for part in range(5):
+        for f in range(part * 3, part * 3 + 3):
+            for half in range(2):
+                out[f, half * 128 : half * 128 + 128] = (fz[2 * f + half, 0:128] - fz[2 * f + half, 1:129]).T
+        some = slice(part * 3, part * 3 + 3)
+        stores += load_all([(out.at[some], out_h.at[some])], sems.at[part : part + 1])
+    for copy in stores:
+        copy.wait()
+
+
+def flux_xy_kernel(pos, den, mom, ene, ent, tra, along_z_h, xl, xr, yl_h, yr_h, *args):
+    count = len(TREE_CONSTANTS)
+    out_h = args[count]
+    tables = args[count + 1 : 2 * count + 1]
+    ux, fx, uy, fy, yl, yr, along_z, out, sems = args[2 * count + 1 :]
+    loads = load_all(
+        fields_into((den, mom, ene, ent, tra), ux, rows=slice(48, 304))
+        + [(xl, ux.at[:, 0:48]), (xr, ux.at[:, 304:352]), (yl_h, yl), (yr_h, yr), (along_z_h, along_z)],
+        sems.at[0:10],
+    )
+    late = load_all(list(zip(args[:count], tables)), sems.at[10 : 10 + count])
+    for copy in loads[:7]:
+        copy.wait()
+
+    def repeat(source, target):
+        for f in range(NF):
+            cells = ux[f, source : source + 16]
+            for k in range(3):
+                ux[f, target + k * 16 : target + k * 16 + 16] = cells
+
+    pl.when(pos[0] == 0)(lambda: repeat(48, 0))
+    pl.when(pos[0] == GX - 1)(lambda: repeat(288, 304))
+
+    def faces_x(i, carry):
         for s in range(2):
 
             def load(f):
-                return states(*[buf[f, pl.ds(pl.multiple_of((i + k) * 16 + s * 8, 8), 8)] for k in range(6)])
+                return states(*[ux[f, pl.ds(pl.multiple_of((i + k) * 16 + s * 8, 8), 8)] for k in range(6)])
 
             def store(f, flux):
-                target[f, pl.ds(pl.multiple_of(i * 16 + s * 8, 8), 8)] = flux
-
-            fluxes(load, d, store)
+                fx[f, pl.ds(pl.multiple_of(i * 16 + s * 8, 8), 8)] = flux
+
+            fluxes(load, 0, store)
         return carry
 
-    lax.fori_loop(0, 17, step, 0)
-
-
-def flux_z_kernel(den, mom, ene, ent, tra, out_h, u, uz, fz, turn, out, sems):
-    row = row_ids((8, 128))
-    loads = load_all(fields_into((den, mom, ene, ent, tra), u), sems.at[0:5])
-
-    def into(f, carry):
-        for half in range(2):
-            turn[half] = u[f, half * 128 : half * 128 + 128].T
-            cells = [turn[half, pl.ds(m, 8, stride=16)] for m in range(16)]
-            first = jnp.broadcast_to(cells[0][0:1], (8, 128))
-            last = jnp.broadcast_to(cells[15][7:8], (8, 128))
-            below = [jnp.where(row == 0, first, pltpu.roll(cells[m], 1, 0)) for m in (13, 14, 15)]
-            above = [jnp.where(row == 7, last, pltpu.roll(cells[m], 7, 0)) for m in (0, 1, 2)]
-            for m, value in enumerate(below + cells + above):
-                uz[f, m * 16 + half * 8 : m * 16 + half * 8 + 8] = value
+    lax.fori_loop(0, 17, faces_x, 0)
+
+    def spread(x, carry):
+        for f in range(NF):
+            uy[f, pl.ds(pl.multiple_of(x * 32 + 8, 8), 16)] = ux[f, pl.ds(pl.multiple_of(48 + x * 16, 8), 16)]
         return carry
 
-    for copy, (start, n) in zip(loads, PLACES):
-        copy.wait()
-        lax.fori_loop(start, start + n, into, 0)
-    sweep(uz, fz, 2)
-
-    def back(f, carry):
-        for half in range(2):
-            at = half * 8
-            for m in range(16):
-                low = fz[f, m * 16 + at : m * 16 + at + 8]
-                high = fz[f, m * 16 + 16 + at : m * 16 + 24 + at]
-                turn[half, pl.ds(m, 8, stride=16)] = low - high
-            out[f, half * 128 : half * 128 + 128] = turn[half].T
+    lax.fori_loop(0, 16, spread, 0)
+    for copy in loads[7:9]:
+        copy.wait()
+    first, last = pos[1] == 0, pos[1] == GY - 1
+    for f in range(NF):
+        for s in range(2):
+            low, high = ux[f, pl.ds(48 + s * 128, 8, stride=16)], ux[f, pl.ds(63 + s * 128, 8, stride=16)]
+            for k in range(3):
+                at = slice(k * 16 + s * 8, k * 16 + s * 8 + 8)
+                uy[f, pl.ds(s * 256 + 5 + k, 8, stride=32)] = jnp.where(first, low, yl[f, at])
+                uy[f, pl.ds(s * 256 + 24 + k, 8, stride=32)] = jnp.where(last, high, yr[f, at])
+
+    def faces_y(x, carry):
+        for s in range(2):
+
+            def load(f):
+                return states(*[uy[f, pl.ds(x * 32 + s * 8 + 5 + k, 8)] for k in range(6)])
+
+            def store(f, flux):
+                fy[f, pl.ds(pl.multiple_of(x * 24 + s * 8, 8), 8)] = flux
+
+            fluxes(load, 1, store)
         return carry
 
-    stores = []
-    for part in range(3):
-        lax.fori_loop(part * 5, part * 5 + 5, back, 0)
-        some = slice(part * 5, part * 5 + 5)
-        stores.append(pltpu.make_async_copy(out.at[some], out_h.at[some], sems.at[5 + part]))
-        stores[-1].start()
-    for copy in stores:
-        copy.wait()
-
-
-def flux_xy_kernel(pos, den, mom, ene, ent, tra, along_z_h, xl, xr, yl, yr, out_h, ux, uy, fx, fy, along_z, out, sems):
-    interior = load_all(fields_into((den, mom, ene, ent, tra), ux, rows=slice(48, 304)), sems.at[0:5])
-    loads = load_all(
-        [
-            (yl, uy.at[:, 0:48]),
-            (yr, uy.at[:, 304:352]),
-            (xl, ux.at[:, 0:48]),
-            (xr, ux.at[:, 304:352]),
-            (along_z_h, along_z),
-        ],
-        sems.at[5:10],
-    )
-    for copy, (start, n) in zip(interior, PLACES):
-        copy.wait()
-        for f in range(start, start + n):
-            for y in range(16):
-                for s in range(2):
-                    at = (3 + y) * 16 + s * 8
-                    uy[f, at : at + 8] = ux[f, pl.ds(48 + s * 128 + y, 8, stride=16)]
-    for copy in loads[:-1]:
-        copy.wait()
-
-    def repeat(buf, source, target):
-        for f in range(NF):
-            cells = buf[f, source : source + 16]
-            for k in range(3):
-                buf[f, target + k * 16 : target + k * 16 + 16] = cells
-
-    pl.when(pos[0] == 0)(lambda: repeat(ux, 48, 0))
-    pl.when(pos[0] == GX - 1)(lambda: repeat(ux, 288, 304))
-    pl.when(pos[1] == 0)(lambda: repeat(uy, 48, 0))
-    pl.when(pos[1] == GY - 1)(lambda: repeat(uy, 288, 304))
-    sweep(uy, fy, 1)
-    sweep(ux, fx, 0)
-    loads[-1].wait()
+    lax.fori_loop(0, 16, faces_y, 0)
+    for s in range(2):
+
+        def load_end(f, s=s):
+            return states(*[uy[f, pl.ds(s * 256 + 21 + k, 8, stride=32)] for k in range(6)])
+
+        def store_end(f, flux, s=s):
+            fy[f, pl.ds(s * 192 + 16, 8, stride=24)] = flux
+
+        fluxes(load_end, 1, store_end)
+    loads[9].wait()
 
     def gather(x, carry):
         for f in range(NF):
             for s in range(2):
                 at = pl.multiple_of(x * 16 + s * 8, 8)
-                change = along_z[f, pl.ds(at, 8)] + (fx[f, pl.ds(at, 8)] - fx[f, pl.ds(at + 16, 8)])
-                low, high = fy[f, pl.ds(s * 128 + x, 8, stride=16)], fy[f, pl.ds(s * 128 + 16 + x, 8, stride=16)]
-                out[f, pl.ds(at, 8)] = change + (low - high)
+                rows = pl.ds(at, 8)
+                change = along_z[f, rows] + (fx[f, rows] - fx[f, pl.ds(at + 16, 8)])
+                y = x * 24 + s * 8
+                out[f, rows] = change + (fy[f, pl.ds(pl.multiple_of(y, 8), 8)] - fy[f, pl.ds(y + 1, 8)])
         return carry
 
-    stores = []
     for part in range(4):
         lax.fori_loop(part * 4, part * 4 + 4, gather, 0)
         rows = slice(part * 64, part * 64 + 64)
-        stores.append(pltpu.make_async_copy(out.at[:, rows], out_h.at[:, rows], sems.at[10 + part]))
-        stores[-1].start()
-    for copy in stores:
+        late += load_all([(out.at[:, rows], out_h.at[:, rows])], sems.at[10 + count + part : 11 + count + part])
+    for copy in late:
         copy.wait()
 
 
@@ -476,17 +503,11 @@
 )
 
 
-def tree_kernel(
-    pos, far_h, den, mom, ene, ent, tra, change_h, *args,
-):
+def tree_kernel(pos, far, den, mom, ene, ent, tra, change_h, *args):
     count = len(TREE_CONSTANTS)
-    section, accel, rhs, field, result, force, far, change, u, sems = args[count : count + 10]
-    loaded = args[count + 10 :]
-    late = fields_into((den, mom, ene, ent, tra), u) + [(change_h, change)]
-    loads = load_all([(far_h, far)] + list(zip(args[:count], loaded)) + late, sems)
-    for copy in loads[: 1 + count]:
-        copy.wait()
-    (w_high, w_low, sel_zero, lane_odd, up, alpha_odd, agg, mask, info, expand, gamma_odd, down, spread, poly) = loaded
+    w_high, w_low, sel_zero, lane_odd, up, alpha_odd, agg, mask, info, expand, gamma_odd, down, spread, poly = args[:count]
+    section, accel, rhs, field, result, force, u, change, sems = args[count:]
+    late = load_all(fields_into((den, mom, ene, ent, tra), u) + [(change_h, change)], sems.at[0:6])
     px, py = pos[0], pos[1]
     blocks = []
     for dx in range(3):
@@ -582,7 +603,7 @@
     )
     field[...] = exact(poly[...], terms)
     step = jnp.full((8, 128), COURANT / SUB, F32) / fastest
-    for copy in loads[1 + count :]:
+    for copy in late:
         copy.wait()
     stores = []
     for half in range(2):
@@ -608,7 +629,7 @@
         lax.fori_loop(0, 8, finish, 0)
         rows = slice(half * 128, half * 128 + 128)
         for k, (source, target) in enumerate(((result, section), (force, accel))):
-            stores.append(pltpu.make_async_copy(source.at[:, rows], target.at[:, rows], sems.at[2 * half + k]))
+            stores.append(pltpu.make_async_copy(source.at[:, rows], target.at[:, rows], sems.at[6 + 2 * half + k]))
             stores[-1].start()
     for copy in stores:
         copy.wait()
@@ -620,13 +641,15 @@
 SMEM = pl.BlockSpec(memory_space=pltpu.SMEM)
 
 
-def call(kernel, name, ins, outs, scratch, cost):
+def call(kernel, name, ins, outs, scratch, cost, aliases=None):
+    outs = [(o[0], o[1], o[2] if len(o) > 2 else F32) for o in outs]
     return pl.pallas_call(
         kernel,
-        out_shape=[pltpu.HBM(s, F32) if spec is HBM else jax.ShapeDtypeStruct(s, F32) for s, spec in outs],
+        out_shape=[pltpu.HBM(s, t) if spec is HBM else jax.ShapeDtypeStruct(s, t) for s, spec, t in outs],
         in_specs=[spec for _, spec in ins],
-        out_specs=[spec for _, spec in outs],
+        out_specs=[spec for _, spec, _ in outs],
         scratch_shapes=scratch,
+        input_output_aliases=aliases or {},
         cost_estimate=pl.CostEstimate(flops=cost[0], bytes_accessed=cost[1], transcendentals=cost[2]),
         name=name,
         compiler_params=pltpu.CompilerParams(vmem_limit_bytes=32 << 20),
@@ -647,14 +670,16 @@
     ix, iy = lax.axis_index("mx"), lax.axis_index("my")
     pos = (jnp.stack([ix, iy]).astype(jnp.int32), SMEM)
     first = [con[n] for n in ("left", "right", "flag")]
-    whole = (NF, ROWS, 128)
-    slab = ((NF, 48, 128), HBM)
-    pay, xlo, xhi, ylo, yhi = call(
+    whole, slab = (NF, ROWS, 128), (NF, 48, 128)
+    block, halo = pltpu.VMEM(whole, F32), pltpu.VMEM(slab, F32)
+    pay, u, xlo, xhi, ylo, yhi = call(
         prepare_kernel,
         "prepare",
         fields + [(leaf_flags, HBM)] + [(x, HBM) for x in first],
-        [((GY, 24, 128), VMEM), slab, slab, ((NF, 48, 128), VMEM), ((NF, 48, 128), VMEM)],
-        [pltpu.VMEM(whole, F32), pltpu.VMEM((8, 128), F32), scratch_like(leaf_flags)] + [scratch_like(x) for x in first] + [pltpu.SemaphoreType.DMA((11,))],
+        [((GY, 24, 128), HBM), (whole, VMEM)] + [(slab, HBM)] * 4,
+        [pltpu.VMEM((24, 128), F32), halo, halo, pltpu.VMEM((8, 128), F32), scratch_like(leaf_flags)]
+        + [scratch_like(x) for x in first]
+        + [pltpu.SemaphoreType.DMA((13 + GY,))],
         (10**7, 4 * 10**6, 10**5),
     )
     up_x, down_x = [(i, i + 1) for i in range(GX - 1)], [(i + 1, i) for i in range(GX - 1)]
@@ -664,45 +689,57 @@
     yr = lax.ppermute(ylo, "my", down_y)
     xl = lax.ppermute(xhi, "mx", up_x)
     xr = lax.ppermute(xlo, "mx", down_x)
-    block = pltpu.VMEM(whole, F32)
-    extended, faces = pltpu.VMEM((NF, 352, 128), F32), pltpu.VMEM((NF, 272, 128), F32)
     (along_z,) = call(
         flux_z_kernel,
         "flux_z",
-        fields,
+        [(u, VMEM)],
         [(whole, HBM)],
-        [block, extended, faces, pltpu.VMEM((2, 128, 128), F32), block, pltpu.SemaphoreType.DMA((8,))],
+        [pltpu.VMEM((2 * NF, 144, 128), F32), pltpu.VMEM((2 * NF, 136, 128), F32), block, pltpu.SemaphoreType.DMA((5,))],
         (2 * 10**7, 4 * 10**6, 3 * 10**5),
     )
+    halos = [(x, ANY) for x in (xl, xr, yl, yr)]
     (chunks,) = call(
-        relay_kernel, "relay", [pos, (column.reshape(GY * 24, 128), VMEM), (along_z, HBM)] + [(x, ANY) for x in (xl, xr, yl, yr)], [((GX, 64, 128), VMEM)], [], (10**4, 10**6, 0)
+        relay_kernel,
+        "relay",
+        [pos, (column.reshape(GY * 24, 128), VMEM), (along_z, HBM)] + halos,
+        [((GX, 64, 128), HBM)],
+        [pltpu.VMEM((64, 128), F32), pltpu.SemaphoreType.DMA((GX,))],
+        (10**4, 10**6, 0),
     )
     far = lax.all_to_all(chunks, "mx", 0, 0)
-    (tend,) = call(
+    second = [con[n] for n in TREE_CONSTANTS]
+    tend, *tables = call(
         flux_xy_kernel,
         "flux_xy",
-        [pos] + fields + [(along_z, HBM)] + [(x, ANY) for x in (xl, xr, yl, yr)],
-        [(whole, HBM)],
-        [extended, extended, faces, faces, block, block, pltpu.SemaphoreType.DMA((14,))],
+        [pos] + fields + [(along_z, HBM)] + halos + [(x, HBM) for x in second],
+        [(whole, HBM)] + [(x.shape, VMEM, x.dtype) for x in second],
+        [
+            pltpu.VMEM((NF, 352, 128), F32),
+            pltpu.VMEM((NF, 272, 128), F32),
+            pltpu.VMEM((NF, 512, 128), F32),
+            pltpu.VMEM((NF, 384, 128), F32),
+            halo,
+            halo,
+            block,
+            block,
+            pltpu.SemaphoreType.DMA((14 + len(second),)),
+        ],
         (4 * 10**7, 6 * 10**6, 6 * 10**5),
     )
-    second = [con[n] for n in TREE_CONSTANTS]
     section, accel = call(
         tree_kernel,
         "tree",
-        [pos, (far, ANY)] + fields + [(tend, HBM)] + [(x, HBM) for x in second],
-        [(whole, ANY), ((3, ROWS, 128), ANY)],
+        [pos, (far, VMEM)] + fields + [(tend, HBM)] + [(x, VMEM) for x in tables],
+        [(whole, HBM), ((3, ROWS, 128), HBM)],
         [
             pltpu.VMEM((NA * WIN, 128), F32),
             pltpu.VMEM((192, 512), F32),
-            pltpu.VMEM(whole, F32),
+            block,
             pltpu.VMEM((3, ROWS, 128), F32),
-            pltpu.VMEM((GX, 64, 128), F32),
             block,
             block,
-            pltpu.SemaphoreType.DMA((7 + len(second),)),
-        ]
-        + [scratch_like(x) for x in second],
+            pltpu.SemaphoreType.DMA((10,)),
+        ],
         (10**8, 8 * 10**6, 0),
     )
     return section.reshape(NF, 16, 16, 128), accel.reshape(3, 16, 16, 128)

time: 57 us -> 54.8 us (0.961)
  Pallas kernels: 29.1 us -> 25.1 us
  waiting for transfers between devices: 2.84 us -> 4.66 us
    pallas_call x5, Pallas kernels: 29.1 us -> 25.1 us  [call(): pl.pallas_call(kernel, out_shape=[pltpu.HBM(s, t) if spec is HBM else jax...]
    all_to_all x1, waiting for transfers between devices: 0.01 us -> 1.85 us  [shards(): column = lax.all_to_all(pay, 'my', 0, 0)]
  transfers between devices with their start and end apart: 6 -> 6, of which waited for: 1 -> 2; matrix products, arithmetic and copies ran while one was open for 0% -> 0% of each run, Pallas kernels for 30% -> 23%
where the time goes in v2:
time: 54.8 us; the launch traced here: 54.4 us
  Pallas kernels  25.1 us (46%)
  starting transfers between devices  23.9 us (44%)
  waiting for transfers between devices  4.66 us (9%)
  between operations  0.72 us (1%)
    pallas_call x5, Pallas kernels, call(): pl.pallas_call(kernel, out_shape=[pltpu.HBM(s, t) if spec is HBM else jax...  25.1 us
    all_to_all x1, starting transfers between devices, shards(): far = lax.all_to_all(chunks, 'mx', 0, 0)  8.18 us
    all_to_all x1, starting transfers between devices, shards(): column = lax.all_to_all(pay, 'my', 0, 0)  8.11 us
    ppermute x1, starting transfers between devices, shards(): xl = lax.ppermute(xhi, 'mx', up_x)  3.5 us
    all_to_all x1, waiting for transfers between devices, shards(): far = lax.all_to_all(chunks, 'mx', 0, 0)  2.8 us
    all_to_all x1, waiting for transfers between devices, shards(): column = lax.all_to_all(pay, 'my', 0, 0)  1.85 us
    ppermute x1, starting transfers between devices, shards(): yl = lax.ppermute(yhi, 'my', up_y)  1.48 us
    ppermute x1, starting transfers between devices, shards(): xr = lax.ppermute(xlo, 'mx', down_x)  1.29 us
  transfers between devices with their start and end apart: 6, of which 2 were waited for; matrix products, arithmetic and copies ran while one was open for 0% of the time, Pallas kernels for 23%

profile of v2, /device:TPU:0, one launch (start us, length us, event | category | flops | bytes accessed | tf_op | source)
XLA Modules:
  0.0 54.4 jit_solution(17596232383985492874)
XLA Ops:
  0.6 3.6 %prepare.1 = (f32[8,24,128]{2,1,0:T(8,128)}, f32[15,256,128]{2,1,0:T(8,128)S(1)}, f32[15,48,128]{2,1,0:T(8,128)}, f32[15,48,128]{2,1,0:T(8,128)}, f32[15,48,128]{2,1,0:T(8,128)}, /*index=5*/f32[15,48,128]{2,1,0:T(8,128)}) custom-call(f32[1,256,128]{2,1,0:T(8,128)} %bitcast.17, f32[3,256,128]{2,1,0:T(8,128)} %bitcast.14, f32[1,256,128]{2,1,0:T(8,128)} %bitcast.20, ...), custom_call_target="tpu_custom_call" | custom-call | flops 10000000 | bytes 4000000 | tf_op jit(solution)/shard_map/prepare/pallas_call | solution.py:646
  4.2 3.5 %collective-permute-start = (f32[15,48,128]{2,1,0:T(8,128)}, f32[15,48,128]{2,1,0:T(8,128)S(1)}, u32[]{:S(2)}, u32[]{:S(2)}) collective-permute-start(f32[15,48,128]{2,1,0:T(8,128)} %get-tuple-element.27), channel_id=1, source_target_pairs={{0,8},{8,16},{16,24},{24,32},{32,40},{40,48},{48,56},{56,64},{64,7... | collective-permute-start | bytes 1105928 | tf_op jit(solution)/shard_map/ppermute | solution.py:690
  7.7 1.3 %collective-permute-start.1 = (f32[15,48,128]{2,1,0:T(8,128)}, f32[15,48,128]{2,1,0:T(8,128)S(1)}, u32[]{:S(2)}, u32[]{:S(2)}) collective-permute-start(f32[15,48,128]{2,1,0:T(8,128)} %get-tuple-element.28), channel_id=1, source_target_pairs={{8,0},{16,8},{24,16},{32,24},{40,32},{48,40},{56,48},{64,56},{72,6... | collective-permute-start | bytes 1105928 | tf_op jit(solution)/shard_map/ppermute | solution.py:691
  9.0 1.5 %collective-permute-start.2 = (f32[15,48,128]{2,1,0:T(8,128)}, f32[15,48,128]{2,1,0:T(8,128)S(1)}, u32[]{:S(2)}, u32[]{:S(2)}) collective-permute-start(f32[15,48,128]{2,1,0:T(8,128)} %get-tuple-element.29), channel_id=1, source_target_pairs={{0,1},{1,2},{2,3},{3,4},{4,5},{5,6},{6,7},{8,9},{9,10},{10,11},{11... | collective-permute-start | bytes 1105928 | tf_op jit(solution)/shard_map/ppermute | solution.py:688
  10.5 1.3 %collective-permute-start.3 = (f32[15,48,128]{2,1,0:T(8,128)}, f32[15,48,128]{2,1,0:T(8,128)S(1)}, u32[]{:S(2)}, u32[]{:S(2)}) collective-permute-start(f32[15,48,128]{2,1,0:T(8,128)} %get-tuple-element.30), channel_id=1, source_target_pairs={{1,0},{2,1},{3,2},{4,3},{5,4},{6,5},{7,6},{9,8},{10,9},{11,10},{12... | collective-permute-start | bytes 1105928 | tf_op jit(solution)/shard_map/ppermute | solution.py:689
  11.8 8.1 %all-to-all-start = ((f32[8,24,128]{2,1,0:T(8,128)}), f32[8,24,128]{2,1,0:T(8,128)S(1)}, u32[]{:S(2)}, u32[]{:S(2)}) async-start(f32[8,24,128]{2,1,0:T(8,128)} %get-tuple-element.25), calls=%async_computation | async-start | bytes 196608 | tf_op jit(solution)/shard_map/all_to_all | solution.py:687
  19.9 3.9 %flux_z.1.rest_0_.along_z_h = f32[15,256,128]{2,1,0:T(8,128)} custom-call(f32[15,256,128]{2,1,0:T(8,128)S(1)} %get-tuple-element.26.u), custom_call_target="tpu_custom_call" | custom-call | flops 20000000 | bytes 4000000 | tf_op jit(solution)/shard_map/flux_z/pallas_call | solution.py:646
  23.8 0.1 pad_add_fusion.pos
  23.9 1.8 %all-to-all-done = f32[8,24,128]{2,1,0:T(8,128)S(1)} async-done(((f32[8,24,128]{2,1,0:T(8,128)}), f32[8,24,128]{2,1,0:T(8,128)S(1)}, u32[]{:S(2)}, u32[]{:S(2)}) %all-to-all-start) | async-done | bytes 98336 | tf_op jit(solution)/shard_map/all_to_all | solution.py:687
  25.7 0.0 collective-permute-done.rest_1_.xl
  25.7 0.0 collective-permute-done.1.rest_2_.xr
  25.7 0.0 collective-permute-done.2.rest_3_.yl_h
  25.7 0.0 collective-permute-done.3.rest_4_.yr_h
  25.7 1.5 %relay.1 = f32[16,64,128]{2,1,0:T(8,128)} custom-call(s32[2]{0:T(128)S(1)} %pad_add_fusion.pos, f32[192,128]{1,0:T(8,128)S(1)} %bitcast.10, f32[15,256,128]{2,1,0:T(8,128)} %flux_z.1.rest_0_.along_z_h, f32[15,48,128]{2,1,0:T(8,128)S(1)} %collective-permute-done.rest_1_.xl, f32[15,48,128]{2,1,0:T(8,128)S(1)} %collective-permute-done.1.rest_2_.xr, ...), custom_call_target="tpu_custom_call" | custom-call | flops 10000 | bytes 1000000 | tf_op jit(solution)/shard_map/relay/pallas_call | solution.py:646
  27.2 8.2 %all-to-all-start.1 = ((f32[16,64,128]{2,1,0:T(8,128)}), f32[16,64,128]{2,1,0:T(8,128)S(1)}, u32[]{:S(2)}, u32[]{:S(2)}) async-start(f32[16,64,128]{2,1,0:T(8,128)} %relay.1), calls=%async_computation.1 | async-start | bytes 1048576 | tf_op jit(solution)/shard_map/all_to_all | solution.py:709
  35.4 8.6 %flux_xy.1 = (f32[15,256,128]{2,1,0:T(8,128)}, bf16[168,800]{1,0:T(8,128)(2,1)S(1)}, bf16[168,800]{1,0:T(8,128)(2,1)S(1)}, bf16[160,40]{1,0:T(8,128)(2,1)S(1)}, ...) custom-call(s32[2]{0:T(128)S(1)} %pad_add_fusion.pos, ...), custom_call_target="tpu_custom_call" | custom-call | flops 40000000 | bytes 6000000 | tf_op jit(solution)/shard_map/flux_xy/pallas_call | solution.py:646
  44.0 2.8 %all-to-all-done.1.far = f32[16,64,128]{2,1,0:T(8,128)S(1)} async-done(((f32[16,64,128]{2,1,0:T(8,128)}), f32[16,64,128]{2,1,0:T(8,128)S(1)}, u32[]{:S(2)}, u32[]{:S(2)}) %all-to-all-start.1) | async-done | bytes 524320 | tf_op jit(solution)/shard_map/all_to_all | solution.py:709
  46.8 7.5 %tree.1 = (f32[15,256,128]{2,1,0:T(8,128)}, f32[3,256,128]{2,1,0:T(8,128)}) custom-call(s32[2]{0:T(128)S(1)} %pad_add_fusion.pos, f32[16,64,128]{2,1,0:T(8,128)S(1)} %all-to-all-done.1.far, f32[1,256,128]{2,1,0:T(8,128)} %bitcast.19, f32[3,256,128]{2,1,0:T(8,128)} %bitcast.16, f32[1,256,128]{2,1,0:T(8,128)} %bitcast.22, f32[1,256,128]{2,1,0:T(8,128)} %bitcast.25, ...), custom_call_target="tpu_custom_call" | custom-call | flops 100000000 | bytes 8000000 | tf_op jit(solution)/shard_map/tree/pallas_call | solution.py:646
Async XLA Ops:
  4.2 21.5 %collective-permute-start = (f32[15,48,128]{2,1,0:T(8,128)}, f32[15,48,128]{2,1,0:T(8,128)S(1)}, u32[]{:S(2)}, u32[]{:S(2)}) collective-permute-start(f32[15,48,128]{2,1,0:T(8,128)} %get-tuple-element.27), channel_id=1, source_target_pairs={{0,8},{8,16},{16,24},{24,32},{32,40},{40,48},{48,56},{56,64},{64,7... | collective-permute-start | bytes 1105928 | tf_op jit(solution)/shard_map/ppermute | solution.py:690
  7.7 18.0 %collective-permute-start.1 = (f32[15,48,128]{2,1,0:T(8,128)}, f32[15,48,128]{2,1,0:T(8,128)S(1)}, u32[]{:S(2)}, u32[]{:S(2)}) collective-permute-start(f32[15,48,128]{2,1,0:T(8,128)} %get-tuple-element.28), channel_id=1, source_target_pairs={{8,0},{16,8},{24,16},{32,24},{40,32},{48,40},{56,48},{64,56},{72,6... | collective-permute-start | bytes 1105928 | tf_op jit(solution)/shard_map/ppermute | solution.py:691
  9.0 16.7 %collective-permute-start.2 = (f32[15,48,128]{2,1,0:T(8,128)}, f32[15,48,128]{2,1,0:T(8,128)S(1)}, u32[]{:S(2)}, u32[]{:S(2)}) collective-permute-start(f32[15,48,128]{2,1,0:T(8,128)} %get-tuple-element.29), channel_id=1, source_target_pairs={{0,1},{1,2},{2,3},{3,4},{4,5},{5,6},{6,7},{8,9},{9,10},{10,11},{11... | collective-permute-start | bytes 1105928 | tf_op jit(solution)/shard_map/ppermute | solution.py:688
  10.5 15.2 %collective-permute-start.3 = (f32[15,48,128]{2,1,0:T(8,128)}, f32[15,48,128]{2,1,0:T(8,128)S(1)}, u32[]{:S(2)}, u32[]{:S(2)}) collective-permute-start(f32[15,48,128]{2,1,0:T(8,128)} %get-tuple-element.30), channel_id=1, source_target_pairs={{1,0},{2,1},{3,2},{4,3},{5,4},{6,5},{7,6},{9,8},{10,9},{11,10},{12... | collective-permute-start | bytes 1105928 | tf_op jit(solution)/shard_map/ppermute | solution.py:689
  11.8 13.9 %all-to-all-start = ((f32[8,24,128]{2,1,0:T(8,128)}), f32[8,24,128]{2,1,0:T(8,128)S(1)}, u32[]{:S(2)}, u32[]{:S(2)}) async-start(f32[8,24,128]{2,1,0:T(8,128)} %get-tuple-element.25), calls=%async_computation | async-start | bytes 196608 | tf_op jit(solution)/shard_map/all_to_all | solution.py:687
  27.2 19.6 %all-to-all-start.1 = ((f32[16,64,128]{2,1,0:T(8,128)}), f32[16,64,128]{2,1,0:T(8,128)S(1)}, u32[]{:S(2)}, u32[]{:S(2)}) async-start(f32[16,64,128]{2,1,0:T(8,128)} %relay.1), calls=%async_computation.1 | async-start | bytes 1048576 | tf_op jit(solution)/shard_map/all_to_all | solution.py:709

commit v3 on v2

--- a/solution.py
+++ b/solution.py
@@ -60,6 +60,12 @@
     return high, low
 
 
+def exact_np(x):
+    y = x.astype(ml_dtypes.bfloat16)
+    assert np.array_equal(x, y.astype(np.float64))
+    return y
+
+
 @functools.cache
 def constants():
     out = {}
@@ -73,7 +79,10 @@
                         if sum(eg) + sum(ea) <= 3:
                             e = tuple(eg[k] + ea[k] for k in range(3))
                             w[z, g, a, i * 6 + j] = (
-                                -GRAVITY * (-1.0) ** sum(ea) / factorial_of(ea) * inverse_derivative(e, r)
+                                -GRAVITY
+                                * (-1.0) ** sum(ea)
+                                / (factorial_of(ea) * factorial_of(eg))
+                                * inverse_derivative(e, r)
                             )
     out["w_high"], out["w_low"] = split_np(w.reshape(7 * NG, NA * WIN))
     sel = np.zeros((4, WIN, 40))
@@ -107,8 +116,7 @@
                             d = -0.5 if k < 2 or z % 2 == 0 else 0.5
                             v *= math.comb(et[k], es[k]) * d ** (et[k] - es[k])
                         up[s * 16 + base + z, t * 16 + to + z // 2] = v
-    assert np.array_equal(up, up.astype(ml_dtypes.bfloat16).astype(np.float64))
-    out["up"] = up.astype(ml_dtypes.bfloat16)
+    out["up"] = exact_np(up)
     odd = np.zeros((16, 384), np.float32)
     for a, e in enumerate(ALPHA):
         odd[0, a * 16 : a * 16 + 16] = e[0] % 2
@@ -117,7 +125,7 @@
     agg = np.zeros((32, 128))
     for x in range(GX):
         for y in range(GY):
-            agg[(x // 2) * 4 + y // 2, x * 8 + y] = 1.0
+            agg[(x // 2) * 4 + y // 2, (y % 2) * 64 + x * 4 + y // 2] = 1.0
     out["agg"] = agg.astype(ml_dtypes.bfloat16)
     mask = np.zeros((8, 128), np.float32)
     info = np.zeros((16, 128), np.float32)
@@ -156,9 +164,9 @@
                 expand[64 + 12 + z // 2, lane] = 1.0
     out["mask"] = mask
     out["info"] = info
-    out["expand"] = expand
+    out["expand"] = exact_np(expand)
     gamma_odd = np.zeros((3 * NG, 128), np.float32)
-    down = np.zeros((NG, NG), np.float32)
+    down = np.zeros((NG, NG))
     for g, eg in enumerate(ALPHA):
         for k in range(3):
             gamma_odd[k * NG + g] = eg[k] % 2
@@ -167,16 +175,16 @@
                 v = 2.0 ** -sum(eg)
                 for k in range(3):
                     n = eb[k] - eg[k]
-                    v *= (-0.25) ** n / math.factorial(n)
+                    v *= (-0.25) ** n * math.comb(eb[k], eg[k])
                 down[g, b] = v
     out["gamma_odd"] = gamma_odd
-    out["down"] = down
+    out["down"] = exact_np(down)
     h = (np.arange(SUB) + 0.5) / SUB - 0.5
     spread = np.zeros((16, 384))
     for k in range(3):
         for z in range(128):
             spread[z // 8, k * 128 + z] = h[z % 8] ** k
-    out["spread"] = spread.astype(np.float32)
+    out["spread"] = exact_np(spread)
     poly = np.zeros((3, 8, 8, 3, NG))
     for i in range(3):
         for g, e in enumerate(ALPHA):
@@ -184,9 +192,9 @@
                 low = list(e)
                 low[i] -= 1
                 poly[i, :, :, low[2], g] = (
-                    -e[i] / factorial_of(e) * h[:, None] ** low[0] * h[None, :] ** low[1]
+                    -e[i] * h[:, None] ** low[0] * h[None, :] ** low[1]
                 )
-    out["poly"] = poly.reshape(192, 72).astype(np.float32)
+    out["poly"] = exact_np(poly.reshape(192, 72))
     cells = np.arange(16)
     near = h[cells % 8]
     far = ((cells + 0.5) / 8 - 1.0) / 2
@@ -217,6 +225,11 @@
 def split(x):
     high = x.astype(BF16)
     return high, (x - high.astype(F32)).astype(BF16)
+
+
+def split_rows(x):
+    high = x.astype(BF16).astype(F32)
+    return jnp.concatenate([high, x - high], 0).astype(BF16)
 
 
 def mxu(a, b):
@@ -300,7 +313,7 @@
         here = (lane >= to) & (lane < to + 16)
         tiles[c] = jnp.where(here & (row < 4), low, tiles[c])
         tiles[c] = jnp.where(here & (row == 4) & (lane < to + 8), top, tiles[c])
-    tiles[2] = jnp.where((row == 4) & (lane >= 64), fastest, tiles[2])
+    tiles[2] = jnp.where((row == 4) & (lane >= 64) & (lane < 72), fastest, tiles[2])
     for c in range(3):
         pay[c * 8 : c * 8 + 8] = tiles[c]
     slabs += load_all([(pay, pay_h.at[y]) for y in range(GY)], sems.at[13 : 13 + GY])
@@ -311,7 +324,8 @@
 def relay_kernel(pos, column, *rest):
     out_h, out, sems = rest[-3:]
     y = pos[1]
-    tiles = [column[pl.ds(c * 8 + 4, 8, stride=24)] for c in range(3)]
+    even = [column[pl.ds(c * 8 + 4, 4, stride=48)] for c in range(3)]
+    odd = [column[pl.ds(c * 8 + 28, 4, stride=48)] for c in range(3)]
     near = []
     for dy in range(3):
         here = jnp.clip(y + dy - 1, 0, GY - 1)
@@ -320,10 +334,9 @@
             tile = column[pl.ds(pl.multiple_of(here * 24 + c * 8, 8), 8)]
             near.append(jnp.where(inside, tile, 0.0))
     for c in range(3):
-        out[c * 8 : c * 8 + 8] = tiles[c]
+        out[c * 4 : c * 4 + 4] = even[c] + pltpu.roll(odd[c], 8, 1)
     for n, tile in enumerate(near):
-        out[24 + n * 4 : 28 + n * 4] = tile[0:4]
-    out[60:64] = jnp.zeros((4, 128), F32)
+        out[12 + n * 4 : 16 + n * 4] = tile[0:4]
     for copy in load_all([(out, out_h.at[x]) for x in range(GX)], sems):
         copy.wait()
 
@@ -455,7 +468,16 @@
                 uy[f, pl.ds(s * 256 + 5 + k, 8, stride=32)] = jnp.where(first, low, yl[f, at])
                 uy[f, pl.ds(s * 256 + 24 + k, 8, stride=32)] = jnp.where(last, high, yr[f, at])
 
-    def faces_y(x, carry):
+    for s in range(2):
+
+        def load_end(f, s=s):
+            return states(*[uy[f, pl.ds(s * 256 + 21 + k, 8, stride=32)] for k in range(6)])
+
+        def store_end(f, flux, s=s):
+            fy[f, pl.ds(s * 192 + 16, 8, stride=24)] = flux
+
+        fluxes(load_end, 1, store_end)
+    def faces_y(x):
         for s in range(2):
 
             def load(f):
@@ -465,32 +487,28 @@
                 fy[f, pl.ds(pl.multiple_of(x * 24 + s * 8, 8), 8)] = flux
 
             fluxes(load, 1, store)
-        return carry
-
-    lax.fori_loop(0, 16, faces_y, 0)
-    for s in range(2):
-
-        def load_end(f, s=s):
-            return states(*[uy[f, pl.ds(s * 256 + 21 + k, 8, stride=32)] for k in range(6)])
-
-        def store_end(f, flux, s=s):
-            fy[f, pl.ds(s * 192 + 16, 8, stride=24)] = flux
-
-        fluxes(load_end, 1, store_end)
+
     loads[9].wait()
 
-    def gather(x, carry):
+    def gather(x):
         for f in range(NF):
             for s in range(2):
                 at = pl.multiple_of(x * 16 + s * 8, 8)
                 rows = pl.ds(at, 8)
-                change = along_z[f, rows] + (fx[f, rows] - fx[f, pl.ds(at + 16, 8)])
-                y = x * 24 + s * 8
-                out[f, rows] = change + (fy[f, pl.ds(pl.multiple_of(y, 8), 8)] - fy[f, pl.ds(y + 1, 8)])
+                change = along_z[f, rows] + (fx[f, rows] - fx[f, pl.ds(pl.multiple_of(at + 16, 8), 8)])
+                y = pl.multiple_of(x * 24 + s * 8, 8)
+                out[f, rows] = change + (fy[f, pl.ds(y, 8)] - fy[f, pl.ds(y + 1, 8)])
+
+    def both(x, carry):
+        gather(x - 1)
+        faces_y(x)
         return carry
 
+    faces_y(0)
     for part in range(4):
-        lax.fori_loop(part * 4, part * 4 + 4, gather, 0)
+        lax.fori_loop(part * 4 + 1, min(part * 4 + 5, 16), both, 0)
+        if part == 3:
+            gather(15)
         rows = slice(part * 64, part * 64 + 64)
         late += load_all([(out.at[:, rows], out_h.at[:, rows])], sems.at[10 + count + part : 11 + count + part])
     for copy in late:
@@ -513,7 +531,7 @@
     for dx in range(3):
         here = jnp.clip(px + dx - 1, 0, GX - 1)
         inside = here == px + dx - 1
-        blocks.append([jnp.where(inside, far[here, 24 + n * 4 : 28 + n * 4], 0.0) for n in range(9)])
+        blocks.append([jnp.where(inside, far[here, 12 + n * 4 : 16 + n * 4], 0.0) for n in range(9)])
     gap = jnp.zeros((4, 128), F32)
     around = jnp.concatenate(
         [jnp.concatenate([blocks[dx][dy * 3 + c] for dx in range(3) for dy in range(3)] + [gap], 0) for c in range(3)], 1
@@ -521,7 +539,11 @@
     zero = mxu(sel_zero[...], jnp.concatenate(split(around), 1))
     zero = zero[:, :384] + zero[:, 384:]
     arrays = [zero[c * WIN : c * WIN + WIN] * lane_odd[c : c + 1] for c in range(4)]
-    gathered = jnp.concatenate([far[:, c * 8 : c * 8 + 8].reshape(128, 128) for c in range(3)], 1)
+    packed = [jnp.concatenate([far[x, c * 4 : c * 4 + 4] for x in range(GX)], 0) for c in range(3)]
+    lower = lane_ids((128, 128)) % 16 < 8
+    gathered = jnp.concatenate(
+        [jnp.where(lower, jnp.concatenate([rows, pltpu.roll(rows, 120, 1)], 0), 0.0) for rows in packed], 1
+    )
     speeds = gathered[:, 256:]
     fastest = jnp.max(jnp.where(lane_ids((128, 128)) >= 64, speeds, 0.0))
 
@@ -536,25 +558,29 @@
         return y[:, :384] + y[:, 384:]
 
     dev = lax.broadcasted_iota(jnp.int32, (128, 1), 0)
-    raised = lifted(gathered, ((dev // 8) % 2).astype(F32), (dev % 2).astype(F32))
+    raised = lifted(gathered, ((dev // 4) % 2).astype(F32), (dev // 64).astype(F32))
     two = picked(agg[...], raised)
     cell = lax.broadcasted_iota(jnp.int32, (32, 1), 0)
     raised_two = lifted(two, ((cell // 4) % 2).astype(F32), (cell % 2).astype(F32))
 
-    def window(level, columns, count_y, shift):
+    def window(level, columns, shift):
         tx, ty = px >> (level - 1), py >> (level - 1)
         row = lax.broadcasted_iota(jnp.int32, (WIN, columns), 0)
         col = lax.broadcasted_iota(jnp.int32, (WIN, columns), 1)
         i, j = row // 6, row % 6
         i = jnp.where((tx & 1) == 1, 5 - i, i) + 2 * ((tx >> 1) - 1)
         j = jnp.where((ty & 1) == 1, 5 - j, j) + 2 * ((ty >> 1) - 1)
-        sx, sy = (col // count_y) >> shift, (col % count_y) >> shift
+        if columns == 128:
+            sx, sy = (col % 64) // 4, 2 * (col % 4) + col // 64
+        else:
+            sx, sy = col // 4, col % 4
+        sx, sy = sx >> shift, sy >> shift
         return ((row < 36) & (sx == i) & (sy == j)).astype(F32).astype(BF16)
 
     levels = (
-        picked(window(1, 128, 8, 0), gathered)
-        + picked(window(2, 128, 8, 1), raised)
-        + picked(window(3, 32, 4, 1), raised_two)
+        picked(window(1, 128, 0), gathered)
+        + picked(window(2, 128, 1), raised)
+        + picked(window(3, 32, 1), raised_two)
     )
     sign = jnp.ones((1, 384), F32)
     for level in (1, 2, 3):
@@ -591,9 +617,13 @@
     flip = flip * (1.0 - 2.0 * info[9:10] * gamma_odd[2 * NG :])
     total = base
     for _ in range(3):
-        total = base + flip * exact(down[...], flip * exact(total, expand[...]))
+        parents = mxu(split_rows(total), expand[...])
+        pieces = jnp.concatenate(split(flip * (parents[:NG] + parents[NG:])), 1)
+        carried = mxu(down[...], pieces)
+        total = base + flip * (carried[:, :128] + carried[:, 128:])
     rows = jnp.concatenate([pltpu.roll(total, (128 - 16 * c) % 128, 1) for c in range(4)], 0)[:, :16]
-    spreads = exact(rows, spread[...])
+    spreads = mxu(split_rows(rows), spread[...])
+    spreads = spreads[: 4 * NG] + spreads[4 * NG :]
     terms = jnp.concatenate(
         [
             jnp.concatenate([spreads[c * NG : c * NG + NG, k * 128 : k * 128 + 128] for k in range(3)], 0)
@@ -601,12 +631,14 @@
         ],
         1,
     )
-    field[...] = exact(poly[...], terms)
+    values = mxu(poly[...], jnp.concatenate(split(terms), 1))
+    field[...] = values[:, :512] + values[:, 512:]
     step = jnp.full((8, 128), COURANT / SUB, F32) / fastest
     for copy in late:
         copy.wait()
     stores = []
-    for half in range(2):
+    for part in range(4):
+        half = part // 2
 
         def finish(x, carry, half=half):
             for s in range(2):
@@ -626,11 +658,12 @@
                     result[f, rows] = old[f] + step * slope
             return carry
 
-        lax.fori_loop(0, 8, finish, 0)
-        rows = slice(half * 128, half * 128 + 128)
-        for k, (source, target) in enumerate(((result, section), (force, accel))):
-            stores.append(pltpu.make_async_copy(source.at[:, rows], target.at[:, rows], sems.at[6 + 2 * half + k]))
-            stores[-1].start()
+        lax.fori_loop((part % 2) * 4, (part % 2) * 4 + 4, finish, 0)
+        rows = slice(part * 64, part * 64 + 64)
+        stores += load_all(
+            [(result.at[:, rows], section.at[:, rows]), (force.at[:, rows], accel.at[:, rows])],
+            sems.at[6 + 2 * part : 8 + 2 * part],
+        )
     for copy in stores:
         copy.wait()
 
@@ -702,8 +735,8 @@
         relay_kernel,
         "relay",
         [pos, (column.reshape(GY * 24, 128), VMEM), (along_z, HBM)] + halos,
-        [((GX, 64, 128), HBM)],
-        [pltpu.VMEM((64, 128), F32), pltpu.SemaphoreType.DMA((GX,))],
+        [((GX, 48, 128), HBM)],
+        [pltpu.VMEM((48, 128), F32), pltpu.SemaphoreType.DMA((GX,))],
         (10**4, 10**6, 0),
     )
     far = lax.all_to_all(chunks, "mx", 0, 0)
@@ -738,7 +771,7 @@
             pltpu.VMEM((3, ROWS, 128), F32),
             block,
             block,
-            pltpu.SemaphoreType.DMA((10,)),
+            pltpu.SemaphoreType.DMA((14,)),
         ],
         (10**8, 8 * 10**6, 0),
     )

time: 54.8 us -> 52.6 us (0.960)
  waiting for transfers between devices: 4.66 us -> 3.29 us
  Pallas kernels: 25.1 us -> 24.3 us
    all_to_all x1, waiting for transfers between devices: 2.8 us -> 1.43 us  [shards(): far = lax.all_to_all(chunks, 'mx', 0, 0)]
    pallas_call x5, Pallas kernels: 25.1 us -> 24.3 us  [call(): pl.pallas_call(kernel, out_shape=[pltpu.HBM(s, t) if spec is HBM else jax...]
  transfers between devices with their start and end apart: 6 -> 6, of which waited for: 2 -> 2; matrix products, arithmetic and copies ran while one was open for 0% -> 0% of each run, Pallas kernels for 23% -> 24%
where the time goes in v3:
time: 52.6 us; the launch traced here: 52.2 us
  Pallas kernels  24.3 us (46%)
  starting transfers between devices  23.9 us (45%)
  waiting for transfers between devices  3.29 us (6%)
  between operations  0.72 us (1%)
    pallas_call x5, Pallas kernels, call(): pl.pallas_call(kernel, out_shape=[pltpu.HBM(s, t) if spec is HBM else jax...  24.3 us
    all_to_all x1, starting transfers between devices, shards(): far = lax.all_to_all(chunks, 'mx', 0, 0)  8.18 us
    all_to_all x1, starting transfers between devices, shards(): column = lax.all_to_all(pay, 'my', 0, 0)  8.11 us
    ppermute x1, starting transfers between devices, shards(): xl = lax.ppermute(xhi, 'mx', up_x)  3.5 us
    all_to_all x1, waiting for transfers between devices, shards(): column = lax.all_to_all(pay, 'my', 0, 0)  1.85 us
    ppermute x1, starting transfers between devices, shards(): yl = lax.ppermute(yhi, 'my', up_y)  1.48 us
    all_to_all x1, waiting for transfers between devices, shards(): far = lax.all_to_all(chunks, 'mx', 0, 0)  1.43 us
    ppermute x1, starting transfers between devices, shards(): xr = lax.ppermute(xlo, 'mx', down_x)  1.29 us
  transfers between devices with their start and end apart: 6, of which 2 were waited for; matrix products, arithmetic and copies ran while one was open for 0% of the time, Pallas kernels for 24%

profile of v3, /device:TPU:0, one launch (start us, length us, event | category | flops | bytes accessed | tf_op | source)
XLA Modules:
  0.0 52.2 jit_solution(18114899687215052266)
XLA Ops:
  0.6 3.6 %prepare.1 = (f32[8,24,128]{2,1,0:T(8,128)}, f32[15,256,128]{2,1,0:T(8,128)S(1)}, f32[15,48,128]{2,1,0:T(8,128)}, f32[15,48,128]{2,1,0:T(8,128)}, f32[15,48,128]{2,1,0:T(8,128)}, /*index=5*/f32[15,48,128]{2,1,0:T(8,128)}) custom-call(f32[1,256,128]{2,1,0:T(8,128)} %bitcast.17, f32[3,256,128]{2,1,0:T(8,128)} %bitcast.14, f32[1,256,128]{2,1,0:T(8,128)} %bitcast.20, ...), custom_call_target="tpu_custom_call" | custom-call | flops 10000000 | bytes 4000000 | tf_op jit(solution)/shard_map/prepare/pallas_call | solution.py:679
  4.2 3.5 %collective-permute-start = (f32[15,48,128]{2,1,0:T(8,128)}, f32[15,48,128]{2,1,0:T(8,128)S(1)}, u32[]{:S(2)}, u32[]{:S(2)}) collective-permute-start(f32[15,48,128]{2,1,0:T(8,128)} %get-tuple-element.27), channel_id=1, source_target_pairs={{0,8},{8,16},{16,24},{24,32},{32,40},{40,48},{48,56},{56,64},{64,7... | collective-permute-start | bytes 1105928 | tf_op jit(solution)/shard_map/ppermute | solution.py:723
  7.7 1.3 %collective-permute-start.1 = (f32[15,48,128]{2,1,0:T(8,128)}, f32[15,48,128]{2,1,0:T(8,128)S(1)}, u32[]{:S(2)}, u32[]{:S(2)}) collective-permute-start(f32[15,48,128]{2,1,0:T(8,128)} %get-tuple-element.28), channel_id=1, source_target_pairs={{8,0},{16,8},{24,16},{32,24},{40,32},{48,40},{56,48},{64,56},{72,6... | collective-permute-start | bytes 1105928 | tf_op jit(solution)/shard_map/ppermute | solution.py:724
  9.0 1.5 %collective-permute-start.2 = (f32[15,48,128]{2,1,0:T(8,128)}, f32[15,48,128]{2,1,0:T(8,128)S(1)}, u32[]{:S(2)}, u32[]{:S(2)}) collective-permute-start(f32[15,48,128]{2,1,0:T(8,128)} %get-tuple-element.29), channel_id=1, source_target_pairs={{0,1},{1,2},{2,3},{3,4},{4,5},{5,6},{6,7},{8,9},{9,10},{10,11},{11... | collective-permute-start | bytes 1105928 | tf_op jit(solution)/shard_map/ppermute | solution.py:721
  10.5 1.3 %collective-permute-start.3 = (f32[15,48,128]{2,1,0:T(8,128)}, f32[15,48,128]{2,1,0:T(8,128)S(1)}, u32[]{:S(2)}, u32[]{:S(2)}) collective-permute-start(f32[15,48,128]{2,1,0:T(8,128)} %get-tuple-element.30), channel_id=1, source_target_pairs={{1,0},{2,1},{3,2},{4,3},{5,4},{6,5},{7,6},{9,8},{10,9},{11,10},{12... | collective-permute-start | bytes 1105928 | tf_op jit(solution)/shard_map/ppermute | solution.py:722
  11.8 8.1 %all-to-all-start = ((f32[8,24,128]{2,1,0:T(8,128)}), f32[8,24,128]{2,1,0:T(8,128)S(1)}, u32[]{:S(2)}, u32[]{:S(2)}) async-start(f32[8,24,128]{2,1,0:T(8,128)} %get-tuple-element.25), calls=%async_computation | async-start | bytes 196608 | tf_op jit(solution)/shard_map/all_to_all | solution.py:720
  19.9 3.9 %flux_z.1.rest_0_.along_z_h = f32[15,256,128]{2,1,0:T(8,128)} custom-call(f32[15,256,128]{2,1,0:T(8,128)S(1)} %get-tuple-element.26.u), custom_call_target="tpu_custom_call" | custom-call | flops 20000000 | bytes 4000000 | tf_op jit(solution)/shard_map/flux_z/pallas_call | solution.py:679
  23.8 0.1 pad_add_fusion.pos
  23.9 1.8 %all-to-all-done = f32[8,24,128]{2,1,0:T(8,128)S(1)} async-done(((f32[8,24,128]{2,1,0:T(8,128)}), f32[8,24,128]{2,1,0:T(8,128)S(1)}, u32[]{:S(2)}, u32[]{:S(2)}) %all-to-all-start) | async-done | bytes 98336 | tf_op jit(solution)/shard_map/all_to_all | solution.py:720
  25.7 0.0 collective-permute-done.rest_1_.xl
  25.7 0.0 collective-permute-done.1.rest_2_.xr
  25.7 0.0 collective-permute-done.2.rest_3_.yl_h
  25.7 0.0 collective-permute-done.3.rest_4_.yr_h
  25.7 1.5 %relay.1 = f32[16,48,128]{2,1,0:T(8,128)} custom-call(s32[2]{0:T(128)S(1)} %pad_add_fusion.pos, f32[192,128]{1,0:T(8,128)S(1)} %bitcast.10, f32[15,256,128]{2,1,0:T(8,128)} %flux_z.1.rest_0_.along_z_h, f32[15,48,128]{2,1,0:T(8,128)S(1)} %collective-permute-done.rest_1_.xl, f32[15,48,128]{2,1,0:T(8,128)S(1)} %collective-permute-done.1.rest_2_.xr, ...), custom_call_target="tpu_custom_call" | custom-call | flops 10000 | bytes 1000000 | tf_op jit(solution)/shard_map/relay/pallas_call | solution.py:679
  27.2 8.2 %all-to-all-start.1 = ((f32[16,48,128]{2,1,0:T(8,128)}), f32[16,48,128]{2,1,0:T(8,128)S(1)}, u32[]{:S(2)}, u32[]{:S(2)}) async-start(f32[16,48,128]{2,1,0:T(8,128)} %relay.1), calls=%async_computation.1 | async-start | bytes 786432 | tf_op jit(solution)/shard_map/all_to_all | solution.py:742
  35.4 8.5 %flux_xy.1 = (f32[15,256,128]{2,1,0:T(8,128)}, bf16[168,800]{1,0:T(8,128)(2,1)S(1)}, bf16[168,800]{1,0:T(8,128)(2,1)S(1)}, bf16[160,40]{1,0:T(8,128)(2,1)S(1)}, ...) custom-call(s32[2]{0:T(128)S(1)} %pad_add_fusion.pos, ...), custom_call_target="tpu_custom_call" | custom-call | flops 40000000 | bytes 6000000 | tf_op jit(solution)/shard_map/flux_xy/pallas_call | solution.py:679
  43.9 1.4 %all-to-all-done.1.far = f32[16,48,128]{2,1,0:T(8,128)S(1)} async-done(((f32[16,48,128]{2,1,0:T(8,128)}), f32[16,48,128]{2,1,0:T(8,128)S(1)}, u32[]{:S(2)}, u32[]{:S(2)}) %all-to-all-start.1) | async-done | bytes 393248 | tf_op jit(solution)/shard_map/all_to_all | solution.py:742
  45.4 6.8 %tree.1 = (f32[15,256,128]{2,1,0:T(8,128)}, f32[3,256,128]{2,1,0:T(8,128)}) custom-call(s32[2]{0:T(128)S(1)} %pad_add_fusion.pos, f32[16,48,128]{2,1,0:T(8,128)S(1)} %all-to-all-done.1.far, f32[1,256,128]{2,1,0:T(8,128)} %bitcast.19, f32[3,256,128]{2,1,0:T(8,128)} %bitcast.16, f32[1,256,128]{2,1,0:T(8,128)} %bitcast.22, f32[1,256,128]{2,1,0:T(8,128)} %bitcast.25, ...), custom_call_target="tpu_custom_call" | custom-call | flops 100000000 | bytes 8000000 | tf_op jit(solution)/shard_map/tree/pallas_call | solution.py:679
Async XLA Ops:
  4.2 21.5 %collective-permute-start = (f32[15,48,128]{2,1,0:T(8,128)}, f32[15,48,128]{2,1,0:T(8,128)S(1)}, u32[]{:S(2)}, u32[]{:S(2)}) collective-permute-start(f32[15,48,128]{2,1,0:T(8,128)} %get-tuple-element.27), channel_id=1, source_target_pairs={{0,8},{8,16},{16,24},{24,32},{32,40},{40,48},{48,56},{56,64},{64,7... | collective-permute-start | bytes 1105928 | tf_op jit(solution)/shard_map/ppermute | solution.py:723
  7.7 18.0 %collective-permute-start.1 = (f32[15,48,128]{2,1,0:T(8,128)}, f32[15,48,128]{2,1,0:T(8,128)S(1)}, u32[]{:S(2)}, u32[]{:S(2)}) collective-permute-start(f32[15,48,128]{2,1,0:T(8,128)} %get-tuple-element.28), channel_id=1, source_target_pairs={{8,0},{16,8},{24,16},{32,24},{40,32},{48,40},{56,48},{64,56},{72,6... | collective-permute-start | bytes 1105928 | tf_op jit(solution)/shard_map/ppermute | solution.py:724
  9.0 16.7 %collective-permute-start.2 = (f32[15,48,128]{2,1,0:T(8,128)}, f32[15,48,128]{2,1,0:T(8,128)S(1)}, u32[]{:S(2)}, u32[]{:S(2)}) collective-permute-start(f32[15,48,128]{2,1,0:T(8,128)} %get-tuple-element.29), channel_id=1, source_target_pairs={{0,1},{1,2},{2,3},{3,4},{4,5},{5,6},{6,7},{8,9},{9,10},{10,11},{11... | collective-permute-start | bytes 1105928 | tf_op jit(solution)/shard_map/ppermute | solution.py:721
  10.5 15.2 %collective-permute-start.3 = (f32[15,48,128]{2,1,0:T(8,128)}, f32[15,48,128]{2,1,0:T(8,128)S(1)}, u32[]{:S(2)}, u32[]{:S(2)}) collective-permute-start(f32[15,48,128]{2,1,0:T(8,128)} %get-tuple-element.30), channel_id=1, source_target_pairs={{1,0},{2,1},{3,2},{4,3},{5,4},{6,5},{7,6},{9,8},{10,9},{11,10},{12... | collective-permute-start | bytes 1105928 | tf_op jit(solution)/shard_map/ppermute | solution.py:722
  11.8 13.9 %all-to-all-start = ((f32[8,24,128]{2,1,0:T(8,128)}), f32[8,24,128]{2,1,0:T(8,128)S(1)}, u32[]{:S(2)}, u32[]{:S(2)}) async-start(f32[8,24,128]{2,1,0:T(8,128)} %get-tuple-element.25), calls=%async_computation | async-start | bytes 196608 | tf_op jit(solution)/shard_map/all_to_all | solution.py:720
  27.2 18.1 %all-to-all-start.1 = ((f32[16,48,128]{2,1,0:T(8,128)}), f32[16,48,128]{2,1,0:T(8,128)S(1)}, u32[]{:S(2)}, u32[]{:S(2)}) async-start(f32[16,48,128]{2,1,0:T(8,128)} %relay.1), calls=%async_computation.1 | async-start | bytes 786432 | tf_op jit(solution)/shard_map/all_to_all | solution.py:742

commit v4 on v3

--- a/solution.py
+++ b/solution.py
@@ -273,24 +273,19 @@
     ]
 
 
-def prepare_kernel(den, mom, ene, ent, tra, flags, left, right, flag, pay_h, u, xlo, xhi, ylo_h, yhi_h, pay, ylo, yhi, fl, flv, leftv, rightv, flagv, sems):
+def prepare_kernel(pos, den, mom, ene, ent, tra, flags, left, right, flag, pay_h, u, xa, xb, ya_h, yb_h, *scratch):
+    pay, ya, yb, fl, flv, leftv, rightv, flagv, sems = scratch
     small = load_all(zip((flags, left, right, flag), (flv, leftv, rightv, flagv)), sems.at[7:11])
     loads = load_all(fields_into((den, mom, ene, ent, tra), u), sems.at[0:5])
-    for copy in loads:
-        copy.wait()
-    slabs = load_all([(u.at[:, 0:48], xlo), (u.at[:, 208:256], xhi)], sems.at[5:7])
-    for f in range(NF):
-        for k in range(3):
-            for s in range(2):
-                ylo[f, k * 16 + s * 8 : k * 16 + s * 8 + 8] = u[f, pl.ds(s * 128 + k, 8, stride=16)]
-                yhi[f, k * 16 + s * 8 : k * 16 + s * 8 + 8] = u[f, pl.ds(s * 128 + 13 + k, 8, stride=16)]
-    slabs += load_all([(ylo, ylo_h), (yhi, yhi_h)], sems.at[11:13])
+    even_x, even_y = pos[0] % 2 == 0, pos[1] % 2 == 0
     for copy in small:
         copy.wait()
     fl[...] = jnp.zeros((8, 128), F32)
     fl[0:2, 0:16] = flv[0].astype(F32)
     fl[2:4, 0:16] = flv[1].astype(F32)
     tile = mxu(fl[...].astype(BF16), flagv[...])
+    for k in (0, 1, 3):
+        loads[k].wait()
     rho = u[0]
     sums = exact(leftv[...], exact(rho, rightv[...]))
     inverse = 1.0 / rho
@@ -316,7 +311,21 @@
     tiles[2] = jnp.where((row == 4) & (lane >= 64) & (lane < 72), fastest, tiles[2])
     for c in range(3):
         pay[c * 8 : c * 8 + 8] = tiles[c]
-    slabs += load_all([(pay, pay_h.at[y]) for y in range(GY)], sems.at[13 : 13 + GY])
+    slabs = load_all([(pay, pay_h.at[y]) for y in range(GY)], sems.at[13 : 13 + GY])
+    for k in (2, 4):
+        loads[k].wait()
+    row_a, row_b = jnp.where(even_x, 208, 0), jnp.where(even_x, 0, 208)
+    slabs += load_all(
+        [(u.at[:, pl.ds(pl.multiple_of(r, 8), 48)], slab) for r, slab in ((row_a, xa), (row_b, xb))], sems.at[5:7]
+    )
+    for k in range(3):
+        for s in range(2):
+            at = slice(k * 16 + s * 8, k * 16 + s * 8 + 8)
+            for f in range(NF):
+                low, high = u[f, pl.ds(s * 128 + k, 8, stride=16)], u[f, pl.ds(s * 128 + 13 + k, 8, stride=16)]
+                ya[f, at] = jnp.where(even_y, high, low)
+                yb[f, at] = jnp.where(even_y, low, high)
+    slabs += load_all([(ya, ya_h), (yb, yb_h)], sems.at[11:13])
     for copy in slabs:
         copy.wait()
 
@@ -414,14 +423,16 @@
         copy.wait()
 
 
-def flux_xy_kernel(pos, den, mom, ene, ent, tra, along_z_h, xl, xr, yl_h, yr_h, *args):
+def flux_xy_kernel(pos, den, mom, ene, ent, tra, along_z_h, xa, xb, ya_h, yb_h, *args):
     count = len(TREE_CONSTANTS)
     out_h = args[count]
     tables = args[count + 1 : 2 * count + 1]
-    ux, fx, uy, fy, yl, yr, along_z, out, sems = args[2 * count + 1 :]
+    ux, fx, uy, fy, ya, yb, along_z, out, sems = args[2 * count + 1 :]
+    even_x, even_y = pos[0] % 2 == 0, pos[1] % 2 == 0
+    row_a, row_b = [pl.ds(pl.multiple_of(jnp.where(even_x, p, q), 8), 48) for p, q in ((304, 0), (0, 304))]
     loads = load_all(
         fields_into((den, mom, ene, ent, tra), ux, rows=slice(48, 304))
-        + [(xl, ux.at[:, 0:48]), (xr, ux.at[:, 304:352]), (yl_h, yl), (yr_h, yr), (along_z_h, along_z)],
+        + [(xa, ux.at[:, row_a]), (xb, ux.at[:, row_b]), (ya_h, ya), (yb_h, yb), (along_z_h, along_z)],
         sems.at[0:10],
     )
     late = load_all(list(zip(args[:count], tables)), sems.at[10 : 10 + count])
@@ -465,8 +476,8 @@
             low, high = ux[f, pl.ds(48 + s * 128, 8, stride=16)], ux[f, pl.ds(63 + s * 128, 8, stride=16)]
             for k in range(3):
                 at = slice(k * 16 + s * 8, k * 16 + s * 8 + 8)
-                uy[f, pl.ds(s * 256 + 5 + k, 8, stride=32)] = jnp.where(first, low, yl[f, at])
-                uy[f, pl.ds(s * 256 + 24 + k, 8, stride=32)] = jnp.where(last, high, yr[f, at])
+                uy[f, pl.ds(s * 256 + 5 + k, 8, stride=32)] = jnp.where(first, low, jnp.where(even_y, yb[f, at], ya[f, at]))
+                uy[f, pl.ds(s * 256 + 24 + k, 8, stride=32)] = jnp.where(last, high, jnp.where(even_y, ya[f, at], yb[f, at]))
 
     for s in range(2):
 
@@ -525,7 +536,11 @@
     count = len(TREE_CONSTANTS)
     w_high, w_low, sel_zero, lane_odd, up, alpha_odd, agg, mask, info, expand, gamma_odd, down, spread, poly = args[:count]
     section, accel, rhs, field, result, force, u, change, sems = args[count:]
-    late = load_all(fields_into((den, mom, ene, ent, tra), u) + [(change_h, change)], sems.at[0:6])
+    late = []
+    for q in range(4):
+        rows = slice(q * 64, q * 64 + 64)
+        pairs = fields_into((den, mom, ene, ent, tra), u, rows, rows) + [(change_h.at[:, rows], change.at[:, rows])]
+        late.append(load_all(pairs, sems.at[8 + 6 * q : 14 + 6 * q]))
     px, py = pos[0], pos[1]
     blocks = []
     for dx in range(3):
@@ -634,11 +649,11 @@
     values = mxu(poly[...], jnp.concatenate(split(terms), 1))
     field[...] = values[:, :512] + values[:, 512:]
     step = jnp.full((8, 128), COURANT / SUB, F32) / fastest
-    for copy in late:
-        copy.wait()
     stores = []
     for part in range(4):
         half = part // 2
+        for copy in late[part]:
+            copy.wait()
 
         def finish(x, carry, half=half):
             for s in range(2):
@@ -662,7 +677,7 @@
         rows = slice(part * 64, part * 64 + 64)
         stores += load_all(
             [(result.at[:, rows], section.at[:, rows]), (force.at[:, rows], accel.at[:, rows])],
-            sems.at[6 + 2 * part : 8 + 2 * part],
+            sems.at[2 * part : 2 * part + 2],
         )
     for copy in stores:
         copy.wait()
@@ -705,23 +720,26 @@
     first = [con[n] for n in ("left", "right", "flag")]
     whole, slab = (NF, ROWS, 128), (NF, 48, 128)
     block, halo = pltpu.VMEM(whole, F32), pltpu.VMEM(slab, F32)
-    pay, u, xlo, xhi, ylo, yhi = call(
+    pay, u, xa, xb, ya, yb = call(
         prepare_kernel,
         "prepare",
-        fields + [(leaf_flags, HBM)] + [(x, HBM) for x in first],
+        [pos] + fields + [(leaf_flags, HBM)] + [(x, HBM) for x in first],
         [((GY, 24, 128), HBM), (whole, VMEM)] + [(slab, HBM)] * 4,
         [pltpu.VMEM((24, 128), F32), halo, halo, pltpu.VMEM((8, 128), F32), scratch_like(leaf_flags)]
         + [scratch_like(x) for x in first]
         + [pltpu.SemaphoreType.DMA((13 + GY,))],
         (10**7, 4 * 10**6, 10**5),
     )
-    up_x, down_x = [(i, i + 1) for i in range(GX - 1)], [(i + 1, i) for i in range(GX - 1)]
-    up_y, down_y = [(i, i + 1) for i in range(GY - 1)], [(i + 1, i) for i in range(GY - 1)]
+
+    def pairs(count, start):
+        lows = range(start, count - 1, 2)
+        return [(i, i + 1) for i in lows] + [(i + 1, i) for i in lows]
+
     column = lax.all_to_all(pay, "my", 0, 0)
-    yl = lax.ppermute(yhi, "my", up_y)
-    yr = lax.ppermute(ylo, "my", down_y)
-    xl = lax.ppermute(xhi, "mx", up_x)
-    xr = lax.ppermute(xlo, "mx", down_x)
+    halos = [
+        (lax.ppermute(slab, axis, pairs(count, start)), ANY)
+        for slab, axis, count, start in ((xa, "mx", GX, 0), (xb, "mx", GX, 1), (ya, "my", GY, 0), (yb, "my", GY, 1))
+    ]
     (along_z,) = call(
         flux_z_kernel,
         "flux_z",
@@ -730,7 +748,6 @@
         [pltpu.VMEM((2 * NF, 144, 128), F32), pltpu.VMEM((2 * NF, 136, 128), F32), block, pltpu.SemaphoreType.DMA((5,))],
         (2 * 10**7, 4 * 10**6, 3 * 10**5),
     )
-    halos = [(x, ANY) for x in (xl, xr, yl, yr)]
     (chunks,) = call(
         relay_kernel,
         "relay",
@@ -771,7 +788,7 @@
             pltpu.VMEM((3, ROWS, 128), F32),
             block,
             block,
-            pltpu.SemaphoreType.DMA((14,)),
+            pltpu.SemaphoreType.DMA((32,)),
         ],
         (10**8, 8 * 10**6, 0),
     )

time: 52.6 us -> 48.7 us (0.926)
  starting transfers between devices: 23.9 us -> 20 us
    ppermute x4, starting transfers between devices: 7.57 us -> 3.09 us  [shards(): lax.ppermute(slab, axis, pairs(count, start))]
    all_to_all x1, starting transfers between devices: 8.18 us -> 9.2 us  [shards(): far = lax.all_to_all(chunks, 'mx', 0, 0)]
  transfers between devices with their start and end apart: 6 -> 6, of which waited for: 2 -> 2; matrix products, arithmetic and copies ran while one was open for 0% -> 0% of each run, Pallas kernels for 24% -> 26%
where the time goes in v4:
time: 48.7 us; the launch traced here: 48.4 us
  Pallas kernels  24.2 us (50%)
  starting transfers between devices  20 us (41%)
  waiting for transfers between devices  3.38 us (7%)
  between operations  0.71 us (1%)
    pallas_call x5, Pallas kernels, call(): pl.pallas_call(kernel, out_shape=[pltpu.HBM(s, t) if spec is HBM else jax...  24.2 us
    all_to_all x1, starting transfers between devices, shards(): far = lax.all_to_all(chunks, 'mx', 0, 0)  9.2 us
    all_to_all x1, starting transfers between devices, shards(): column = lax.all_to_all(pay, 'my', 0, 0)  7.73 us
    ppermute x4, starting transfers between devices, shards(): lax.ppermute(slab, axis, pairs(count, start))  3.09 us
    all_to_all x1, waiting for transfers between devices, shards(): column = lax.all_to_all(pay, 'my', 0, 0)  1.93 us
    all_to_all x1, waiting for transfers between devices, shards(): far = lax.all_to_all(chunks, 'mx', 0, 0)  1.44 us
  transfers between devices with their start and end apart: 6, of which 2 were waited for; matrix products, arithmetic and copies ran while one was open for 0% of the time, Pallas kernels for 26%

profile of v4, /device:TPU:0, one launch (start us, length us, event | category | flops | bytes accessed | tf_op | source)
XLA Modules:
  0.0 48.4 jit_solution(2379637883996016895)
XLA Ops:
  0.6 0.1 pad_add_fusion.pos
  0.7 4.0 %prepare.1 = (f32[8,24,128]{2,1,0:T(8,128)}, f32[15,256,128]{2,1,0:T(8,128)S(1)}, f32[15,48,128]{2,1,0:T(8,128)}, f32[15,48,128]{2,1,0:T(8,128)}, f32[15,48,128]{2,1,0:T(8,128)}, /*index=5*/f32[15,48,128]{2,1,0:T(8,128)}) custom-call(s32[2]{0:T(128)S(1)} %pad_add_fusion.pos, f32[1,256,128]{2,1,0:T(8,128)} %bitcast.17, f32[3,256,128]{2,1,0:T(8,128)} %bitcast.14, ...), custom_call_target="tpu_custom_call" | custom-call | flops 10000000 | bytes 4000000 | tf_op jit(solution)/shard_map/prepare/pallas_call | solution.py:694
  4.7 1.7 %collective-permute-start = (f32[15,48,128]{2,1,0:T(8,128)}, f32[15,48,128]{2,1,0:T(8,128)S(1)}, u32[]{:S(2)}, u32[]{:S(2)}) collective-permute-start(f32[15,48,128]{2,1,0:T(8,128)} %get-tuple-element.27), channel_id=1, source_target_pairs={{0,8},{16,24},{32,40},{48,56},{64,72},{80,88},{96,104},{112,120},{... | collective-permute-start | bytes 1105928 | tf_op jit(solution)/shard_map/ppermute | solution.py:740
  6.3 0.7 %collective-permute-start.1 = (f32[15,48,128]{2,1,0:T(8,128)}, f32[15,48,128]{2,1,0:T(8,128)S(1)}, u32[]{:S(2)}, u32[]{:S(2)}) collective-permute-start(f32[15,48,128]{2,1,0:T(8,128)} %get-tuple-element.28), channel_id=1, source_target_pairs={{8,16},{24,32},{40,48},{56,64},{72,80},{88,96},{104,112},{16,8},{3... | collective-permute-start | bytes 1105928 | tf_op jit(solution)/shard_map/ppermute | solution.py:740
  7.0 0.1 collective-permute-start.2
  7.1 0.7 %collective-permute-start.3 = (f32[15,48,128]{2,1,0:T(8,128)}, f32[15,48,128]{2,1,0:T(8,128)S(1)}, u32[]{:S(2)}, u32[]{:S(2)}) collective-permute-start(f32[15,48,128]{2,1,0:T(8,128)} %get-tuple-element.30), channel_id=1, source_target_pairs={{1,2},{3,4},{5,6},{2,1},{4,3},{6,5},{9,10},{11,12},{13,14},{10,9},... | collective-permute-start | bytes 1105928 | tf_op jit(solution)/shard_map/ppermute | solution.py:740
  7.8 7.7 %all-to-all-start = ((f32[8,24,128]{2,1,0:T(8,128)}), f32[8,24,128]{2,1,0:T(8,128)S(1)}, u32[]{:S(2)}, u32[]{:S(2)}) async-start(f32[8,24,128]{2,1,0:T(8,128)} %get-tuple-element.25), calls=%async_computation | async-start | bytes 196608 | tf_op jit(solution)/shard_map/all_to_all | solution.py:738
  15.5 3.9 %flux_z.1.rest_0_.along_z_h = f32[15,256,128]{2,1,0:T(8,128)} custom-call(f32[15,256,128]{2,1,0:T(8,128)S(1)} %get-tuple-element.26.u), custom_call_target="tpu_custom_call" | custom-call | flops 20000000 | bytes 4000000 | tf_op jit(solution)/shard_map/flux_z/pallas_call | solution.py:694
  19.4 1.9 %all-to-all-done = f32[8,24,128]{2,1,0:T(8,128)S(1)} async-done(((f32[8,24,128]{2,1,0:T(8,128)}), f32[8,24,128]{2,1,0:T(8,128)S(1)}, u32[]{:S(2)}, u32[]{:S(2)}) %all-to-all-start) | async-done | bytes 98336 | tf_op jit(solution)/shard_map/all_to_all | solution.py:738
  21.3 0.0 collective-permute-done.rest_1_.xa
  21.3 0.0 collective-permute-done.1.rest_2_.xb
  21.3 0.0 collective-permute-done.2.rest_3_.ya_h
  21.4 0.0 collective-permute-done.3.rest_4_.yb_h
  21.4 1.5 %relay.1 = f32[16,48,128]{2,1,0:T(8,128)} custom-call(s32[2]{0:T(128)S(1)} %pad_add_fusion.pos, f32[192,128]{1,0:T(8,128)S(1)} %bitcast.10, f32[15,256,128]{2,1,0:T(8,128)} %flux_z.1.rest_0_.along_z_h, f32[15,48,128]{2,1,0:T(8,128)S(1)} %collective-permute-done.rest_1_.xa, f32[15,48,128]{2,1,0:T(8,128)S(1)} %collective-permute-done.1.rest_2_.xb, ...), custom_call_target="tpu_custom_call" | custom-call | flops 10000 | bytes 1000000 | tf_op jit(solution)/shard_map/relay/pallas_call | solution.py:694
  22.9 9.2 %all-to-all-start.1 = ((f32[16,48,128]{2,1,0:T(8,128)}), f32[16,48,128]{2,1,0:T(8,128)S(1)}, u32[]{:S(2)}, u32[]{:S(2)}) async-start(f32[16,48,128]{2,1,0:T(8,128)} %relay.1), calls=%async_computation.1 | async-start | bytes 786432 | tf_op jit(solution)/shard_map/all_to_all | solution.py:759
  32.1 8.5 %flux_xy.1 = (f32[15,256,128]{2,1,0:T(8,128)}, bf16[168,800]{1,0:T(8,128)(2,1)S(1)}, bf16[168,800]{1,0:T(8,128)(2,1)S(1)}, bf16[160,40]{1,0:T(8,128)(2,1)S(1)}, ...) custom-call(s32[2]{0:T(128)S(1)} %pad_add_fusion.pos, ...), custom_call_target="tpu_custom_call" | custom-call | flops 40000000 | bytes 6000000 | tf_op jit(solution)/shard_map/flux_xy/pallas_call | solution.py:694
  40.6 1.4 %all-to-all-done.1.far = f32[16,48,128]{2,1,0:T(8,128)S(1)} async-done(((f32[16,48,128]{2,1,0:T(8,128)}), f32[16,48,128]{2,1,0:T(8,128)S(1)}, u32[]{:S(2)}, u32[]{:S(2)}) %all-to-all-start.1) | async-done | bytes 393248 | tf_op jit(solution)/shard_map/all_to_all | solution.py:759
  42.0 6.3 %tree.1 = (f32[15,256,128]{2,1,0:T(8,128)}, f32[3,256,128]{2,1,0:T(8,128)}) custom-call(s32[2]{0:T(128)S(1)} %pad_add_fusion.pos, f32[16,48,128]{2,1,0:T(8,128)S(1)} %all-to-all-done.1.far, f32[1,256,128]{2,1,0:T(8,128)} %bitcast.19, f32[3,256,128]{2,1,0:T(8,128)} %bitcast.16, f32[1,256,128]{2,1,0:T(8,128)} %bitcast.22, f32[1,256,128]{2,1,0:T(8,128)} %bitcast.25, ...), custom_call_target="tpu_custom_call" | custom-call | flops 100000000 | bytes 8000000 | tf_op jit(solution)/shard_map/tree/pallas_call | solution.py:694
Async XLA Ops:
  4.7 16.7 %collective-permute-start = (f32[15,48,128]{2,1,0:T(8,128)}, f32[15,48,128]{2,1,0:T(8,128)S(1)}, u32[]{:S(2)}, u32[]{:S(2)}) collective-permute-start(f32[15,48,128]{2,1,0:T(8,128)} %get-tuple-element.27), channel_id=1, source_target_pairs={{0,8},{16,24},{32,40},{48,56},{64,72},{80,88},{96,104},{112,120},{... | collective-permute-start | bytes 1105928 | tf_op jit(solution)/shard_map/ppermute | solution.py:740
  6.3 15.0 %collective-permute-start.1 = (f32[15,48,128]{2,1,0:T(8,128)}, f32[15,48,128]{2,1,0:T(8,128)S(1)}, u32[]{:S(2)}, u32[]{:S(2)}) collective-permute-start(f32[15,48,128]{2,1,0:T(8,128)} %get-tuple-element.28), channel_id=1, source_target_pairs={{8,16},{24,32},{40,48},{56,64},{72,80},{88,96},{104,112},{16,8},{3... | collective-permute-start | bytes 1105928 | tf_op jit(solution)/shard_map/ppermute | solution.py:740
  7.0 14.3 %collective-permute-start.2 = (f32[15,48,128]{2,1,0:T(8,128)}, f32[15,48,128]{2,1,0:T(8,128)S(1)}, u32[]{:S(2)}, u32[]{:S(2)}) collective-permute-start(f32[15,48,128]{2,1,0:T(8,128)} %get-tuple-element.29), channel_id=1, source_target_pairs={{0,1},{2,3},{4,5},{6,7},{1,0},{3,2},{5,4},{7,6},{8,9},{10,11},{12,... | collective-permute-start | bytes 1105928 | tf_op jit(solution)/shard_map/ppermute | solution.py:740
  7.1 14.2 %collective-permute-start.3 = (f32[15,48,128]{2,1,0:T(8,128)}, f32[15,48,128]{2,1,0:T(8,128)S(1)}, u32[]{:S(2)}, u32[]{:S(2)}) collective-permute-start(f32[15,48,128]{2,1,0:T(8,128)} %get-tuple-element.30), channel_id=1, source_target_pairs={{1,2},{3,4},{5,6},{2,1},{4,3},{6,5},{9,10},{11,12},{13,14},{10,9},... | collective-permute-start | bytes 1105928 | tf_op jit(solution)/shard_map/ppermute | solution.py:740
  7.8 13.5 %all-to-all-start = ((f32[8,24,128]{2,1,0:T(8,128)}), f32[8,24,128]{2,1,0:T(8,128)S(1)}, u32[]{:S(2)}, u32[]{:S(2)}) async-start(f32[8,24,128]{2,1,0:T(8,128)} %get-tuple-element.25), calls=%async_computation | async-start | bytes 196608 | tf_op jit(solution)/shard_map/all_to_all | solution.py:738
  22.9 19.1 %all-to-all-start.1 = ((f32[16,48,128]{2,1,0:T(8,128)}), f32[16,48,128]{2,1,0:T(8,128)S(1)}, u32[]{:S(2)}, u32[]{:S(2)}) async-start(f32[16,48,128]{2,1,0:T(8,128)} %relay.1), calls=%async_computation.1 | async-start | bytes 786432 | tf_op jit(solution)/shard_map/all_to_all | solution.py:759

commit v5 on v4

--- a/solution.py
+++ b/solution.py
@@ -259,6 +259,10 @@
 PLACES = ((0, 1), (1, 3), (4, 1), (5, 1), (6, 9))
 
 
+def position():
+    return lax.axis_index("mx"), lax.axis_index("my")
+
+
 def load_all(pairs, sems):
     copies = [pltpu.make_async_copy(source, target, sems.at[k]) for k, (source, target) in enumerate(pairs)]
     for copy in copies:
@@ -273,19 +277,32 @@
     ]
 
 
-def prepare_kernel(pos, den, mom, ene, ent, tra, flags, left, right, flag, pay_h, u, xa, xb, ya_h, yb_h, *scratch):
-    pay, ya, yb, fl, flv, leftv, rightv, flagv, sems = scratch
+def prepare_kernel(den, mom, ene, ent, tra, flags, left, right, flag, pay_h, u, xa, xb, ya, yb, *scratch):
+    pos = position()
+    pay, sides, fl, flv, leftv, rightv, flagv, sems = scratch
     small = load_all(zip((flags, left, right, flag), (flv, leftv, rightv, flagv)), sems.at[7:11])
     loads = load_all(fields_into((den, mom, ene, ent, tra), u), sems.at[0:5])
     even_x, even_y = pos[0] % 2 == 0, pos[1] % 2 == 0
+    for copy in loads:
+        copy.wait()
+    row_a, row_b = jnp.where(even_x, 208, 0), jnp.where(even_x, 0, 208)
+    slabs = load_all(
+        [(u.at[:, pl.ds(pl.multiple_of(r, 8), 48)], slab) for r, slab in ((row_a, xa), (row_b, xb))], sems.at[5:7]
+    )
+    for f in range(NF):
+        for k in range(3):
+            for s in range(2):
+                at = slice(k * 16 + s * 8, k * 16 + s * 8 + 8)
+                sides[0, f, at] = u[f, pl.ds(s * 128 + k, 8, stride=16)]
+                sides[1, f, at] = u[f, pl.ds(s * 128 + 13 + k, 8, stride=16)]
+    side_a, side_b = jnp.where(even_y, 1, 0), jnp.where(even_y, 0, 1)
+    slabs += load_all([(sides.at[side_a], ya), (sides.at[side_b], yb)], sems.at[11:13])
     for copy in small:
         copy.wait()
     fl[...] = jnp.zeros((8, 128), F32)
     fl[0:2, 0:16] = flv[0].astype(F32)
     fl[2:4, 0:16] = flv[1].astype(F32)
     tile = mxu(fl[...].astype(BF16), flagv[...])
-    for k in (0, 1, 3):
-        loads[k].wait()
     rho = u[0]
     sums = exact(leftv[...], exact(rho, rightv[...]))
     inverse = 1.0 / rho
@@ -311,28 +328,14 @@
     tiles[2] = jnp.where((row == 4) & (lane >= 64) & (lane < 72), fastest, tiles[2])
     for c in range(3):
         pay[c * 8 : c * 8 + 8] = tiles[c]
-    slabs = load_all([(pay, pay_h.at[y]) for y in range(GY)], sems.at[13 : 13 + GY])
-    for k in (2, 4):
-        loads[k].wait()
-    row_a, row_b = jnp.where(even_x, 208, 0), jnp.where(even_x, 0, 208)
-    slabs += load_all(
-        [(u.at[:, pl.ds(pl.multiple_of(r, 8), 48)], slab) for r, slab in ((row_a, xa), (row_b, xb))], sems.at[5:7]
-    )
-    for k in range(3):
-        for s in range(2):
-            at = slice(k * 16 + s * 8, k * 16 + s * 8 + 8)
-            for f in range(NF):
-                low, high = u[f, pl.ds(s * 128 + k, 8, stride=16)], u[f, pl.ds(s * 128 + 13 + k, 8, stride=16)]
-                ya[f, at] = jnp.where(even_y, high, low)
-                yb[f, at] = jnp.where(even_y, low, high)
-    slabs += load_all([(ya, ya_h), (yb, yb_h)], sems.at[11:13])
+    slabs += load_all([(pay, pay_h.at[y]) for y in range(GY)], sems.at[13 : 13 + GY])
     for copy in slabs:
         copy.wait()
 
 
-def relay_kernel(pos, column, *rest):
+def relay_kernel(column, *rest):
     out_h, out, sems = rest[-3:]
-    y = pos[1]
+    y = position()[1]
     even = [column[pl.ds(c * 8 + 4, 4, stride=48)] for c in range(3)]
     odd = [column[pl.ds(c * 8 + 28, 4, stride=48)] for c in range(3)]
     near = []
@@ -423,7 +426,8 @@
         copy.wait()
 
 
-def flux_xy_kernel(pos, den, mom, ene, ent, tra, along_z_h, xa, xb, ya_h, yb_h, *args):
+def flux_xy_kernel(den, mom, ene, ent, tra, along_z_h, xa, xb, ya_h, yb_h, *args):
+    pos = position()
     count = len(TREE_CONSTANTS)
     out_h = args[count]
     tables = args[count + 1 : 2 * count + 1]
@@ -532,7 +536,7 @@
 )
 
 
-def tree_kernel(pos, far, den, mom, ene, ent, tra, change_h, *args):
+def tree_kernel(far, den, mom, ene, ent, tra, change_h, *args):
     count = len(TREE_CONSTANTS)
     w_high, w_low, sel_zero, lane_odd, up, alpha_odd, agg, mask, info, expand, gamma_odd, down, spread, poly = args[:count]
     section, accel, rhs, field, result, force, u, change, sems = args[count:]
@@ -541,7 +545,7 @@
         rows = slice(q * 64, q * 64 + 64)
         pairs = fields_into((den, mom, ene, ent, tra), u, rows, rows) + [(change_h.at[:, rows], change.at[:, rows])]
         late.append(load_all(pairs, sems.at[8 + 6 * q : 14 + 6 * q]))
-    px, py = pos[0], pos[1]
+    px, py = position()
     blocks = []
     for dx in range(3):
         here = jnp.clip(px + dx - 1, 0, GX - 1)
@@ -686,7 +690,6 @@
 ANY = pl.BlockSpec(memory_space=pl.ANY)
 HBM = pl.BlockSpec(memory_space=pltpu.HBM)
 VMEM = pl.BlockSpec(memory_space=pltpu.VMEM)
-SMEM = pl.BlockSpec(memory_space=pltpu.SMEM)
 
 
 def call(kernel, name, ins, outs, scratch, cost, aliases=None):
@@ -715,25 +718,23 @@
 def shards(density, momentum, energy, entropy, tracers, leaf_flags):
     con = {k: jnp.asarray(v) for k, v in constants().items()}
     fields = [(x.reshape(-1, ROWS, 128), HBM) for x in (density, momentum, energy, entropy, tracers)]
-    ix, iy = lax.axis_index("mx"), lax.axis_index("my")
-    pos = (jnp.stack([ix, iy]).astype(jnp.int32), SMEM)
     first = [con[n] for n in ("left", "right", "flag")]
     whole, slab = (NF, ROWS, 128), (NF, 48, 128)
     block, halo = pltpu.VMEM(whole, F32), pltpu.VMEM(slab, F32)
     pay, u, xa, xb, ya, yb = call(
         prepare_kernel,
         "prepare",
-        [pos] + fields + [(leaf_flags, HBM)] + [(x, HBM) for x in first],
+        fields + [(leaf_flags, HBM)] + [(x, HBM) for x in first],
         [((GY, 24, 128), HBM), (whole, VMEM)] + [(slab, HBM)] * 4,
-        [pltpu.VMEM((24, 128), F32), halo, halo, pltpu.VMEM((8, 128), F32), scratch_like(leaf_flags)]
+        [pltpu.VMEM((24, 128), F32), pltpu.VMEM((2, *slab), F32), pltpu.VMEM((8, 128), F32), scratch_like(leaf_flags)]
         + [scratch_like(x) for x in first]
         + [pltpu.SemaphoreType.DMA((13 + GY,))],
         (10**7, 4 * 10**6, 10**5),
     )
 
     def pairs(count, start):
-        lows = range(start, count - 1, 2)
-        return [(i, i + 1) for i in lows] + [(i + 1, i) for i in lows]
+        lows = range(start, count, 2)
+        return [(i, (i + 1) % count) for i in lows] + [((i + 1) % count, i) for i in lows]
 
     column = lax.all_to_all(pay, "my", 0, 0)
     halos = [
@@ -751,7 +752,7 @@
     (chunks,) = call(
         relay_kernel,
         "relay",
-        [pos, (column.reshape(GY * 24, 128), VMEM), (along_z, HBM)] + halos,
+        [(column.reshape(GY * 24, 128), VMEM), (along_z, HBM)] + halos,
         [((GX, 48, 128), HBM)],
         [pltpu.VMEM((48, 128), F32), pltpu.SemaphoreType.DMA((GX,))],
         (10**4, 10**6, 0),
@@ -761,7 +762,7 @@
     tend, *tables = call(
         flux_xy_kernel,
         "flux_xy",
-        [pos] + fields + [(along_z, HBM)] + halos + [(x, HBM) for x in second],
+        fields + [(along_z, HBM)] + halos + [(x, HBM) for x in second],
         [(whole, HBM)] + [(x.shape, VMEM, x.dtype) for x in second],
         [
             pltpu.VMEM((NF, 352, 128), F32),
@@ -779,7 +780,7 @@
     section, accel = call(
         tree_kernel,
         "tree",
-        [pos, (far, VMEM)] + fields + [(tend, HBM)] + [(x, VMEM) for x in tables],
+        [(far, VMEM)] + fields + [(tend, HBM)] + [(x, VMEM) for x in tables],
         [(whole, HBM), ((3, ROWS, 128), HBM)],
         [
             pltpu.VMEM((NA * WIN, 128), F32),

time: 48.7 us -> 44.6 us (0.916)
  starting transfers between devices: 20 us -> 17.3 us
  Pallas kernels: 24.2 us -> 22.1 us
  waiting for transfers between devices: 3.38 us -> 4.1 us
    ppermute x4, starting transfers between devices: 3.09 us -> 10.4 us  [shards(): lax.ppermute(slab, axis, pairs(count, start))]
    all_to_all x1, starting transfers between devices: 9.2 us -> 3.57 us  [shards(): far = lax.all_to_all(chunks, 'mx', 0, 0)]
    all_to_all x1, starting transfers between devices: 7.73 us -> 3.36 us  [shards(): column = lax.all_to_all(pay, 'my', 0, 0)]
    pallas_call x5, Pallas kernels: 24.2 us -> 22.1 us  [call(): pl.pallas_call(kernel, out_shape=[pltpu.HBM(s, t) if spec is HBM else jax...]
    all_to_all x1, waiting for transfers between devices: 1.44 us -> 2.25 us  [shards(): far = lax.all_to_all(chunks, 'mx', 0, 0)]
  transfers between devices with their start and end apart: 6 -> 6, of which waited for: 2 -> 2; matrix products, arithmetic and copies ran while one was open for 0% -> 0% of each run, Pallas kernels for 26% -> 27%
where the time goes in v5:
time: 44.6 us; the launch traced here: 44.2 us
  Pallas kernels  22.1 us (50%)
  starting transfers between devices  17.3 us (39%)
  waiting for transfers between devices  4.1 us (9%)
  between operations  0.69 us (2%)
    pallas_call x5, Pallas kernels, call(): pl.pallas_call(kernel, out_shape=[pltpu.HBM(s, t) if spec is HBM else jax...  22.1 us
    ppermute x4, starting transfers between devices, shards(): lax.ppermute(slab, axis, pairs(count, start))  10.4 us
    all_to_all x1, starting transfers between devices, shards(): far = lax.all_to_all(chunks, 'mx', 0, 0)  3.57 us
    all_to_all x1, starting transfers between devices, shards(): column = lax.all_to_all(pay, 'my', 0, 0)  3.36 us
    all_to_all x1, waiting for transfers between devices, shards(): far = lax.all_to_all(chunks, 'mx', 0, 0)  2.25 us
    all_to_all x1, waiting for transfers between devices, shards(): column = lax.all_to_all(pay, 'my', 0, 0)  1.84 us
  transfers between devices with their start and end apart: 6, of which 2 were waited for; matrix products, arithmetic and copies ran while one was open for 0% of the time, Pallas kernels for 27%

profile of v5, /device:TPU:0, one launch (start us, length us, event | category | flops | bytes accessed | tf_op | source)
XLA Modules:
  0.0 44.2 jit_solution(1528476333965389723)
XLA Ops:
  0.6 3.6 %prepare.1 = (f32[8,24,128]{2,1,0:T(8,128)}, f32[15,256,128]{2,1,0:T(8,128)S(1)}, f32[15,48,128]{2,1,0:T(8,128)}, f32[15,48,128]{2,1,0:T(8,128)}, f32[15,48,128]{2,1,0:T(8,128)}, /*index=5*/f32[15,48,128]{2,1,0:T(8,128)}) custom-call(f32[1,256,128]{2,1,0:T(8,128)} %bitcast.15, f32[3,256,128]{2,1,0:T(8,128)} %bitcast.12, f32[1,256,128]{2,1,0:T(8,128)} %bitcast.18, ...), custom_call_target="tpu_custom_call" | custom-call | flops 10000000 | bytes 4000000 | tf_op jit(solution)/shard_map/prepare/pallas_call | solution.py:697
  4.2 1.7 %collective-permute-start = (f32[15,48,128]{2,1,0:T(8,128)}, f32[15,48,128]{2,1,0:T(8,128)S(1)}, u32[]{:S(2)}, u32[]{:S(2)}) collective-permute-start(f32[15,48,128]{2,1,0:T(8,128)} %get-tuple-element.27), channel_id=1, source_target_pairs={{0,8},{16,24},{32,40},{48,56},{64,72},{80,88},{96,104},{112,120},{... | collective-permute-start | bytes 1105928 | tf_op jit(solution)/shard_map/ppermute | solution.py:741
  5.9 4.5 %collective-permute-start.1 = (f32[15,48,128]{2,1,0:T(8,128)}, f32[15,48,128]{2,1,0:T(8,128)S(1)}, u32[]{:S(2)}, u32[]{:S(2)}) collective-permute-start(f32[15,48,128]{2,1,0:T(8,128)} %get-tuple-element.28), channel_id=1, source_target_pairs={{8,16},{24,32},{40,48},{56,64},{72,80},{88,96},{104,112},{120,0},{... | collective-permute-start | bytes 1105928 | tf_op jit(solution)/shard_map/ppermute | solution.py:741
  10.4 0.0 collective-permute-start.2
  10.4 4.1 %collective-permute-start.3 = (f32[15,48,128]{2,1,0:T(8,128)}, f32[15,48,128]{2,1,0:T(8,128)S(1)}, u32[]{:S(2)}, u32[]{:S(2)}) collective-permute-start(f32[15,48,128]{2,1,0:T(8,128)} %get-tuple-element.30), channel_id=1, source_target_pairs={{1,2},{3,4},{5,6},{7,0},{2,1},{4,3},{6,5},{0,7},{9,10},{11,12},{13... | collective-permute-start | bytes 1105928 | tf_op jit(solution)/shard_map/ppermute | solution.py:741
  14.6 3.4 %all-to-all-start = ((f32[8,24,128]{2,1,0:T(8,128)}), f32[8,24,128]{2,1,0:T(8,128)S(1)}, u32[]{:S(2)}, u32[]{:S(2)}) async-start(f32[8,24,128]{2,1,0:T(8,128)} %get-tuple-element.25), calls=%async_computation | async-start | bytes 196608 | tf_op jit(solution)/shard_map/all_to_all | solution.py:739
  17.9 3.9 %flux_z.1.rest_0_.along_z_h = f32[15,256,128]{2,1,0:T(8,128)} custom-call(f32[15,256,128]{2,1,0:T(8,128)S(1)} %get-tuple-element.26.u), custom_call_target="tpu_custom_call" | custom-call | flops 20000000 | bytes 4000000 | tf_op jit(solution)/shard_map/flux_z/pallas_call | solution.py:697
  21.8 1.8 %all-to-all-done = f32[8,24,128]{2,1,0:T(8,128)S(1)} async-done(((f32[8,24,128]{2,1,0:T(8,128)}), f32[8,24,128]{2,1,0:T(8,128)S(1)}, u32[]{:S(2)}, u32[]{:S(2)}) %all-to-all-start) | async-done | bytes 98336 | tf_op jit(solution)/shard_map/all_to_all | solution.py:739
  23.7 0.0 collective-permute-done.rest_1_.xa
  23.7 0.0 collective-permute-done.1.rest_2_.xb
  23.7 0.0 collective-permute-done.2.rest_3_.ya_h
  23.7 0.0 collective-permute-done.3.rest_4_.yb_h
  23.7 0.9 %relay.1 = f32[16,48,128]{2,1,0:T(8,128)} custom-call(f32[192,128]{1,0:T(8,128)S(1)} %bitcast.8, f32[15,256,128]{2,1,0:T(8,128)} %flux_z.1.rest_0_.along_z_h, f32[15,48,128]{2,1,0:T(8,128)S(1)} %collective-permute-done.rest_1_.xa, f32[15,48,128]{2,1,0:T(8,128)S(1)} %collective-permute-done.1.rest_2_.xb, ...), custom_call_target="tpu_custom_call" | custom-call | flops 10000 | bytes 1000000 | tf_op jit(solution)/shard_map/relay/pallas_call | solution.py:697
  24.6 3.6 %all-to-all-start.1 = ((f32[16,48,128]{2,1,0:T(8,128)}), f32[16,48,128]{2,1,0:T(8,128)S(1)}, u32[]{:S(2)}, u32[]{:S(2)}) async-start(f32[16,48,128]{2,1,0:T(8,128)} %relay.1), calls=%async_computation.1 | async-start | bytes 786432 | tf_op jit(solution)/shard_map/all_to_all | solution.py:760
  28.2 7.9 %flux_xy.1 = (f32[15,256,128]{2,1,0:T(8,128)}, bf16[168,800]{1,0:T(8,128)(2,1)S(1)}, bf16[168,800]{1,0:T(8,128)(2,1)S(1)}, bf16[160,40]{1,0:T(8,128)(2,1)S(1)}, ...) custom-call(f32[1,256,128]{2,1,0:T(8,128)} %bitcast.16, ...), custom_call_target="tpu_custom_call" | custom-call | flops 40000000 | bytes 6000000 | tf_op jit(solution)/shard_map/flux_xy/pallas_call | solution.py:697
  36.2 2.2 %all-to-all-done.1.far = f32[16,48,128]{2,1,0:T(8,128)S(1)} async-done(((f32[16,48,128]{2,1,0:T(8,128)}), f32[16,48,128]{2,1,0:T(8,128)S(1)}, u32[]{:S(2)}, u32[]{:S(2)}) %all-to-all-start.1) | async-done | bytes 393248 | tf_op jit(solution)/shard_map/all_to_all | solution.py:760
  38.4 5.8 %tree.1 = (f32[15,256,128]{2,1,0:T(8,128)}, f32[3,256,128]{2,1,0:T(8,128)}) custom-call(f32[16,48,128]{2,1,0:T(8,128)S(1)} %all-to-all-done.1.far, f32[1,256,128]{2,1,0:T(8,128)} %bitcast.17, f32[3,256,128]{2,1,0:T(8,128)} %bitcast.14, f32[1,256,128]{2,1,0:T(8,128)} %bitcast.20, f32[1,256,128]{2,1,0:T(8,128)} %bitcast.23, f32[9,256,128]{2,1,0:T(8,128)} %bitcast.11, ...), custom_call_target="tpu_custom_call" | custom-call | flops 100000000 | bytes 8000000 | tf_op jit(solution)/shard_map/tree/pallas_call | solution.py:697
Async XLA Ops:
  4.2 19.4 %collective-permute-start = (f32[15,48,128]{2,1,0:T(8,128)}, f32[15,48,128]{2,1,0:T(8,128)S(1)}, u32[]{:S(2)}, u32[]{:S(2)}) collective-permute-start(f32[15,48,128]{2,1,0:T(8,128)} %get-tuple-element.27), channel_id=1, source_target_pairs={{0,8},{16,24},{32,40},{48,56},{64,72},{80,88},{96,104},{112,120},{... | collective-permute-start | bytes 1105928 | tf_op jit(solution)/shard_map/ppermute | solution.py:741
  5.9 17.8 %collective-permute-start.1 = (f32[15,48,128]{2,1,0:T(8,128)}, f32[15,48,128]{2,1,0:T(8,128)S(1)}, u32[]{:S(2)}, u32[]{:S(2)}) collective-permute-start(f32[15,48,128]{2,1,0:T(8,128)} %get-tuple-element.28), channel_id=1, source_target_pairs={{8,16},{24,32},{40,48},{56,64},{72,80},{88,96},{104,112},{120,0},{... | collective-permute-start | bytes 1105928 | tf_op jit(solution)/shard_map/ppermute | solution.py:741
  10.4 13.2 %collective-permute-start.2 = (f32[15,48,128]{2,1,0:T(8,128)}, f32[15,48,128]{2,1,0:T(8,128)S(1)}, u32[]{:S(2)}, u32[]{:S(2)}) collective-permute-start(f32[15,48,128]{2,1,0:T(8,128)} %get-tuple-element.29), channel_id=1, source_target_pairs={{0,1},{2,3},{4,5},{6,7},{1,0},{3,2},{5,4},{7,6},{8,9},{10,11},{12,... | collective-permute-start | bytes 1105928 | tf_op jit(solution)/shard_map/ppermute | solution.py:741
  10.4 13.2 %collective-permute-start.3 = (f32[15,48,128]{2,1,0:T(8,128)}, f32[15,48,128]{2,1,0:T(8,128)S(1)}, u32[]{:S(2)}, u32[]{:S(2)}) collective-permute-start(f32[15,48,128]{2,1,0:T(8,128)} %get-tuple-element.30), channel_id=1, source_target_pairs={{1,2},{3,4},{5,6},{7,0},{2,1},{4,3},{6,5},{0,7},{9,10},{11,12},{13... | collective-permute-start | bytes 1105928 | tf_op jit(solution)/shard_map/ppermute | solution.py:741
  14.6 9.1 %all-to-all-start = ((f32[8,24,128]{2,1,0:T(8,128)}), f32[8,24,128]{2,1,0:T(8,128)S(1)}, u32[]{:S(2)}, u32[]{:S(2)}) async-start(f32[8,24,128]{2,1,0:T(8,128)} %get-tuple-element.25), calls=%async_computation | async-start | bytes 196608 | tf_op jit(solution)/shard_map/all_to_all | solution.py:739
  24.6 13.8 %all-to-all-start.1 = ((f32[16,48,128]{2,1,0:T(8,128)}), f32[16,48,128]{2,1,0:T(8,128)S(1)}, u32[]{:S(2)}, u32[]{:S(2)}) async-start(f32[16,48,128]{2,1,0:T(8,128)} %relay.1), calls=%async_computation.1 | async-start | bytes 786432 | tf_op jit(solution)/shard_map/all_to_all | solution.py:760

commit v6 on v5

--- a/solution.py
+++ b/solution.py
@@ -326,8 +326,9 @@
         tiles[c] = jnp.where(here & (row < 4), low, tiles[c])
         tiles[c] = jnp.where(here & (row == 4) & (lane < to + 8), top, tiles[c])
     tiles[2] = jnp.where((row == 4) & (lane >= 64) & (lane < 72), fastest, tiles[2])
+    pay[8:16] = jnp.zeros((8, 128), F32)
     for c in range(3):
-        pay[c * 8 : c * 8 + 8] = tiles[c]
+        pay[c * 5 : c * 5 + 5] = tiles[c][0:5]
     slabs += load_all([(pay, pay_h.at[y]) for y in range(GY)], sems.at[13 : 13 + GY])
     for copy in slabs:
         copy.wait()
@@ -336,19 +337,19 @@
 def relay_kernel(column, *rest):
     out_h, out, sems = rest[-3:]
     y = position()[1]
-    even = [column[pl.ds(c * 8 + 4, 4, stride=48)] for c in range(3)]
-    odd = [column[pl.ds(c * 8 + 28, 4, stride=48)] for c in range(3)]
+    even = [column[pl.ds(c * 5 + 4, 4, stride=32)] for c in range(3)]
+    odd = [column[pl.ds(c * 5 + 20, 4, stride=32)] for c in range(3)]
     near = []
     for dy in range(3):
         here = jnp.clip(y + dy - 1, 0, GY - 1)
         inside = here == y + dy - 1
         for c in range(3):
-            tile = column[pl.ds(pl.multiple_of(here * 24 + c * 8, 8), 8)]
+            tile = column[pl.ds(here * 16 + c * 5, 4)]
             near.append(jnp.where(inside, tile, 0.0))
     for c in range(3):
         out[c * 4 : c * 4 + 4] = even[c] + pltpu.roll(odd[c], 8, 1)
     for n, tile in enumerate(near):
-        out[12 + n * 4 : 16 + n * 4] = tile[0:4]
+        out[12 + n * 4 : 16 + n * 4] = tile
     for copy in load_all([(out, out_h.at[x]) for x in range(GX)], sems):
         copy.wait()
 
@@ -725,8 +726,8 @@
         prepare_kernel,
         "prepare",
         fields + [(leaf_flags, HBM)] + [(x, HBM) for x in first],
-        [((GY, 24, 128), HBM), (whole, VMEM)] + [(slab, HBM)] * 4,
-        [pltpu.VMEM((24, 128), F32), pltpu.VMEM((2, *slab), F32), pltpu.VMEM((8, 128), F32), scratch_like(leaf_flags)]
+        [((GY, 16, 128), HBM), (whole, VMEM)] + [(slab, HBM)] * 4,
+        [pltpu.VMEM((16, 128), F32), pltpu.VMEM((2, *slab), F32), pltpu.VMEM((8, 128), F32), scratch_like(leaf_flags)]
         + [scratch_like(x) for x in first]
         + [pltpu.SemaphoreType.DMA((13 + GY,))],
         (10**7, 4 * 10**6, 10**5),
@@ -737,10 +738,11 @@
         return [(i, (i + 1) % count) for i in lows] + [((i + 1) % count, i) for i in lows]
 
     column = lax.all_to_all(pay, "my", 0, 0)
-    halos = [
+    swaps = [
         (lax.ppermute(slab, axis, pairs(count, start)), ANY)
-        for slab, axis, count, start in ((xa, "mx", GX, 0), (xb, "mx", GX, 1), (ya, "my", GY, 0), (yb, "my", GY, 1))
+        for slab, axis, count, start in ((xb, "mx", GX, 1), (yb, "my", GY, 1), (xa, "mx", GX, 0), (ya, "my", GY, 0))
     ]
+    halos = [swaps[i] for i in (2, 0, 3, 1)]
     (along_z,) = call(
         flux_z_kernel,
         "flux_z",
@@ -752,7 +754,7 @@
     (chunks,) = call(
         relay_kernel,
         "relay",
-        [(column.reshape(GY * 24, 128), VMEM), (along_z, HBM)] + halos,
+        [(column.reshape(GY * 16, 128), VMEM), (along_z, HBM)] + swaps,
         [((GX, 48, 128), HBM)],
         [pltpu.VMEM((48, 128), F32), pltpu.SemaphoreType.DMA((GX,))],
         (10**4, 10**6, 0),

time: 44.6 us -> 43.2 us (0.969)
  starting transfers between devices: 17.3 us -> 16 us
    ppermute x4, starting transfers between devices: 10.4 us -> 8.57 us  [shards(): lax.ppermute(slab, axis, pairs(count, start))]
  transfers between devices with their start and end apart: 6 -> 6, of which waited for: 2 -> 3; matrix products, arithmetic and copies ran while one was open for 0% -> 0% of each run, Pallas kernels for 27% -> 28%
where the time goes in v6:
time: 43.2 us; the launch traced here: 42.8 us
  Pallas kernels  22.1 us (51%)
  starting transfers between devices  16 us (37%)
  waiting for transfers between devices  4.02 us (9%)
  between operations  0.67 us (2%)
    pallas_call x5, Pallas kernels, call(): pl.pallas_call(kernel, out_shape=[pltpu.HBM(s, t) if spec is HBM else jax...  22.1 us
    ppermute x4, starting transfers between devices, shards(): lax.ppermute(slab, axis, pairs(count, start))  8.57 us
    all_to_all x1, starting transfers between devices, shards(): far = lax.all_to_all(chunks, 'mx', 0, 0)  3.75 us
    all_to_all x1, starting transfers between devices, shards(): column = lax.all_to_all(pay, 'my', 0, 0)  3.69 us
    all_to_all x1, waiting for transfers between devices, shards(): far = lax.all_to_all(chunks, 'mx', 0, 0)  2.05 us
    all_to_all x1, waiting for transfers between devices, shards(): column = lax.all_to_all(pay, 'my', 0, 0)  1.75 us
  transfers between devices with their start and end apart: 6, of which 3 were waited for; matrix products, arithmetic and copies ran while one was open for 0% of the time, Pallas kernels for 28%

profile of v6, /device:TPU:0, one launch (start us, length us, event | category | flops | bytes accessed | tf_op | source)
XLA Modules:
  0.0 42.8 jit_solution(14704993815406254712)
XLA Ops:
  0.6 3.6 %prepare.1 = (f32[8,16,128]{2,1,0:T(8,128)}, f32[15,256,128]{2,1,0:T(8,128)S(1)}, f32[15,48,128]{2,1,0:T(8,128)}, f32[15,48,128]{2,1,0:T(8,128)}, f32[15,48,128]{2,1,0:T(8,128)}, /*index=5*/f32[15,48,128]{2,1,0:T(8,128)}) custom-call(f32[1,256,128]{2,1,0:T(8,128)} %bitcast.15, f32[3,256,128]{2,1,0:T(8,128)} %bitcast.12, f32[1,256,128]{2,1,0:T(8,128)} %bitcast.18, ...), custom_call_target="tpu_custom_call" | custom-call | flops 10000000 | bytes 4000000 | tf_op jit(solution)/shard_map/prepare/pallas_call | solution.py:698
  4.2 5.4 %collective-permute-start = (f32[15,48,128]{2,1,0:T(8,128)}, f32[15,48,128]{2,1,0:T(8,128)S(1)}, u32[]{:S(2)}, u32[]{:S(2)}) collective-permute-start(f32[15,48,128]{2,1,0:T(8,128)} %get-tuple-element.27), channel_id=1, source_target_pairs={{8,16},{24,32},{40,48},{56,64},{72,80},{88,96},{104,112},{120,0},{... | collective-permute-start | bytes 1105928 | tf_op jit(solution)/shard_map/ppermute | solution.py:742
  9.6 3.2 %collective-permute-start.1 = (f32[15,48,128]{2,1,0:T(8,128)}, f32[15,48,128]{2,1,0:T(8,128)S(1)}, u32[]{:S(2)}, u32[]{:S(2)}) collective-permute-start(f32[15,48,128]{2,1,0:T(8,128)} %get-tuple-element.28), channel_id=1, source_target_pairs={{1,2},{3,4},{5,6},{7,0},{2,1},{4,3},{6,5},{0,7},{9,10},{11,12},{13... | collective-permute-start | bytes 1105928 | tf_op jit(solution)/shard_map/ppermute | solution.py:742
  12.8 0.0 collective-permute-start.2
  12.8 0.0 collective-permute-start.3
  12.8 3.7 %all-to-all-start = ((f32[8,16,128]{2,1,0:T(8,128)}), f32[8,16,128]{2,1,0:T(8,128)S(1)}, u32[]{:S(2)}, u32[]{:S(2)}) async-start(f32[8,16,128]{2,1,0:T(8,128)} %get-tuple-element.25), calls=%async_computation | async-start | bytes 131072 | tf_op jit(solution)/shard_map/all_to_all | solution.py:740
  16.5 3.9 %flux_z.1.rest_0_.along_z_h = f32[15,256,128]{2,1,0:T(8,128)} custom-call(f32[15,256,128]{2,1,0:T(8,128)S(1)} %get-tuple-element.26.u), custom_call_target="tpu_custom_call" | custom-call | flops 20000000 | bytes 4000000 | tf_op jit(solution)/shard_map/flux_z/pallas_call | solution.py:698
  20.4 1.8 %all-to-all-done = f32[8,16,128]{2,1,0:T(8,128)S(1)} async-done(((f32[8,16,128]{2,1,0:T(8,128)}), f32[8,16,128]{2,1,0:T(8,128)S(1)}, u32[]{:S(2)}, u32[]{:S(2)}) %all-to-all-start) | async-done | bytes 65568 | tf_op jit(solution)/shard_map/all_to_all | solution.py:740
  22.1 0.0 collective-permute-done.rest_1_.xb
  22.1 0.0 collective-permute-done.1.rest_2_.yb_h
  22.1 0.2 collective-permute-done.2.rest_3_.xa
  22.3 0.0 collective-permute-done.3.rest_4_.ya_h
  22.3 0.9 %relay.1 = f32[16,48,128]{2,1,0:T(8,128)} custom-call(f32[128,128]{1,0:T(8,128)S(1)} %bitcast.8, f32[15,256,128]{2,1,0:T(8,128)} %flux_z.1.rest_0_.along_z_h, f32[15,48,128]{2,1,0:T(8,128)S(1)} %collective-permute-done.rest_1_.xb, f32[15,48,128]{2,1,0:T(8,128)S(1)} %collective-permute-done.1.rest_2_.yb_h, ...), custom_call_target="tpu_custom_call" | custom-call | flops 10000 | bytes 1000000 | tf_op jit(solution)/shard_map/relay/pallas_call | solution.py:698
  23.3 3.8 %all-to-all-start.1 = ((f32[16,48,128]{2,1,0:T(8,128)}), f32[16,48,128]{2,1,0:T(8,128)S(1)}, u32[]{:S(2)}, u32[]{:S(2)}) async-start(f32[16,48,128]{2,1,0:T(8,128)} %relay.1), calls=%async_computation.1 | async-start | bytes 786432 | tf_op jit(solution)/shard_map/all_to_all | solution.py:762
  27.1 7.9 %flux_xy.1 = (f32[15,256,128]{2,1,0:T(8,128)}, bf16[168,800]{1,0:T(8,128)(2,1)S(1)}, bf16[168,800]{1,0:T(8,128)(2,1)S(1)}, bf16[160,40]{1,0:T(8,128)(2,1)S(1)}, ...) custom-call(f32[1,256,128]{2,1,0:T(8,128)} %bitcast.16, ...), custom_call_target="tpu_custom_call" | custom-call | flops 40000000 | bytes 6000000 | tf_op jit(solution)/shard_map/flux_xy/pallas_call | solution.py:698
  35.0 2.0 %all-to-all-done.1.far = f32[16,48,128]{2,1,0:T(8,128)S(1)} async-done(((f32[16,48,128]{2,1,0:T(8,128)}), f32[16,48,128]{2,1,0:T(8,128)S(1)}, u32[]{:S(2)}, u32[]{:S(2)}) %all-to-all-start.1) | async-done | bytes 393248 | tf_op jit(solution)/shard_map/all_to_all | solution.py:762
  37.0 5.8 %tree.1 = (f32[15,256,128]{2,1,0:T(8,128)}, f32[3,256,128]{2,1,0:T(8,128)}) custom-call(f32[16,48,128]{2,1,0:T(8,128)S(1)} %all-to-all-done.1.far, f32[1,256,128]{2,1,0:T(8,128)} %bitcast.17, f32[3,256,128]{2,1,0:T(8,128)} %bitcast.14, f32[1,256,128]{2,1,0:T(8,128)} %bitcast.20, f32[1,256,128]{2,1,0:T(8,128)} %bitcast.23, f32[9,256,128]{2,1,0:T(8,128)} %bitcast.11, ...), custom_call_target="tpu_custom_call" | custom-call | flops 100000000 | bytes 8000000 | tf_op jit(solution)/shard_map/tree/pallas_call | solution.py:698
Async XLA Ops:
  4.2 17.9 %collective-permute-start = (f32[15,48,128]{2,1,0:T(8,128)}, f32[15,48,128]{2,1,0:T(8,128)S(1)}, u32[]{:S(2)}, u32[]{:S(2)}) collective-permute-start(f32[15,48,128]{2,1,0:T(8,128)} %get-tuple-element.27), channel_id=1, source_target_pairs={{8,16},{24,32},{40,48},{56,64},{72,80},{88,96},{104,112},{120,0},{... | collective-permute-start | bytes 1105928 | tf_op jit(solution)/shard_map/ppermute | solution.py:742
  9.6 12.5 %collective-permute-start.1 = (f32[15,48,128]{2,1,0:T(8,128)}, f32[15,48,128]{2,1,0:T(8,128)S(1)}, u32[]{:S(2)}, u32[]{:S(2)}) collective-permute-start(f32[15,48,128]{2,1,0:T(8,128)} %get-tuple-element.28), channel_id=1, source_target_pairs={{1,2},{3,4},{5,6},{7,0},{2,1},{4,3},{6,5},{0,7},{9,10},{11,12},{13... | collective-permute-start | bytes 1105928 | tf_op jit(solution)/shard_map/ppermute | solution.py:742
  12.8 9.5 %collective-permute-start.2 = (f32[15,48,128]{2,1,0:T(8,128)}, f32[15,48,128]{2,1,0:T(8,128)S(1)}, u32[]{:S(2)}, u32[]{:S(2)}) collective-permute-start(f32[15,48,128]{2,1,0:T(8,128)} %get-tuple-element.29), channel_id=1, source_target_pairs={{0,8},{16,24},{32,40},{48,56},{64,72},{80,88},{96,104},{112,120},{... | collective-permute-start | bytes 1105928 | tf_op jit(solution)/shard_map/ppermute | solution.py:742
  12.8 9.5 %collective-permute-start.3 = (f32[15,48,128]{2,1,0:T(8,128)}, f32[15,48,128]{2,1,0:T(8,128)S(1)}, u32[]{:S(2)}, u32[]{:S(2)}) collective-permute-start(f32[15,48,128]{2,1,0:T(8,128)} %get-tuple-element.30), channel_id=1, source_target_pairs={{0,1},{2,3},{4,5},{6,7},{1,0},{3,2},{5,4},{7,6},{8,9},{10,11},{12,... | collective-permute-start | bytes 1105928 | tf_op jit(solution)/shard_map/ppermute | solution.py:742
  12.8 9.3 %all-to-all-start = ((f32[8,16,128]{2,1,0:T(8,128)}), f32[8,16,128]{2,1,0:T(8,128)S(1)}, u32[]{:S(2)}, u32[]{:S(2)}) async-start(f32[8,16,128]{2,1,0:T(8,128)} %get-tuple-element.25), calls=%async_computation | async-start | bytes 131072 | tf_op jit(solution)/shard_map/all_to_all | solution.py:740
  23.3 13.7 %all-to-all-start.1 = ((f32[16,48,128]{2,1,0:T(8,128)}), f32[16,48,128]{2,1,0:T(8,128)S(1)}, u32[]{:S(2)}, u32[]{:S(2)}) async-start(f32[16,48,128]{2,1,0:T(8,128)} %relay.1), calls=%async_computation.1 | async-start | bytes 786432 | tf_op jit(solution)/shard_map/all_to_all | solution.py:762

commit v7 on v6

--- a/solution.py
+++ b/solution.py
@@ -283,26 +283,14 @@
     small = load_all(zip((flags, left, right, flag), (flv, leftv, rightv, flagv)), sems.at[7:11])
     loads = load_all(fields_into((den, mom, ene, ent, tra), u), sems.at[0:5])
     even_x, even_y = pos[0] % 2 == 0, pos[1] % 2 == 0
-    for copy in loads:
-        copy.wait()
-    row_a, row_b = jnp.where(even_x, 208, 0), jnp.where(even_x, 0, 208)
-    slabs = load_all(
-        [(u.at[:, pl.ds(pl.multiple_of(r, 8), 48)], slab) for r, slab in ((row_a, xa), (row_b, xb))], sems.at[5:7]
-    )
-    for f in range(NF):
-        for k in range(3):
-            for s in range(2):
-                at = slice(k * 16 + s * 8, k * 16 + s * 8 + 8)
-                sides[0, f, at] = u[f, pl.ds(s * 128 + k, 8, stride=16)]
-                sides[1, f, at] = u[f, pl.ds(s * 128 + 13 + k, 8, stride=16)]
-    side_a, side_b = jnp.where(even_y, 1, 0), jnp.where(even_y, 0, 1)
-    slabs += load_all([(sides.at[side_a], ya), (sides.at[side_b], yb)], sems.at[11:13])
     for copy in small:
         copy.wait()
     fl[...] = jnp.zeros((8, 128), F32)
     fl[0:2, 0:16] = flv[0].astype(F32)
     fl[2:4, 0:16] = flv[1].astype(F32)
     tile = mxu(fl[...].astype(BF16), flagv[...])
+    for k in (0, 1, 3):
+        loads[k].wait()
     rho = u[0]
     sums = exact(leftv[...], exact(rho, rightv[...]))
     inverse = 1.0 / rho
@@ -329,7 +317,21 @@
     pay[8:16] = jnp.zeros((8, 128), F32)
     for c in range(3):
         pay[c * 5 : c * 5 + 5] = tiles[c][0:5]
-    slabs += load_all([(pay, pay_h.at[y]) for y in range(GY)], sems.at[13 : 13 + GY])
+    slabs = load_all([(pay, pay_h.at[y]) for y in range(GY)], sems.at[13 : 13 + GY])
+    for k in (2, 4):
+        loads[k].wait()
+    row_a, row_b = jnp.where(even_x, 208, 0), jnp.where(even_x, 0, 208)
+    slabs += load_all(
+        [(u.at[:, pl.ds(pl.multiple_of(r, 8), 48)], slab) for r, slab in ((row_a, xa), (row_b, xb))], sems.at[5:7]
+    )
+    for f in range(NF):
+        for k in range(3):
+            for s in range(2):
+                at = slice(k * 16 + s * 8, k * 16 + s * 8 + 8)
+                sides[0, f, at] = u[f, pl.ds(s * 128 + k, 8, stride=16)]
+                sides[1, f, at] = u[f, pl.ds(s * 128 + 13 + k, 8, stride=16)]
+    side_a, side_b = jnp.where(even_y, 1, 0), jnp.where(even_y, 0, 1)
+    slabs += load_all([(sides.at[side_a], ya), (sides.at[side_b], yb)], sems.at[11:13])
     for copy in slabs:
         copy.wait()
 

time: 43.2 us -> 43 us (level)
  no operation moved by 1% of the time
where the time goes in v7:
time: 43 us; the launch traced here: 42.7 us
  Pallas kernels  22 us (51%)
  starting transfers between devices  16 us (37%)
  waiting for transfers between devices  4.02 us (9%)
  between operations  0.67 us (2%)
    pallas_call x5, Pallas kernels, call(): pl.pallas_call(kernel, out_shape=[pltpu.HBM(s, t) if spec is HBM else jax...  22 us
    ppermute x4, starting transfers between devices, shards(): lax.ppermute(slab, axis, pairs(count, start))  8.57 us
    all_to_all x1, starting transfers between devices, shards(): far = lax.all_to_all(chunks, 'mx', 0, 0)  3.75 us
    all_to_all x1, starting transfers between devices, shards(): column = lax.all_to_all(pay, 'my', 0, 0)  3.69 us
    all_to_all x1, waiting for transfers between devices, shards(): far = lax.all_to_all(chunks, 'mx', 0, 0)  2.05 us
    all_to_all x1, waiting for transfers between devices, shards(): column = lax.all_to_all(pay, 'my', 0, 0)  1.75 us
  transfers between devices with their start and end apart: 6, of which 3 were waited for; matrix products, arithmetic and copies ran while one was open for 0% of the time, Pallas kernels for 28%

profile of v7, /device:TPU:0, one launch (start us, length us, event | category | flops | bytes accessed | tf_op | source)
XLA Modules:
  0.0 42.7 jit_solution(6875855819332604224)
XLA Ops:
  0.6 3.4 %prepare.1 = (f32[8,16,128]{2,1,0:T(8,128)}, f32[15,256,128]{2,1,0:T(8,128)S(1)}, f32[15,48,128]{2,1,0:T(8,128)}, f32[15,48,128]{2,1,0:T(8,128)}, f32[15,48,128]{2,1,0:T(8,128)}, /*index=5*/f32[15,48,128]{2,1,0:T(8,128)}) custom-call(f32[1,256,128]{2,1,0:T(8,128)} %bitcast.15, f32[3,256,128]{2,1,0:T(8,128)} %bitcast.12, f32[1,256,128]{2,1,0:T(8,128)} %bitcast.18, ...), custom_call_target="tpu_custom_call" | custom-call | flops 10000000 | bytes 4000000 | tf_op jit(solution)/shard_map/prepare/pallas_call | solution.py:700
  4.1 5.4 %collective-permute-start = (f32[15,48,128]{2,1,0:T(8,128)}, f32[15,48,128]{2,1,0:T(8,128)S(1)}, u32[]{:S(2)}, u32[]{:S(2)}) collective-permute-start(f32[15,48,128]{2,1,0:T(8,128)} %get-tuple-element.27), channel_id=1, source_target_pairs={{8,16},{24,32},{40,48},{56,64},{72,80},{88,96},{104,112},{120,0},{... | collective-permute-start | bytes 1105928 | tf_op jit(solution)/shard_map/ppermute | solution.py:744
  9.5 3.2 %collective-permute-start.1 = (f32[15,48,128]{2,1,0:T(8,128)}, f32[15,48,128]{2,1,0:T(8,128)S(1)}, u32[]{:S(2)}, u32[]{:S(2)}) collective-permute-start(f32[15,48,128]{2,1,0:T(8,128)} %get-tuple-element.28), channel_id=1, source_target_pairs={{1,2},{3,4},{5,6},{7,0},{2,1},{4,3},{6,5},{0,7},{9,10},{11,12},{13... | collective-permute-start | bytes 1105928 | tf_op jit(solution)/shard_map/ppermute | solution.py:744
  12.7 0.0 collective-permute-start.2
  12.7 0.0 collective-permute-start.3
  12.7 3.7 %all-to-all-start = ((f32[8,16,128]{2,1,0:T(8,128)}), f32[8,16,128]{2,1,0:T(8,128)S(1)}, u32[]{:S(2)}, u32[]{:S(2)}) async-start(f32[8,16,128]{2,1,0:T(8,128)} %get-tuple-element.25), calls=%async_computation | async-start | bytes 131072 | tf_op jit(solution)/shard_map/all_to_all | solution.py:742
  16.3 3.9 %flux_z.1.rest_0_.along_z_h = f32[15,256,128]{2,1,0:T(8,128)} custom-call(f32[15,256,128]{2,1,0:T(8,128)S(1)} %get-tuple-element.26.u), custom_call_target="tpu_custom_call" | custom-call | flops 20000000 | bytes 4000000 | tf_op jit(solution)/shard_map/flux_z/pallas_call | solution.py:700
  20.2 1.8 %all-to-all-done = f32[8,16,128]{2,1,0:T(8,128)S(1)} async-done(((f32[8,16,128]{2,1,0:T(8,128)}), f32[8,16,128]{2,1,0:T(8,128)S(1)}, u32[]{:S(2)}, u32[]{:S(2)}) %all-to-all-start) | async-done | bytes 65568 | tf_op jit(solution)/shard_map/all_to_all | solution.py:742
  22.0 0.0 collective-permute-done.rest_1_.xb
  22.0 0.0 collective-permute-done.1.rest_2_.yb_h
  22.0 0.2 collective-permute-done.2.rest_3_.xa
  22.2 0.0 collective-permute-done.3.rest_4_.ya_h
  22.2 0.9 %relay.1 = f32[16,48,128]{2,1,0:T(8,128)} custom-call(f32[128,128]{1,0:T(8,128)S(1)} %bitcast.8, f32[15,256,128]{2,1,0:T(8,128)} %flux_z.1.rest_0_.along_z_h, f32[15,48,128]{2,1,0:T(8,128)S(1)} %collective-permute-done.rest_1_.xb, f32[15,48,128]{2,1,0:T(8,128)S(1)} %collective-permute-done.1.rest_2_.yb_h, ...), custom_call_target="tpu_custom_call" | custom-call | flops 10000 | bytes 1000000 | tf_op jit(solution)/shard_map/relay/pallas_call | solution.py:700
  23.1 3.8 %all-to-all-start.1 = ((f32[16,48,128]{2,1,0:T(8,128)}), f32[16,48,128]{2,1,0:T(8,128)S(1)}, u32[]{:S(2)}, u32[]{:S(2)}) async-start(f32[16,48,128]{2,1,0:T(8,128)} %relay.1), calls=%async_computation.1 | async-start | bytes 786432 | tf_op jit(solution)/shard_map/all_to_all | solution.py:764
  26.9 7.9 %flux_xy.1 = (f32[15,256,128]{2,1,0:T(8,128)}, bf16[168,800]{1,0:T(8,128)(2,1)S(1)}, bf16[168,800]{1,0:T(8,128)(2,1)S(1)}, bf16[160,40]{1,0:T(8,128)(2,1)S(1)}, ...) custom-call(f32[1,256,128]{2,1,0:T(8,128)} %bitcast.16, ...), custom_call_target="tpu_custom_call" | custom-call | flops 40000000 | bytes 6000000 | tf_op jit(solution)/shard_map/flux_xy/pallas_call | solution.py:700
  34.8 2.0 %all-to-all-done.1.far = f32[16,48,128]{2,1,0:T(8,128)S(1)} async-done(((f32[16,48,128]{2,1,0:T(8,128)}), f32[16,48,128]{2,1,0:T(8,128)S(1)}, u32[]{:S(2)}, u32[]{:S(2)}) %all-to-all-start.1) | async-done | bytes 393248 | tf_op jit(solution)/shard_map/all_to_all | solution.py:764
  36.9 5.8 %tree.1 = (f32[15,256,128]{2,1,0:T(8,128)}, f32[3,256,128]{2,1,0:T(8,128)}) custom-call(f32[16,48,128]{2,1,0:T(8,128)S(1)} %all-to-all-done.1.far, f32[1,256,128]{2,1,0:T(8,128)} %bitcast.17, f32[3,256,128]{2,1,0:T(8,128)} %bitcast.14, f32[1,256,128]{2,1,0:T(8,128)} %bitcast.20, f32[1,256,128]{2,1,0:T(8,128)} %bitcast.23, f32[9,256,128]{2,1,0:T(8,128)} %bitcast.11, ...), custom_call_target="tpu_custom_call" | custom-call | flops 100000000 | bytes 8000000 | tf_op jit(solution)/shard_map/tree/pallas_call | solution.py:700
Async XLA Ops:
  4.1 17.9 %collective-permute-start = (f32[15,48,128]{2,1,0:T(8,128)}, f32[15,48,128]{2,1,0:T(8,128)S(1)}, u32[]{:S(2)}, u32[]{:S(2)}) collective-permute-start(f32[15,48,128]{2,1,0:T(8,128)} %get-tuple-element.27), channel_id=1, source_target_pairs={{8,16},{24,32},{40,48},{56,64},{72,80},{88,96},{104,112},{120,0},{... | collective-permute-start | bytes 1105928 | tf_op jit(solution)/shard_map/ppermute | solution.py:744
  9.5 12.5 %collective-permute-start.1 = (f32[15,48,128]{2,1,0:T(8,128)}, f32[15,48,128]{2,1,0:T(8,128)S(1)}, u32[]{:S(2)}, u32[]{:S(2)}) collective-permute-start(f32[15,48,128]{2,1,0:T(8,128)} %get-tuple-element.28), channel_id=1, source_target_pairs={{1,2},{3,4},{5,6},{7,0},{2,1},{4,3},{6,5},{0,7},{9,10},{11,12},{13... | collective-permute-start | bytes 1105928 | tf_op jit(solution)/shard_map/ppermute | solution.py:744
  12.7 9.5 %collective-permute-start.2 = (f32[15,48,128]{2,1,0:T(8,128)}, f32[15,48,128]{2,1,0:T(8,128)S(1)}, u32[]{:S(2)}, u32[]{:S(2)}) collective-permute-start(f32[15,48,128]{2,1,0:T(8,128)} %get-tuple-element.29), channel_id=1, source_target_pairs={{0,8},{16,24},{32,40},{48,56},{64,72},{80,88},{96,104},{112,120},{... | collective-permute-start | bytes 1105928 | tf_op jit(solution)/shard_map/ppermute | solution.py:744
  12.7 9.5 %collective-permute-start.3 = (f32[15,48,128]{2,1,0:T(8,128)}, f32[15,48,128]{2,1,0:T(8,128)S(1)}, u32[]{:S(2)}, u32[]{:S(2)}) collective-permute-start(f32[15,48,128]{2,1,0:T(8,128)} %get-tuple-element.30), channel_id=1, source_target_pairs={{0,1},{2,3},{4,5},{6,7},{1,0},{3,2},{5,4},{7,6},{8,9},{10,11},{12,... | collective-permute-start | bytes 1105928 | tf_op jit(solution)/shard_map/ppermute | solution.py:744
  12.7 9.3 %all-to-all-start = ((f32[8,16,128]{2,1,0:T(8,128)}), f32[8,16,128]{2,1,0:T(8,128)S(1)}, u32[]{:S(2)}, u32[]{:S(2)}) async-start(f32[8,16,128]{2,1,0:T(8,128)} %get-tuple-element.25), calls=%async_computation | async-start | bytes 131072 | tf_op jit(solution)/shard_map/all_to_all | solution.py:742
  23.1 13.7 %all-to-all-start.1 = ((f32[16,48,128]{2,1,0:T(8,128)}), f32[16,48,128]{2,1,0:T(8,128)S(1)}, u32[]{:S(2)}, u32[]{:S(2)}) async-start(f32[16,48,128]{2,1,0:T(8,128)} %relay.1), calls=%async_computation.1 | async-start | bytes 786432 | tf_op jit(solution)/shard_map/all_to_all | solution.py:764
